TPU v7x, 32 devices: a whole 2x2x4 slice. The times are simulated.
32 devices in a mesh: row: 4 (over y, x), col: 8 (over z, core).
Axes of the slice: x: 2, y: 2, z: 4, core: 2. Of those that a mesh axis runs over, the one named last changes fastest.
Arguments:
- vectors: float32 [32, 32768], P(None, ('row', 'col'))
- tiles: float32 [4096, 128, 128], P(('row', 'col'))
- tile_row: int32 [32, 128], P(('row', 'col')), may hold values from 0 to 63, never falling along the last dimension, each value on 1 to 6 neighbouring positions
- tile_col: int32 [32, 128], P(('row', 'col')), may hold values from 0 to 31
Outputs:
- filtered: float32 [32, 32768], P(None, ('row', 'col'))
- gram: float32 [32, 32], replicated
Inputs may be any that keep to these rules, and one draw needn't show every extreme that they name: `tile_row`: on each device the entries never fall along the last dimension, and each of the 64 values is taken by 1 to 6 slots.
All inputs are finite; a program needn't handle non-finite values.
Results may differ from a plain program's by a relative error of at most 0.00015.
Values sent between devices are 32-bit elements; how exact they have to be, the bound alone decides.
No kernel may reach another device: no remote copies, remote signals or barrier semaphores. Data moves between devices by JAX's collectives and lax.ppermute only.
A program may use at most 64 MiB of HBM per device.

v0:
```python
import jax
import jax.numpy as jnp
from jax import lax
from jax.sharding import PartitionSpec as P

TB = 128
K = 32
STEPS = 3


def on_device(vectors, tiles, tile_row, tile_col):
    rows_here = tile_row[0]
    cols_here = tile_col[0]
    n_row = lax.axis_size("row")
    n_col = lax.axis_size("col")
    width = vectors.shape[1]
    owned = width // TB
    local_rows = n_col * owned
    local_cols = n_row * owned
    onehot = (rows_here[:, None] == jnp.arange(local_rows, dtype=jnp.int32)[None, :]).astype(
        jnp.float32
    )
    magnitude = jnp.sum(jnp.abs(tiles), axis=2)
    row_terms = jnp.einsum("ti,tl->li", magnitude, onehot, precision=lax.Precision.HIGHEST).reshape(
        local_rows * TB
    )
    degree = 1.0 + lax.psum_scatter(row_terms, "col", scatter_dimension=0, tiled=True)
    scale = 1.0 / jnp.sqrt(degree)

    def operate(current):
        scaled = current * scale[None, :]
        panel = lax.all_gather(scaled, "row", axis=1, tiled=True)
        picked = jnp.take(panel.reshape(K, local_cols, TB), cols_here, axis=1)
        product = jnp.einsum("tij,ktj->kti", tiles, picked, precision=lax.Precision.HIGHEST)
        partial_value = jnp.einsum(
            "kti,tl->kli", product, onehot, precision=lax.Precision.HIGHEST
        ).reshape(K, local_rows * TB)
        mine = lax.psum_scatter(partial_value, "col", scatter_dimension=1, tiled=True)
        return mine * scale[None, :]

    previous = vectors
    current = operate(vectors)
    for step in range(STEPS - 1):
        following = 2.0 * operate(current) - previous
        previous = current
        current = following
    local_gram = jnp.dot(current, current.T, precision=lax.Precision.HIGHEST)
    gram = lax.psum(local_gram, ("row", "col")) / (width * n_row * n_col)
    return (current, gram)


def solution(mesh):
    in_specs = (
        P(None, ("row", "col")),
        P(("row", "col"), None, None),
        P(("row", "col"), None),
        P(("row", "col"), None),
    )
    out_specs = (P(None, ("row", "col")), P())
    return jax.shard_map(
        on_device, mesh=mesh, in_specs=in_specs, out_specs=out_specs, check_vma=False
    )
```

profile of v0, /device:TPU:0, one launch (start us, length us, event | category | flops | bytes accessed | tf_op | source)
XLA Modules:
  0.0 274.7 jit_solution(16175437541620134693)
XLA Ops:
  7.2 0.0 reduce-scatter.4.cloned.1.call-start
  7.2 0.7 compare_and_fusion
  7.9 0.7 compare_select_fusion
  8.5 0.0 copy-start.3
  8.6 0.0 copy-start.4
  8.6 0.0 copy-start.1
  8.6 5.7 %abs_reduce_fusion = f32[128,128]{1,0:T(8,128)S(1)} fusion(f32[128,128,128]{2,1,0:T(8,128)} %param.7), kind=kLoop, calls=%fused_computation.3 | loop fusion | flops 4177920 | bytes 8454144 | tf_op jit(solution)/shard_map/reduce_sum | solution.py:23
  14.2 0.0 copy-done.3
  14.2 0.2 convolution_bitcast_fusion
  14.4 30.3 %all-reduce = f32[8192]{0:T(1024)S(1)} all-reduce(f32[8192]{0:T(1024)S(1)} %convolution_bitcast_fusion), channel_id=2, replica_groups=mesh['row'=4,'col'=8] {'col'}, use_global_device_ids=true, to_apply=%region_1.0.clone | all-reduce | flops 8192 | bytes 65536
  44.7 0.0 copy-done.4
  44.7 0.6 dynamic-slice
  45.9 0.0 copy-done.1
  46.0 10.1 %all_gather.9 = f32[32,4096]{1,0:T(8,128)S(1)} all-gather(f32[32,1024]{1,0:T(8,128)S(1)} %broadcast_multiply_fusion), channel_id=1, replica_groups=mesh['row'=4,'col'=8] {'row'}, dimensions={1}, use_global_device_ids=true | all-gather | bytes 655360 | tf_op jit(solution)/shard_map/all_gather | solution.py:32
  56.0 0.1 copy_bitcast_fusion.5
  56.1 0.8 gather_fusion
  56.9 15.5 %fusion.15 = f32[32,128,128]{2,0,1:T(8,128)S(1)} fusion(f32[128,128,128]{2,1,0:T(8,128)} %param.7, f32[128,32,128]{2,1,0:T(8,128)S(1)} %gather_fusion, pred[128]{0:T(512)(128)(4,1)S(1)} %compare_and_fusion), kind=kOutput, calls=%fused_computation.19 | convolution fusion | flops 805830656 | bytes 12583040 | tf_op jit(solution)/shard_map/tij,ktj->kti/dot_general | solution.py:34
  72.4 2.1 fusion.10
  74.5 1.6 copy.38
  76.1 0.0 reduce-scatter.4.cloned.1.call-update
  76.1 0.0 reduce-scatter.6.cloned.1.call-start
  76.1 29.7 %reduce-scatter.4.cloned.1.call-done = f32[32,1024]{1,0:T(8,128)} async-done(((f32[32,8192]{1,0:T(8,128)}), f32[32,1024]{1,0:T(8,128)}) %reduce-scatter.4.cloned.1.call-update) | async-done | bytes 131088 | tf_op jit(solution)/shard_map/reduce_scatter | solution.py:38
  105.8 0.9 multiply_multiply_fusion
  106.8 10.3 %all_gather.10 = f32[32,4096]{1,0:T(8,128)S(1)} all-gather(f32[32,1024]{1,0:T(8,128)S(1)} %multiply_multiply_fusion), channel_id=1, replica_groups=mesh['row'=4,'col'=8] {'row'}, dimensions={1}, use_global_device_ids=true | all-gather | bytes 655360 | tf_op jit(solution)/shard_map/all_gather | solution.py:32
  117.0 0.1 copy_bitcast_fusion.4
  117.1 0.8 gather_fusion.1
  117.9 15.5 %fusion.18 = f32[32,128,128]{2,0,1:T(8,128)S(1)} fusion(f32[128,128,128]{2,1,0:T(8,128)} %param.7, f32[128,32,128]{2,1,0:T(8,128)S(1)} %gather_fusion.1, pred[128]{0:T(512)(128)(4,1)S(1)} %compare_and_fusion), kind=kOutput, calls=%fused_computation.20 | convolution fusion | flops 805830656 | bytes 12583040 | tf_op jit(solution)/shard_map/tij,ktj->kti/dot_general | solution.py:34
  133.4 2.1 fusion.8
  135.5 1.6 copy.37
  137.1 0.0 reduce-scatter.6.cloned.1.call-update
  137.1 0.0 reduce-scatter.8.cloned.1.call-start
  137.1 29.8 %reduce-scatter.6.cloned.1.call-done = f32[32,1024]{1,0:T(8,128)} async-done(((f32[32,8192]{1,0:T(8,128)}), f32[32,1024]{1,0:T(8,128)}) %reduce-scatter.6.cloned.1.call-update) | async-done | bytes 131088 | tf_op jit(solution)/shard_map/reduce_scatter | solution.py:38
  166.9 0.9 subtract_multiply_fusion
  167.8 10.5 %all_gather.11 = f32[32,4096]{1,0:T(8,128)S(1)} all-gather(f32[32,1024]{1,0:T(8,128)S(1)} %subtract_multiply_fusion), channel_id=1, replica_groups=mesh['row'=4,'col'=8] {'row'}, dimensions={1}, use_global_device_ids=true | all-gather | bytes 655360 | tf_op jit(solution)/shard_map/all_gather | solution.py:32
  178.4 0.1 copy_bitcast_fusion.3
  178.4 0.8 gather_fusion.2
  179.2 15.5 %fusion.21 = f32[32,128,128]{2,0,1:T(8,128)S(1)} fusion(f32[128,128,128]{2,1,0:T(8,128)} %param.7, f32[128,32,128]{2,1,0:T(8,128)S(1)} %gather_fusion.2, pred[128]{0:T(512)(128)(4,1)S(1)} %compare_and_fusion), kind=kOutput, calls=%fused_computation.21 | convolution fusion | flops 805830656 | bytes 12583040 | tf_op jit(solution)/shard_map/tij,ktj->kti/dot_general | solution.py:34
  194.7 2.1 fusion.6
  196.8 0.0 copy-start.2
  196.8 1.6 copy.36
  198.4 0.0 reduce-scatter.8.cloned.1.call-update
  198.5 29.8 %reduce-scatter.8.cloned.1.call-done = f32[32,1024]{1,0:T(8,128)} async-done(((f32[32,8192]{1,0:T(8,128)}), f32[32,1024]{1,0:T(8,128)}) %reduce-scatter.8.cloned.1.call-update) | async-done | bytes 131088 | tf_op jit(solution)/shard_map/reduce_scatter | solution.py:38
  228.3 0.0 copy-done.2
  228.3 0.9 multiply_subtract_fusion
  229.2 0.0 copy-start
  229.2 0.3 fusion.42
  229.5 38.1 %psum.7 = f32[32,32]{1,0:T(8,128)S(1)} all-reduce(f32[32,32]{1,0:T(8,128)S(1)} %fusion.42), channel_id=1, replica_groups=mesh['row'=4,'col'=8] {'row','col'}, use_global_device_ids=true, to_apply=%region_5.7 | all-reduce | flops 1024 | bytes 8192 | tf_op jit(solution)/shard_map/psum | solution.py:48
  267.6 0.6 broadcast_multiply_fusion.1
  268.2 0.0 copy-done
  (3 shorter events, 0.0 us)
Async XLA Ops:
  7.2 98.7 %reduce-scatter.4.cloned.1.call-start = ((), (), s32[]{:S(2)}) async-start(), calls=%async_computation.3 | async-start | bytes 1179648 | tf_op jit(solution)/shard_map/reduce_scatter | solution.py:38
  8.5 5.7 %copy-start.3 = (s32[1,128]{1,0:T(1,128)S(1)}, s32[1,128]{1,0:T(1,128)}, u32[]{:S(2)}) copy-start(s32[1,128]{1,0:T(1,128)} %param.8) | copy-start | bytes 1540
  8.6 36.1 %copy-start.4 = (u32[32]{0:T(128)S(1)}, u32[32]{0:T(128)}, u32[]{:S(2)}) copy-start(u32[32]{0:T(128)} %constant.23) | copy-start | bytes 388
  8.6 37.4 %copy-start.1 = (f32[32,1024]{1,0:T(8,128)S(1)}, f32[32,1024]{1,0:T(8,128)}, u32[]{:S(2)}) copy-start(f32[32,1024]{1,0:T(8,128)} %param.6) | copy-start | bytes 393220
  76.1 90.8 %reduce-scatter.6.cloned.1.call-start = ((), (), s32[]{:S(2)}) async-start(), calls=%async_computation.4 | async-start | bytes 1179648 | tf_op jit(solution)/shard_map/reduce_scatter | solution.py:38
  137.1 91.2 %reduce-scatter.8.cloned.1.call-start = ((), (), s32[]{:S(2)}) async-start(), calls=%async_computation.5 | async-start | bytes 1179648 | tf_op jit(solution)/shard_map/reduce_scatter | solution.py:38
  196.8 31.5 %copy-start.2 = (f32[32,1024]{1,0:T(8,128)S(1)}, f32[32,1024]{1,0:T(8,128)}, u32[]{:S(2)}) copy-start(f32[32,1024]{1,0:T(8,128)} %reduce-scatter.4.cloned.1.call-done) | copy-start | bytes 393220
  229.2 39.0 %copy-start = (f32[32,1024]{1,0:T(8,128)}, f32[32,1024]{1,0:T(8,128)S(1)}, u32[]{:S(2)}) copy-start(f32[32,1024]{1,0:T(8,128)S(1)} %multiply_subtract_fusion) | copy-start | bytes 393220
Sparse Core Ops, SparseCore 0:
  76.2 29.5 reduce-scatter.3
  137.2 29.6 reduce-scatter.5
  198.6 29.6 reduce-scatter.7
where the time goes:
time: 276 us; the launch traced here: 275 us
  blocking collectives  99.2 us (36%)
  waiting for transfers between devices  89.3 us (32%)
  matrix products  53.1 us (19%)
  between operations  14.6 us (5%)
  other arithmetic  10.4 us (4%)
  local copies, waits for them, and re-layouts  7.97 us (3%)
    reduce_scatter x3, waiting for transfers between devices, operate(): lax.psum_scatter(partial_value, 'col', scatter_dimension=1, tiled=True)  89.3 us
    dot_general x3, matrix products, operate(): jnp.einsum('tij,ktj->kti', tiles, picked, precision=lax.Precision.HIGHEST)  46.4 us
    psum x1, blocking collectives, on_device(): gram = lax.psum(local_gram, ('row', 'col')) / (width * n_row * n_col)  38.1 us
    all_gather x3, blocking collectives, operate(): panel = lax.all_gather(scaled, 'row', axis=1, tiled=True)  30.9 us
    unnamed x1, blocking collectives  30.3 us
    dot_general x3, matrix products, operate(): jnp.einsum('kti,tl->kli', product, onehot, precision=lax.Precision.HIGHEST)  6.26 us
    reduce_sum x1, other arithmetic, on_device(): magnitude = jnp.sum(jnp.abs(tiles), axis=2)  5.65 us
  transfers between devices with their start and end apart: 3, of which 3 were waited for; matrix products, arithmetic and copies ran while one was open for 0% of the time, Pallas kernels for 0%

commit v1 on v0

v1 whole, which is shorter than its diff:
```python
import functools

import jax
import jax.numpy as jnp
from jax import lax
from jax.experimental import pallas as pl
from jax.experimental.pallas import tpu as pltpu
from jax.sharding import PartitionSpec as P

TB = 128
STEPS = 3
GROUP = 16


def split_kernel(rows, tiles_ref, pair_ref, terms_ref, carry):
    step = pl.program_id(0)
    group = tiles_ref.shape[0]
    ones = jnp.ones((16, 2 * TB), jnp.bfloat16)

    @pl.when(step == 0)
    def _():
        carry[...] = jnp.zeros_like(carry)

    total = carry[...]
    for t in range(group):
        index = step * group + t
        row = rows[index]
        same = jnp.logical_and(index > 0, row == rows[jnp.maximum(index - 1, 0)])
        tile = tiles_ref[t]
        high = tile.astype(jnp.bfloat16)
        low = (tile - high.astype(jnp.float32)).astype(jnp.bfloat16)
        pair_ref[t, :, 0:TB] = high
        pair_ref[t, :, TB : 2 * TB] = low
        size = jnp.abs(tile)
        size_high = size.astype(jnp.bfloat16)
        size_low = (size - size_high.astype(jnp.float32)).astype(jnp.bfloat16)
        sums = lax.dot_general(
            ones,
            jnp.concatenate([size_high, size_low], axis=1),
            (((1,), (1,)), ((), ())),
            preferred_element_type=jnp.float32,
        )
        total = sums[0:8] + jnp.where(same, total, 0.0)
        terms_ref[pl.ds(row, 1), :] = total[0:1]
    carry[...] = total


def split_tiles(tiles, rows, local_rows):
    count = tiles.shape[0]
    return pl.pallas_call(
        split_kernel,
        out_shape=(
            jax.ShapeDtypeStruct((count, TB, 2 * TB), jnp.bfloat16),
            jax.ShapeDtypeStruct((local_rows, TB), jnp.float32),
        ),
        grid_spec=pltpu.PrefetchScalarGridSpec(
            num_scalar_prefetch=1,
            grid=(count // GROUP,),
            in_specs=[pl.BlockSpec((GROUP, TB, TB), lambda i, rows: (i, 0, 0))],
            out_specs=[
                pl.BlockSpec((GROUP, TB, 2 * TB), lambda i, rows: (i, 0, 0)),
                pl.BlockSpec((local_rows, TB), lambda i, rows: (0, 0)),
            ],
            scratch_shapes=[pltpu.VMEM((8, TB), jnp.float32)],
        ),
        compiler_params=pltpu.CompilerParams(vmem_limit_bytes=24 << 20),
        cost_estimate=pl.CostEstimate(
            flops=count * TB * TB * 64, bytes_accessed=count * TB * TB * 8, transcendentals=0
        ),
        name="split_tiles",
    )(rows, tiles)


def product_kernel(n_row, n_col, owned, rows, cols, place, *refs):
    sources = refs[:n_row]
    terms_ref, pair_ref, keep_ref, give_ref, scale_ref, operand, sums, carry = refs[n_row:]
    step = pl.program_id(0)
    group = pair_ref.shape[0]
    k = sources[0].shape[0]
    a, b = place[0], place[1]

    @pl.when(step == 0)
    def _():
        carry[...] = jnp.zeros_like(carry)
        for s in range(n_row):
            degree = 1.0 + jnp.sum(terms_ref[a ^ s], axis=0)
            scale = 1.0 / jnp.sqrt(degree)
            for o in range(owned):
                at = slice(o * TB, (o + 1) * TB)
                if s == 0:
                    scale_ref[:, at] = scale[o : o + 1]
                value = sources[s][:, at] * scale[o : o + 1]
                high = value.astype(jnp.bfloat16)
                low = (value - high.astype(jnp.float32)).astype(jnp.bfloat16)
                operand[s * owned + o, 0:k, 0:TB] = high
                operand[s * owned + o, 0:k, TB : 2 * TB] = high
                operand[s * owned + o, k : 2 * k, 0:TB] = low
                operand[s * owned + o, k : 2 * k, TB : 2 * TB] = low

    total = carry[...]
    for t in range(group):
        index = step * group + t
        row, col = rows[index], cols[index]
        same = jnp.logical_and(index > 0, row == rows[jnp.maximum(index - 1, 0)])
        where_from = (lax.div(col, owned) ^ a) * owned + lax.rem(col, owned)
        where_to = (lax.div(row, owned) ^ b) * owned + lax.rem(row, owned)
        both = lax.dot_general(
            operand[where_from],
            pair_ref[t],
            (((1,), (1,)), ((), ())),
            preferred_element_type=jnp.float32,
        )
        total = both[0:k] + both[k : 2 * k] + jnp.where(same, total, 0.0)
        sums[where_to] = total
    carry[...] = total

    @pl.when(step == pl.num_programs(0) - 1)
    def _():
        for d in range(n_col):
            out = give_ref if d % 2 else keep_ref
            for o in range(owned):
                out[d // 2, :, o * TB : (o + 1) * TB] = sums[d * owned + o]


def products(sources, terms, pairs, rows, cols, place, n_row, n_col):
    k, width = sources[0].shape
    owned = width // TB
    count = pairs.shape[0]
    half = jax.ShapeDtypeStruct((n_col // 2, k, width), jnp.float32)
    whole = lambda shape: pl.BlockSpec(shape, lambda i, *_: (0,) * len(shape))
    return pl.pallas_call(
        functools.partial(product_kernel, n_row, n_col, owned),
        out_shape=(half, half, jax.ShapeDtypeStruct((1, width), jnp.float32)),
        grid_spec=pltpu.PrefetchScalarGridSpec(
            num_scalar_prefetch=3,
            grid=(count // GROUP,),
            in_specs=[whole((k, width))] * n_row
            + [
                whole(terms.shape),
                pl.BlockSpec((GROUP, TB, 2 * TB), lambda i, *_: (i, 0, 0)),
            ],
            out_specs=[whole(half.shape)] * 2 + [whole((1, width))],
            scratch_shapes=[
                pltpu.VMEM((n_row * owned, 2 * k, 2 * TB), jnp.bfloat16),
                pltpu.VMEM((n_col * owned, k, TB), jnp.float32),
                pltpu.VMEM((k, TB), jnp.float32),
            ],
        ),
        compiler_params=pltpu.CompilerParams(vmem_limit_bytes=32 << 20),
        cost_estimate=pl.CostEstimate(
            flops=count * TB * TB * 2 * k * 4,
            bytes_accessed=count * TB * TB * 4,
            transcendentals=0,
        ),
        name="products",
    )(rows, cols, place, *sources, terms, pairs)


def swap(value, axis, size, by):
    return lax.ppermute(value, axis, [(i, i ^ by) for i in range(size)])


def on_device(vectors, tiles, tile_row, tile_col):
    rows, cols = tile_row[0], tile_col[0]
    n_row = lax.axis_size("row")
    n_col = lax.axis_size("col")
    k, width = vectors.shape
    owned = width // TB
    local_rows = n_col * owned
    a, b = lax.axis_index("row"), lax.axis_index("col")
    place = jnp.stack([a, b]).astype(jnp.int32)

    def spread(value):
        return [value] + [swap(value, "row", n_row, s) for s in range(1, n_row)]

    sources = spread(vectors)
    pairs, terms = split_tiles(tiles, rows, local_rows)
    sent = jnp.broadcast_to(
        terms.reshape(1, n_col, owned, TB), (n_row, n_col, owned, TB)
    ).reshape(n_row * n_col, owned, TB)
    got = lax.all_to_all(sent, ("row", "col"), 0, 0, tiled=True)
    got = got.reshape(n_row, n_col, owned, TB)

    previous, current = None, vectors
    for step in range(STEPS):
        keep, give, scale = products(sources, got, pairs, rows, cols, place, n_row, n_col)
        chip = keep + swap(give, "col", n_col, 1)
        total = chip[0]
        for d in range(1, n_col // 2):
            total = total + swap(chip[d], "col", n_col, 2 * d)
        if step == 0:
            following = total * scale
        else:
            following = 2.0 * (total * scale) - previous
        previous, current = current, following
        if step < STEPS - 1:
            sources = spread(current)

    local_gram = jnp.dot(current, current.T, precision=lax.Precision.HIGHEST)
    devices = n_row * n_col
    grams = lax.all_to_all(
        jnp.broadcast_to(local_gram[None], (devices, k, k)), ("row", "col"), 0, 0, tiled=True
    )
    gram = jnp.sum(grams, axis=0) / (width * devices)
    return (current, gram)


def solution(mesh):
    in_specs = (
        P(None, ("row", "col")),
        P(("row", "col"), None, None),
        P(("row", "col"), None),
        P(("row", "col"), None),
    )
    out_specs = (P(None, ("row", "col")), P())
    return jax.shard_map(
        on_device, mesh=mesh, in_specs=in_specs, out_specs=out_specs, check_vma=False
    )
```

time: 276 us -> 132 us (0.48)
  blocking collectives: 99.2 us -> 12 us
  matrix products: 53.1 us -> 0.25 us
  waiting for transfers between devices: 89.3 us -> 52.6 us
  starting transfers between devices: 0.12 us -> 33.4 us
  Pallas kernels: 0 us -> 18.1 us
  between operations: 14.6 us -> 0.86 us
  other arithmetic: 10.4 us -> 2.02 us
  local copies, waits for them, and re-layouts: 7.97 us -> 12.4 us
    reduce_scatter x3 -> x0, waiting for transfers between devices: 89.3 us -> none  [operate(): lax.psum_scatter(partial_value, 'col', scatter_dimension=1, tiled=True)]
    dot_general x7 -> x0, matrix products: 52.8 us -> none  [the longest x3 46.4 us: operate(): jnp.einsum('tij,ktj->kti', tiles, picked, precision=lax.Precision.HIGHEST)]
    ppermute x0 -> x21, waiting for transfers between devices: none -> 52.6 us  [swap(): return lax.ppermute(value, axis, [(i, i ^ by) for i in range(size)])]
    psum x1 -> x0, blocking collectives: 38.1 us -> none  [on_device(): gram = lax.psum(local_gram, ('row', 'col')) / (width * n_row * n_col)]
    all_gather x3 -> x0, blocking collectives: 30.9 us -> none  [operate(): panel = lax.all_gather(scaled, 'row', axis=1, tiled=True)]
    unnamed x1 -> x0, blocking collectives: 30.3 us -> none
    ppermute x0 -> x21, starting transfers between devices: none -> 26.1 us  [swap(): return lax.ppermute(value, axis, [(i, i ^ by) for i in range(size)])]
    pallas_call x0 -> x4, Pallas kernels: none -> 18.1 us  [the longest x3 14.2 us: products(): pl.pallas_call(functools.partial(product_kernel, n_row, n_col, owned), ou...]
  transfers between devices with their start and end apart: 3 -> 22, of which waited for: 3 -> 17; matrix products, arithmetic and copies ran while one was open for 0% -> 0% of each run, Pallas kernels for 0% -> 0%
where the time goes in v1:
time: 132 us
  waiting for transfers between devices  52.6 us (40%)
  starting transfers between devices  33.4 us (25%)
  Pallas kernels  18.1 us (14%)
  local copies, waits for them, and re-layouts  12.4 us (9%)
  blocking collectives  12 us (9%)
  other arithmetic  2.02 us (2%)
    ppermute x21, waiting for transfers between devices, swap(): return lax.ppermute(value, axis, [(i, i ^ by) for i in range(size)])  52.6 us
    ppermute x21, starting transfers between devices, swap(): return lax.ppermute(value, axis, [(i, i ^ by) for i in range(size)])  26.1 us
    pallas_call x3, Pallas kernels, products(): pl.pallas_call(functools.partial(product_kernel, n_row, n_col, owned), ou...  14.2 us
    all_to_all x1, blocking collectives, on_device(): lax.all_to_all(jnp.broadcast_to(local_gram[None], (devices, k, k)), ('row...  12 us
    unnamed x18, local copies, waits for them, and re-layouts  11.1 us
    all_to_all x1, starting transfers between devices, on_device(): got = lax.all_to_all(sent, ('row', 'col'), 0, 0, tiled=True)  7.3 us
    pallas_call x1, Pallas kernels, split_tiles(): pl.pallas_call(split_kernel, out_shape=(jax.ShapeDtypeStruct((count, TB,...  3.91 us
  transfers between devices with their start and end apart: 22, of which 17 were waited for; matrix products, arithmetic and copies ran while one was open for 0% of the time, Pallas kernels for 0%

profile of v1, /device:TPU:0, one launch (start us, length us, event | category | flops | bytes accessed | tf_op | source)
XLA Modules:
  0.0 131.7 jit_solution(8667912476605726612)
XLA Ops:
  0.7 3.4 %copy-done.2 = f32[128,128,128]{2,1,0:T(8,128)S(1)} copy-done((f32[128,128,128]{2,1,0:T(8,128)S(1)}, f32[128,128,128]{2,1,0:T(8,128)}, u32[]{:S(2)}) %copy-start.2) | copy-done | bytes 8388632
  4.0 0.7 copy-done.4
  4.7 3.9 %split_tiles.1 = (bf16[128,128,256]{2,1,0:T(8,128)(2,1)S(1)}, f32[64,128]{1,0:T(8,128)S(1)}) custom-call(s32[128]{0:T(128)S(1)} %bitcast.72, f32[128,128,128]{2,1,0:T(8,128)S(1)} %copy-done.2), custom_call_target="tpu_custom_call" | custom-call | flops 134217728 | bytes 16777216 | tf_op jit(solution)/shard_map/split_tiles/pallas_call | solution.py:50
  8.6 3.3 %copy-done = bf16[128,128,256]{2,1,0:T(8,128)(2,1)} copy-done((bf16[128,128,256]{2,1,0:T(8,128)(2,1)}, bf16[128,128,256]{2,1,0:T(8,128)(2,1)S(1)}, u32[]{:S(2)}) %copy-start) | copy-done | bytes 8388632
  11.9 0.7 broadcast_in_dim.14
  12.5 7.3 %all-to-all-start = ((f32[32,8,128]{2,1,0:T(8,128)}), f32[32,8,128]{2,1,0:T(8,128)S(1)}, u32[]{:S(2)}, u32[]{:S(2)}) async-start(f32[32,8,128]{2,1,0:T(8,128)} %bitcast.5), calls=%async_computation | async-start | bytes 262144 | tf_op jit(solution)/shard_map/all_to_all | solution.py:181
  19.9 1.8 %collective-permute-start = (f32[32,1024]{1,0:T(8,128)S(1)}, f32[32,1024]{1,0:T(8,128)S(1)}, u32[]{:S(2)}, u32[]{:S(2)}) collective-permute-start(f32[32,1024]{1,0:T(8,128)S(1)} %copy-done.3), channel_id=1, source_target_pairs={{0,8},{8,0},{16,24},{24,16},{1,9},{9,1},{17,25},{25,17},{2,10},{10... | collective-permute-start | bytes 393224 | tf_op jit(solution)/shard_map/ppermute | solution.py:160
  21.7 1.5 %collective-permute-start.1 = (f32[32,1024]{1,0:T(8,128)S(1)}, f32[32,1024]{1,0:T(8,128)S(1)}, u32[]{:S(2)}, u32[]{:S(2)}) collective-permute-start(f32[32,1024]{1,0:T(8,128)S(1)} %copy-done.3), channel_id=1, source_target_pairs={{0,16},{8,24},{16,0},{24,8},{1,17},{9,25},{17,1},{25,9},{2,18},{10... | collective-permute-start | bytes 393224 | tf_op jit(solution)/shard_map/ppermute | solution.py:160
  23.2 0.3 collective-permute-start.2
  23.4 0.1 pad_add_fusion.place
  23.5 3.8 %collective-permute-done.refs_1_ = f32[32,1024]{1,0:T(8,128)S(1)} collective-permute-done((f32[32,1024]{1,0:T(8,128)S(1)}, f32[32,1024]{1,0:T(8,128)S(1)}, u32[]{:S(2)}, u32[]{:S(2)}) %collective-permute-start) | collective-permute-done | bytes 131104 | tf_op jit(solution)/shard_map/ppermute | solution.py:160
  27.3 3.5 %collective-permute-done.1.refs_2_ = f32[32,1024]{1,0:T(8,128)S(1)} collective-permute-done((f32[32,1024]{1,0:T(8,128)S(1)}, f32[32,1024]{1,0:T(8,128)S(1)}, u32[]{:S(2)}, u32[]{:S(2)}) %collective-permute-start.1) | collective-permute-done | bytes 131104 | tf_op jit(solution)/shard_map/ppermute | solution.py:160
  30.9 3.4 %copy-done.1 = bf16[128,128,256]{2,1,0:T(8,128)(2,1)S(1)} copy-done((bf16[128,128,256]{2,1,0:T(8,128)(2,1)S(1)}, bf16[128,128,256]{2,1,0:T(8,128)(2,1)}, u32[]{:S(2)}) %copy-start.1) | copy-done | bytes 8388632
  34.2 4.7 %products.3 = (f32[4,32,1024]{2,1,0:T(8,128)S(1)}, f32[4,32,1024]{2,1,0:T(8,128)S(1)}, f32[1,1024]{1,0:T(1,128)S(1)}) custom-call(s32[128]{0:T(128)S(1)} %bitcast.73, s32[128]{0:T(128)S(1)} %bitcast.76, s32[2]{0:T(128)S(1)} %pad_add_fusion.place, f32[32,1024]{1,0:T(8,128)S(1)} %copy-done.3, f32[32,1024]{1,0:T(8,128)S(1)} %collective-permute-done.refs_1_, ...), custom_call_target="tpu_custom_call" | custom-call | flops 536870912 | bytes 8388608 | tf_op jit(solution)/shard_map/products/pallas_call | solution.py:131
  39.0 0.1 collective-permute-start.3
  39.1 1.9 %collective-permute-done.3 = f32[4,32,1024]{2,1,0:T(8,128)S(1)} collective-permute-done((f32[4,32,1024]{2,1,0:T(8,128)S(1)}, f32[4,32,1024]{2,1,0:T(8,128)S(1)}, u32[]{:S(2)}, u32[]{:S(2)}) %collective-permute-start.3) | collective-permute-done | bytes 524320 | tf_op jit(solution)/shard_map/ppermute | solution.py:160
  41.0 0.1 add.36
  41.1 1.4 %collective-permute-start.4 = (f32[32,1024]{1,0:T(8,128)S(1)}, f32[32,1024]{1,0:T(8,128)S(1)}, u32[]{:S(2)}, u32[]{:S(2)}) collective-permute-start(f32[32,1024]{1,0:T(8,128)S(1)} %get-tuple-element.30), channel_id=1, source_target_pairs={{0,2},{1,3},{2,0},{3,1},{4,6},{5,7},{6,4},{7,5},{8,10},{9,11},{10,... | collective-permute-start | bytes 393224 | tf_op jit(solution)/shard_map/ppermute | solution.py:160
  42.5 2.3 %collective-permute-start.5 = (f32[32,1024]{1,0:T(8,128)S(1)}, f32[32,1024]{1,0:T(8,128)S(1)}, u32[]{:S(2)}, u32[]{:S(2)}) collective-permute-start(f32[32,1024]{1,0:T(8,128)S(1)} %get-tuple-element.32), channel_id=1, source_target_pairs={{0,4},{1,5},{2,6},{3,7},{4,0},{5,1},{6,2},{7,3},{8,12},{9,13},{10,... | collective-permute-start | bytes 393224 | tf_op jit(solution)/shard_map/ppermute | solution.py:160
  44.8 0.7 collective-permute-start.6
  45.5 3.1 %collective-permute-done.4 = f32[32,1024]{1,0:T(8,128)S(1)} collective-permute-done((f32[32,1024]{1,0:T(8,128)S(1)}, f32[32,1024]{1,0:T(8,128)S(1)}, u32[]{:S(2)}, u32[]{:S(2)}) %collective-permute-start.4) | collective-permute-done | bytes 131104 | tf_op jit(solution)/shard_map/ppermute | solution.py:160
  48.6 6.7 %collective-permute-done.5 = f32[32,1024]{1,0:T(8,128)S(1)} collective-permute-done((f32[32,1024]{1,0:T(8,128)S(1)}, f32[32,1024]{1,0:T(8,128)S(1)}, u32[]{:S(2)}, u32[]{:S(2)}) %collective-permute-start.5) | collective-permute-done | bytes 131104 | tf_op jit(solution)/shard_map/ppermute | solution.py:160
  55.4 1.1 collective-permute-start.7
  56.5 0.8 collective-permute-start.8
  57.3 1.7 %collective-permute-start.9 = (f32[32,1024]{1,0:T(8,128)S(1)}, f32[32,1024]{1,0:T(8,128)S(1)}, u32[]{:S(2)}, u32[]{:S(2)}) collective-permute-start(f32[32,1024]{1,0:T(8,128)S(1)} %fusion.15.refs_0_), channel_id=1, source_target_pairs={{0,24},{8,16},{16,8},{24,0},{1,25},{9,17},{17,9},{25,1},{2,26},{10... | collective-permute-start | bytes 393224 | tf_op jit(solution)/shard_map/ppermute | solution.py:160
  59.0 1.7 %collective-permute-done.7.refs_1_ = f32[32,1024]{1,0:T(8,128)S(1)} collective-permute-done((f32[32,1024]{1,0:T(8,128)S(1)}, f32[32,1024]{1,0:T(8,128)S(1)}, u32[]{:S(2)}, u32[]{:S(2)}) %collective-permute-start.7) | collective-permute-done | bytes 131104 | tf_op jit(solution)/shard_map/ppermute | solution.py:160
  60.7 0.8 collective-permute-done.8.refs_2_
  61.5 1.7 %collective-permute-done.9.refs_3_ = f32[32,1024]{1,0:T(8,128)S(1)} collective-permute-done((f32[32,1024]{1,0:T(8,128)S(1)}, f32[32,1024]{1,0:T(8,128)S(1)}, u32[]{:S(2)}, u32[]{:S(2)}) %collective-permute-start.9) | collective-permute-done | bytes 131104 | tf_op jit(solution)/shard_map/ppermute | solution.py:160
  63.1 4.7 %products.4 = (f32[4,32,1024]{2,1,0:T(8,128)S(1)}, f32[4,32,1024]{2,1,0:T(8,128)S(1)}, f32[1,1024]{1,0:T(1,128)S(1)}) custom-call(s32[128]{0:T(128)S(1)} %bitcast.74, s32[128]{0:T(128)S(1)} %bitcast.77, s32[2]{0:T(128)S(1)} %pad_add_fusion.place, f32[32,1024]{1,0:T(8,128)S(1)} %fusion.15.refs_0_, f32[32,1024]{1,0:T(8,128)S(1)} %collective-permute-done.7.refs_1_, ...), custom_call_target="tpu_custom_call" | custom-call | flops 536870912 | bytes 8388608 | tf_op jit(solution)/shard_map/products/pallas_call | solution.py:131
  67.9 0.1 collective-permute-start.10
  68.0 1.9 %collective-permute-done.10 = f32[4,32,1024]{2,1,0:T(8,128)S(1)} collective-permute-done((f32[4,32,1024]{2,1,0:T(8,128)S(1)}, f32[4,32,1024]{2,1,0:T(8,128)S(1)}, u32[]{:S(2)}, u32[]{:S(2)}) %collective-permute-start.10) | collective-permute-done | bytes 524320 | tf_op jit(solution)/shard_map/ppermute | solution.py:160
  69.9 0.1 add.40
  70.0 3.0 %collective-permute-start.11 = (f32[32,1024]{1,0:T(8,128)S(1)}, f32[32,1024]{1,0:T(8,128)S(1)}, u32[]{:S(2)}, u32[]{:S(2)}) collective-permute-start(f32[32,1024]{1,0:T(8,128)S(1)} %get-tuple-element.27), channel_id=1, source_target_pairs={{0,2},{1,3},{2,0},{3,1},{4,6},{5,7},{6,4},{7,5},{8,10},{9,11},{10,... | collective-permute-start | bytes 393224 | tf_op jit(solution)/shard_map/ppermute | solution.py:160
  72.9 0.9 collective-permute-start.12
  73.8 1.6 %collective-permute-start.13 = (f32[32,1024]{1,0:T(8,128)S(1)}, f32[32,1024]{1,0:T(8,128)S(1)}, u32[]{:S(2)}, u32[]{:S(2)}) collective-permute-start(f32[32,1024]{1,0:T(8,128)S(1)} %get-tuple-element.28), channel_id=1, source_target_pairs={{0,6},{1,7},{2,4},{3,5},{4,2},{5,3},{6,0},{7,1},{8,14},{9,15},{10,... | collective-permute-start | bytes 393224 | tf_op jit(solution)/shard_map/ppermute | solution.py:160
  75.4 3.2 %collective-permute-done.11 = f32[32,1024]{1,0:T(8,128)S(1)} collective-permute-done((f32[32,1024]{1,0:T(8,128)S(1)}, f32[32,1024]{1,0:T(8,128)S(1)}, u32[]{:S(2)}, u32[]{:S(2)}) %collective-permute-start.11) | collective-permute-done | bytes 131104 | tf_op jit(solution)/shard_map/ppermute | solution.py:160
  78.5 7.3 %collective-permute-done.12 = f32[32,1024]{1,0:T(8,128)S(1)} collective-permute-done((f32[32,1024]{1,0:T(8,128)S(1)}, f32[32,1024]{1,0:T(8,128)S(1)}, u32[]{:S(2)}, u32[]{:S(2)}) %collective-permute-start.12) | collective-permute-done | bytes 131104 | tf_op jit(solution)/shard_map/ppermute | solution.py:160
  85.8 0.1 fusion.11.refs_0_
  85.9 1.3 collective-permute-start.14
  87.2 1.0 collective-permute-start.15
  88.2 1.2 collective-permute-start.16
  89.4 1.9 %collective-permute-done.14.refs_1_ = f32[32,1024]{1,0:T(8,128)S(1)} collective-permute-done((f32[32,1024]{1,0:T(8,128)S(1)}, f32[32,1024]{1,0:T(8,128)S(1)}, u32[]{:S(2)}, u32[]{:S(2)}) %collective-permute-start.14) | collective-permute-done | bytes 131104 | tf_op jit(solution)/shard_map/ppermute | solution.py:160
  91.4 0.8 collective-permute-done.15.refs_2_
  92.2 1.9 %collective-permute-done.16.refs_3_ = f32[32,1024]{1,0:T(8,128)S(1)} collective-permute-done((f32[32,1024]{1,0:T(8,128)S(1)}, f32[32,1024]{1,0:T(8,128)S(1)}, u32[]{:S(2)}, u32[]{:S(2)}) %collective-permute-start.16) | collective-permute-done | bytes 131104 | tf_op jit(solution)/shard_map/ppermute | solution.py:160
  94.1 4.7 %products.5 = (f32[4,32,1024]{2,1,0:T(8,128)S(1)}, f32[4,32,1024]{2,1,0:T(8,128)S(1)}, f32[1,1024]{1,0:T(1,128)S(1)}) custom-call(s32[128]{0:T(128)S(1)} %bitcast.75, s32[128]{0:T(128)S(1)} %bitcast.78, s32[2]{0:T(128)S(1)} %pad_add_fusion.place, f32[32,1024]{1,0:T(8,128)S(1)} %fusion.11.refs_0_, f32[32,1024]{1,0:T(8,128)S(1)} %collective-permute-done.14.refs_1_, ...), custom_call_target="tpu_custom_call" | custom-call | flops 536870912 | bytes 8388608 | tf_op jit(solution)/shard_map/products/pallas_call | solution.py:131
  98.8 0.1 collective-permute-start.17
  98.9 1.9 %collective-permute-done.17 = f32[4,32,1024]{2,1,0:T(8,128)S(1)} collective-permute-done((f32[4,32,1024]{2,1,0:T(8,128)S(1)}, f32[4,32,1024]{2,1,0:T(8,128)S(1)}, u32[]{:S(2)}, u32[]{:S(2)}) %collective-permute-start.17) | collective-permute-done | bytes 524320 | tf_op jit(solution)/shard_map/ppermute | solution.py:160
  100.8 0.1 add.44
  100.9 3.0 %collective-permute-start.18 = (f32[32,1024]{1,0:T(8,128)S(1)}, f32[32,1024]{1,0:T(8,128)S(1)}, u32[]{:S(2)}, u32[]{:S(2)}) collective-permute-start(f32[32,1024]{1,0:T(8,128)S(1)} %get-tuple-element.24), channel_id=1, source_target_pairs={{0,2},{1,3},{2,0},{3,1},{4,6},{5,7},{6,4},{7,5},{8,10},{9,11},{10,... | collective-permute-start | bytes 393224 | tf_op jit(solution)/shard_map/ppermute | solution.py:160
  103.9 0.8 collective-permute-start.19
  104.7 1.6 %collective-permute-start.20 = (f32[32,1024]{1,0:T(8,128)S(1)}, f32[32,1024]{1,0:T(8,128)S(1)}, u32[]{:S(2)}, u32[]{:S(2)}) collective-permute-start(f32[32,1024]{1,0:T(8,128)S(1)} %get-tuple-element.25), channel_id=1, source_target_pairs={{0,6},{1,7},{2,4},{3,5},{4,2},{5,3},{6,0},{7,1},{8,14},{9,15},{10,... | collective-permute-start | bytes 393224 | tf_op jit(solution)/shard_map/ppermute | solution.py:160
  106.3 3.2 %collective-permute-done.18 = f32[32,1024]{1,0:T(8,128)S(1)} collective-permute-done((f32[32,1024]{1,0:T(8,128)S(1)}, f32[32,1024]{1,0:T(8,128)S(1)}, u32[]{:S(2)}, u32[]{:S(2)}) %collective-permute-start.18) | collective-permute-done | bytes 131104 | tf_op jit(solution)/shard_map/ppermute | solution.py:160
  109.5 7.3 %collective-permute-done.19 = f32[32,1024]{1,0:T(8,128)S(1)} collective-permute-done((f32[32,1024]{1,0:T(8,128)S(1)}, f32[32,1024]{1,0:T(8,128)S(1)}, u32[]{:S(2)}, u32[]{:S(2)}) %collective-permute-start.19) | collective-permute-done | bytes 131104 | tf_op jit(solution)/shard_map/ppermute | solution.py:160
  116.8 0.1 fusion.5
  116.8 0.0 copy-start.7
  116.9 0.3 fusion.16
  117.1 0.1 broadcast_in_dim.15
  117.2 0.3 reshape.15
  117.4 12.0 %all_to_all.10 = f32[32,1,1024]{2,1,0:T(1,128)S(1)} all-to-all(f32[32,1,1024]{2,1,0:T(1,128)S(1)} %reshape.15), channel_id=1, replica_groups=mesh['row'=4,'col'=8] {'row','col'}, dimensions={0} | all-to-all | bytes 262144 | tf_op jit(solution)/shard_map/all_to_all | solution.py:201
  129.4 0.5 broadcast.8
  129.9 0.9 reduce
  130.9 0.2 reshape.16
  131.0 0.1 reduce_sum.9
  131.1 0.6 broadcast_multiply_fusion
  (20 shorter events, 0.2 us)
Async XLA Ops:
  0.6 30.2 %copy-start.5 = (s32[1,128]{1,0:T(1,128)S(1)}, s32[1,128]{1,0:T(1,128)}, u32[]{:S(2)}) copy-start(s32[1,128]{1,0:T(1,128)} %param.6) | copy-start | bytes 1540
  0.6 30.2 %copy-start.6 = (s32[1,128]{1,0:T(1,128)S(1)}, s32[1,128]{1,0:T(1,128)}, u32[]{:S(2)}) copy-start(s32[1,128]{1,0:T(1,128)} %param.7) | copy-start | bytes 1540
  0.7 3.4 %copy-start.2 = (f32[128,128,128]{2,1,0:T(8,128)S(1)}, f32[128,128,128]{2,1,0:T(8,128)}, u32[]{:S(2)}) copy-start(f32[128,128,128]{2,1,0:T(8,128)} %tiles_ref.1) | copy-start | bytes 25165828
  4.0 0.7 copy-start.4
  4.7 15.2 %copy-start.3 = (f32[32,1024]{1,0:T(8,128)S(1)}, f32[32,1024]{1,0:T(8,128)}, u32[]{:S(2)}) copy-start(f32[32,1024]{1,0:T(8,128)} %refs_0_.1) | copy-start | bytes 393220
  8.6 3.3 %copy-start = (bf16[128,128,256]{2,1,0:T(8,128)(2,1)}, bf16[128,128,256]{2,1,0:T(8,128)(2,1)S(1)}, u32[]{:S(2)}) copy-start(bf16[128,128,256]{2,1,0:T(8,128)(2,1)S(1)} %get-tuple-element.14.refs_5_) | copy-start | bytes 25165828
  12.5 18.3 %all-to-all-start = ((f32[32,8,128]{2,1,0:T(8,128)}), f32[32,8,128]{2,1,0:T(8,128)S(1)}, u32[]{:S(2)}, u32[]{:S(2)}) async-start(f32[32,8,128]{2,1,0:T(8,128)} %bitcast.5), calls=%async_computation | async-start | bytes 262144 | tf_op jit(solution)/shard_map/all_to_all | solution.py:181
  19.9 7.4 %collective-permute-start = (f32[32,1024]{1,0:T(8,128)S(1)}, f32[32,1024]{1,0:T(8,128)S(1)}, u32[]{:S(2)}, u32[]{:S(2)}) collective-permute-start(f32[32,1024]{1,0:T(8,128)S(1)} %copy-done.3), channel_id=1, source_target_pairs={{0,8},{8,0},{16,24},{24,16},{1,9},{9,1},{17,25},{25,17},{2,10},{10... | collective-permute-start | bytes 393224 | tf_op jit(solution)/shard_map/ppermute | solution.py:160
  21.7 9.1 %collective-permute-start.1 = (f32[32,1024]{1,0:T(8,128)S(1)}, f32[32,1024]{1,0:T(8,128)S(1)}, u32[]{:S(2)}, u32[]{:S(2)}) collective-permute-start(f32[32,1024]{1,0:T(8,128)S(1)} %copy-done.3), channel_id=1, source_target_pairs={{0,16},{8,24},{16,0},{24,8},{1,17},{9,25},{17,1},{25,9},{2,18},{10... | collective-permute-start | bytes 393224 | tf_op jit(solution)/shard_map/ppermute | solution.py:160
  23.2 7.7 %collective-permute-start.2 = (f32[32,1024]{1,0:T(8,128)S(1)}, f32[32,1024]{1,0:T(8,128)S(1)}, u32[]{:S(2)}, u32[]{:S(2)}) collective-permute-start(f32[32,1024]{1,0:T(8,128)S(1)} %copy-done.3), channel_id=1, source_target_pairs={{0,24},{8,16},{16,8},{24,0},{1,25},{9,17},{17,9},{25,1},{2,26},{10... | collective-permute-start | bytes 393224 | tf_op jit(solution)/shard_map/ppermute | solution.py:160
  30.9 3.4 %copy-start.1 = (bf16[128,128,256]{2,1,0:T(8,128)(2,1)S(1)}, bf16[128,128,256]{2,1,0:T(8,128)(2,1)}, u32[]{:S(2)}) copy-start(bf16[128,128,256]{2,1,0:T(8,128)(2,1)} %copy-done) | copy-start | bytes 25165828
  39.0 2.0 %collective-permute-start.3 = (f32[4,32,1024]{2,1,0:T(8,128)S(1)}, f32[4,32,1024]{2,1,0:T(8,128)S(1)}, u32[]{:S(2)}, u32[]{:S(2)}) collective-permute-start(f32[4,32,1024]{2,1,0:T(8,128)S(1)} %get-tuple-element.16), channel_id=1, source_target_pairs={{0,1},{1,0},{2,3},{3,2},{4,5},{5,4},{6,7},{7,6},{8,9},{9,8},{10,11... | collective-permute-start | bytes 1572872 | tf_op jit(solution)/shard_map/ppermute | solution.py:160
  41.1 7.6 %collective-permute-start.4 = (f32[32,1024]{1,0:T(8,128)S(1)}, f32[32,1024]{1,0:T(8,128)S(1)}, u32[]{:S(2)}, u32[]{:S(2)}) collective-permute-start(f32[32,1024]{1,0:T(8,128)S(1)} %get-tuple-element.30), channel_id=1, source_target_pairs={{0,2},{1,3},{2,0},{3,1},{4,6},{5,7},{6,4},{7,5},{8,10},{9,11},{10,... | collective-permute-start | bytes 393224 | tf_op jit(solution)/shard_map/ppermute | solution.py:160
  42.5 12.9 %collective-permute-start.5 = (f32[32,1024]{1,0:T(8,128)S(1)}, f32[32,1024]{1,0:T(8,128)S(1)}, u32[]{:S(2)}, u32[]{:S(2)}) collective-permute-start(f32[32,1024]{1,0:T(8,128)S(1)} %get-tuple-element.32), channel_id=1, source_target_pairs={{0,4},{1,5},{2,6},{3,7},{4,0},{5,1},{6,2},{7,3},{8,12},{9,13},{10,... | collective-permute-start | bytes 393224 | tf_op jit(solution)/shard_map/ppermute | solution.py:160
  44.8 10.6 %collective-permute-start.6 = (f32[32,1024]{1,0:T(8,128)S(1)}, f32[32,1024]{1,0:T(8,128)S(1)}, u32[]{:S(2)}, u32[]{:S(2)}) collective-permute-start(f32[32,1024]{1,0:T(8,128)S(1)} %get-tuple-element.31), channel_id=1, source_target_pairs={{0,6},{1,7},{2,4},{3,5},{4,2},{5,3},{6,0},{7,1},{8,14},{9,15},{10,... | collective-permute-start | bytes 393224 | tf_op jit(solution)/shard_map/ppermute | solution.py:160
  55.4 5.3 %collective-permute-start.7 = (f32[32,1024]{1,0:T(8,128)S(1)}, f32[32,1024]{1,0:T(8,128)S(1)}, u32[]{:S(2)}, u32[]{:S(2)}) collective-permute-start(f32[32,1024]{1,0:T(8,128)S(1)} %fusion.15.refs_0_), channel_id=1, source_target_pairs={{0,8},{8,0},{16,24},{24,16},{1,9},{9,1},{17,25},{25,17},{2,10},{10... | collective-permute-start | bytes 393224 | tf_op jit(solution)/shard_map/ppermute | solution.py:160
  56.5 5.0 %collective-permute-start.8 = (f32[32,1024]{1,0:T(8,128)S(1)}, f32[32,1024]{1,0:T(8,128)S(1)}, u32[]{:S(2)}, u32[]{:S(2)}) collective-permute-start(f32[32,1024]{1,0:T(8,128)S(1)} %fusion.15.refs_0_), channel_id=1, source_target_pairs={{0,16},{8,24},{16,0},{24,8},{1,17},{9,25},{17,1},{25,9},{2,18},{10... | collective-permute-start | bytes 393224 | tf_op jit(solution)/shard_map/ppermute | solution.py:160
  57.3 5.9 %collective-permute-start.9 = (f32[32,1024]{1,0:T(8,128)S(1)}, f32[32,1024]{1,0:T(8,128)S(1)}, u32[]{:S(2)}, u32[]{:S(2)}) collective-permute-start(f32[32,1024]{1,0:T(8,128)S(1)} %fusion.15.refs_0_), channel_id=1, source_target_pairs={{0,24},{8,16},{16,8},{24,0},{1,25},{9,17},{17,9},{25,1},{2,26},{10... | collective-permute-start | bytes 393224 | tf_op jit(solution)/shard_map/ppermute | solution.py:160
  67.9 2.0 %collective-permute-start.10 = (f32[4,32,1024]{2,1,0:T(8,128)S(1)}, f32[4,32,1024]{2,1,0:T(8,128)S(1)}, u32[]{:S(2)}, u32[]{:S(2)}) collective-permute-start(f32[4,32,1024]{2,1,0:T(8,128)S(1)} %get-tuple-element.19), channel_id=1, source_target_pairs={{0,1},{1,0},{2,3},{3,2},{4,5},{5,4},{6,7},{7,6},{8,9},{9,8},{10,11... | collective-permute-start | bytes 1572872 | tf_op jit(solution)/shard_map/ppermute | solution.py:160
  70.0 8.6 %collective-permute-start.11 = (f32[32,1024]{1,0:T(8,128)S(1)}, f32[32,1024]{1,0:T(8,128)S(1)}, u32[]{:S(2)}, u32[]{:S(2)}) collective-permute-start(f32[32,1024]{1,0:T(8,128)S(1)} %get-tuple-element.27), channel_id=1, source_target_pairs={{0,2},{1,3},{2,0},{3,1},{4,6},{5,7},{6,4},{7,5},{8,10},{9,11},{10,... | collective-permute-start | bytes 393224 | tf_op jit(solution)/shard_map/ppermute | solution.py:160
  72.9 12.9 %collective-permute-start.12 = (f32[32,1024]{1,0:T(8,128)S(1)}, f32[32,1024]{1,0:T(8,128)S(1)}, u32[]{:S(2)}, u32[]{:S(2)}) collective-permute-start(f32[32,1024]{1,0:T(8,128)S(1)} %get-tuple-element.29), channel_id=1, source_target_pairs={{0,4},{1,5},{2,6},{3,7},{4,0},{5,1},{6,2},{7,3},{8,12},{9,13},{10,... | collective-permute-start | bytes 393224 | tf_op jit(solution)/shard_map/ppermute | solution.py:160
  73.8 12.0 %collective-permute-start.13 = (f32[32,1024]{1,0:T(8,128)S(1)}, f32[32,1024]{1,0:T(8,128)S(1)}, u32[]{:S(2)}, u32[]{:S(2)}) collective-permute-start(f32[32,1024]{1,0:T(8,128)S(1)} %get-tuple-element.28), channel_id=1, source_target_pairs={{0,6},{1,7},{2,4},{3,5},{4,2},{5,3},{6,0},{7,1},{8,14},{9,15},{10,... | collective-permute-start | bytes 393224 | tf_op jit(solution)/shard_map/ppermute | solution.py:160
  85.9 5.5 %collective-permute-start.14 = (f32[32,1024]{1,0:T(8,128)S(1)}, f32[32,1024]{1,0:T(8,128)S(1)}, u32[]{:S(2)}, u32[]{:S(2)}) collective-permute-start(f32[32,1024]{1,0:T(8,128)S(1)} %fusion.11.refs_0_), channel_id=1, source_target_pairs={{0,8},{8,0},{16,24},{24,16},{1,9},{9,1},{17,25},{25,17},{2,10},{10... | collective-permute-start | bytes 393224 | tf_op jit(solution)/shard_map/ppermute | solution.py:160
  87.2 5.0 %collective-permute-start.15 = (f32[32,1024]{1,0:T(8,128)S(1)}, f32[32,1024]{1,0:T(8,128)S(1)}, u32[]{:S(2)}, u32[]{:S(2)}) collective-permute-start(f32[32,1024]{1,0:T(8,128)S(1)} %fusion.11.refs_0_), channel_id=1, source_target_pairs={{0,16},{8,24},{16,0},{24,8},{1,17},{9,25},{17,1},{25,9},{2,18},{10... | collective-permute-start | bytes 393224 | tf_op jit(solution)/shard_map/ppermute | solution.py:160
  88.2 5.9 %collective-permute-start.16 = (f32[32,1024]{1,0:T(8,128)S(1)}, f32[32,1024]{1,0:T(8,128)S(1)}, u32[]{:S(2)}, u32[]{:S(2)}) collective-permute-start(f32[32,1024]{1,0:T(8,128)S(1)} %fusion.11.refs_0_), channel_id=1, source_target_pairs={{0,24},{8,16},{16,8},{24,0},{1,25},{9,17},{17,9},{25,1},{2,26},{10... | collective-permute-start | bytes 393224 | tf_op jit(solution)/shard_map/ppermute | solution.py:160
  98.8 2.0 %collective-permute-start.17 = (f32[4,32,1024]{2,1,0:T(8,128)S(1)}, f32[4,32,1024]{2,1,0:T(8,128)S(1)}, u32[]{:S(2)}, u32[]{:S(2)}) collective-permute-start(f32[4,32,1024]{2,1,0:T(8,128)S(1)} %get-tuple-element.22), channel_id=1, source_target_pairs={{0,1},{1,0},{2,3},{3,2},{4,5},{5,4},{6,7},{7,6},{8,9},{9,8},{10,11... | collective-permute-start | bytes 1572872 | tf_op jit(solution)/shard_map/ppermute | solution.py:160
  100.9 8.6 %collective-permute-start.18 = (f32[32,1024]{1,0:T(8,128)S(1)}, f32[32,1024]{1,0:T(8,128)S(1)}, u32[]{:S(2)}, u32[]{:S(2)}) collective-permute-start(f32[32,1024]{1,0:T(8,128)S(1)} %get-tuple-element.24), channel_id=1, source_target_pairs={{0,2},{1,3},{2,0},{3,1},{4,6},{5,7},{6,4},{7,5},{8,10},{9,11},{10,... | collective-permute-start | bytes 393224 | tf_op jit(solution)/shard_map/ppermute | solution.py:160
  103.9 12.9 %collective-permute-start.19 = (f32[32,1024]{1,0:T(8,128)S(1)}, f32[32,1024]{1,0:T(8,128)S(1)}, u32[]{:S(2)}, u32[]{:S(2)}) collective-permute-start(f32[32,1024]{1,0:T(8,128)S(1)} %get-tuple-element.26), channel_id=1, source_target_pairs={{0,4},{1,5},{2,6},{3,7},{4,0},{5,1},{6,2},{7,3},{8,12},{9,13},{10,... | collective-permute-start | bytes 393224 | tf_op jit(solution)/shard_map/ppermute | solution.py:160
  104.7 12.1 %collective-permute-start.20 = (f32[32,1024]{1,0:T(8,128)S(1)}, f32[32,1024]{1,0:T(8,128)S(1)}, u32[]{:S(2)}, u32[]{:S(2)}) collective-permute-start(f32[32,1024]{1,0:T(8,128)S(1)} %get-tuple-element.25), channel_id=1, source_target_pairs={{0,6},{1,7},{2,4},{3,5},{4,2},{5,3},{6,0},{7,1},{8,14},{9,15},{10,... | collective-permute-start | bytes 393224 | tf_op jit(solution)/shard_map/ppermute | solution.py:160
  116.8 14.9 %copy-start.7 = (f32[32,1024]{1,0:T(8,128)}, f32[32,1024]{1,0:T(8,128)S(1)}, u32[]{:S(2)}) copy-start(f32[32,1024]{1,0:T(8,128)S(1)} %fusion.5) | copy-start | bytes 393220

commit v2 on v0

v2 whole, which is shorter than its diff:
```python
import functools

import jax
import jax.numpy as jnp
from jax import lax
from jax.experimental import pallas as pl
from jax.experimental.pallas import tpu as pltpu
from jax.sharding import PartitionSpec as P

TB = 128
STEPS = 3
GROUP = 16
UNROLL = 32
CHUNKS = 1

SCALARS = pl.BlockSpec(memory_space=pltpu.SMEM)
VECTORS = pl.BlockSpec(memory_space=pltpu.VMEM)


def same_row(rows, index):
    return jnp.logical_and(index > 0, rows[index] == rows[jnp.maximum(index - 1, 0)])


def two_parts(value):
    high = value.astype(jnp.bfloat16)
    return high, (value - high.astype(jnp.float32)).astype(jnp.bfloat16)


def degree_kernel(rows, tiles_hbm, sent_ref, buffer, terms, arrived):
    count = tiles_hbm.shape[0]
    groups = count // GROUP
    ones = jnp.ones((16, 2 * TB), jnp.bfloat16)

    def fetch(group):
        at = pl.ds(group * GROUP, GROUP)
        return pltpu.make_async_copy(tiles_hbm.at[at], buffer.at[at], arrived.at[group])

    for group in range(groups):
        fetch(group).start()

    def body(group, total):
        fetch(group).wait()
        for t in range(GROUP):
            index = group * GROUP + t
            sums = lax.dot_general(
                ones,
                jnp.concatenate(two_parts(jnp.abs(buffer[index])), axis=1),
                (((1,), (1,)), ((), ())),
                preferred_element_type=jnp.float32,
            )
            total = sums[0:8] + jnp.where(same_row(rows, index), total, 0.0)
            terms[pl.ds(rows[index], 1), :] = total[0:1]
        return total

    lax.fori_loop(0, groups, body, jnp.zeros((8, TB), jnp.float32))
    n_row, n_col, owned, _ = sent_ref.shape
    for s in range(n_row):
        for d in range(n_col):
            sent_ref[s, d] = terms[d * owned : (d + 1) * owned]


def degree_terms(tiles, rows, n_row, n_col, owned):
    count = tiles.shape[0]
    return pl.pallas_call(
        degree_kernel,
        out_shape=jax.ShapeDtypeStruct((n_row, n_col, owned, TB), jnp.float32),
        in_specs=[SCALARS, pl.BlockSpec(memory_space=pltpu.HBM)],
        out_specs=VECTORS,
        scratch_shapes=[
            pltpu.VMEM(tiles.shape, jnp.float32),
            pltpu.VMEM((n_col * owned, TB), jnp.float32),
            pltpu.SemaphoreType.DMA((count // GROUP,)),
        ],
        compiler_params=pltpu.CompilerParams(vmem_limit_bytes=24 << 20),
        cost_estimate=pl.CostEstimate(
            flops=count * TB * TB * 64, bytes_accessed=count * TB * TB * 4, transcendentals=0
        ),
        name="degree_terms",
    )(rows, pltpu.with_memory_space_constraint(tiles, pltpu.HBM))


def product_kernel(n_row, n_col, owned, load, rows, cols, place, *refs):
    refs = list(refs)
    take = lambda n: [refs.pop(0) for _ in range(n)]
    sources = [take(CHUNKS) for _ in range(n_row)]
    terms_ref, tiles_from = take(2)
    keeps, gives = take(CHUNKS), take(CHUNKS)
    (scale_ref,) = take(1)
    tiles_ref = refs.pop(0) if load else tiles_from
    operand, sums = take(2)
    count = tiles_ref.shape[0]
    part = keeps[0].shape[1]
    k = part * CHUNKS
    a, b = place[0], place[1]

    def fetch(group):
        at = pl.ds(group * UNROLL, UNROLL)
        return pltpu.make_async_copy(tiles_from.at[at], tiles_ref.at[at], refs[0].at[group])

    if load:
        for group in range(count // UNROLL):
            fetch(group).start()
    for s in range(n_row):
        degree = 1.0 + jnp.sum(terms_ref[a ^ s], axis=0)
        scale = 1.0 / jnp.sqrt(degree)
        for o in range(owned):
            at = slice(o * TB, (o + 1) * TB)
            if s == 0:
                scale_ref[:, at] = scale[o : o + 1]
            for c in range(CHUNKS):
                high, low = two_parts(sources[s][c][:, at] * scale[o : o + 1])
                for first, value in ((c * part, high), (k + c * part, low)):
                    operand[s * owned + o, first : first + part, 0:TB] = value
                    operand[s * owned + o, first : first + part, TB : 2 * TB] = value

    def body(group, total):
        if load:
            fetch(group).wait()
        for t in range(UNROLL):
            index = group * UNROLL + t
            row, col = rows[index], cols[index]
            where_from = (lax.div(col, owned) ^ a) * owned + lax.rem(col, owned)
            where_to = (lax.div(row, owned) ^ b) * owned + lax.rem(row, owned)
            both = lax.dot_general(
                operand[where_from],
                jnp.concatenate(two_parts(tiles_ref[index]), axis=1),
                (((1,), (1,)), ((), ())),
                preferred_element_type=jnp.float32,
            )
            total = both[0:k] + both[k : 2 * k] + jnp.where(same_row(rows, index), total, 0.0)
            sums[where_to] = total
        return total

    lax.fori_loop(0, count // UNROLL, body, jnp.zeros((k, TB), jnp.float32))
    half = n_col // 2
    for d in range(n_col):
        at = d % 2 * half + d // 2
        outs = keeps if at < half else gives
        for o in range(owned):
            for c in range(CHUNKS):
                outs[c][at % half, :, o * TB : (o + 1) * TB] = sums[
                    d * owned + o, c * part : (c + 1) * part
                ]


def products(sources, terms, tiles, rows, cols, place, n_row, n_col, load):
    part, width = sources[0].shape
    k = part * CHUNKS
    owned = width // TB
    count = tiles.shape[0]
    half = jax.ShapeDtypeStruct((n_col // 2, part, width), jnp.float32)
    loaded = [jax.ShapeDtypeStruct(tiles.shape, tiles.dtype)] * load
    if load:
        tiles = pltpu.with_memory_space_constraint(tiles, pltpu.HBM)
    outs = pl.pallas_call(
        functools.partial(product_kernel, n_row, n_col, owned, load),
        out_shape=[half] * (2 * CHUNKS)
        + [jax.ShapeDtypeStruct((1, width), jnp.float32)]
        + loaded,
        in_specs=[SCALARS] * 3
        + [VECTORS] * (n_row * CHUNKS + 1)
        + [pl.BlockSpec(memory_space=pltpu.HBM) if load else VECTORS],
        out_specs=[VECTORS] * (2 * CHUNKS + 1 + load),
        scratch_shapes=[
            pltpu.VMEM((n_row * owned, 2 * k, 2 * TB), jnp.bfloat16),
            pltpu.VMEM((n_col * owned, k, TB), jnp.float32),
        ]
        + [pltpu.SemaphoreType.DMA((count // UNROLL,))] * load,
        compiler_params=pltpu.CompilerParams(vmem_limit_bytes=24 << 20),
        cost_estimate=pl.CostEstimate(
            flops=count * TB * TB * 2 * k * 4,
            bytes_accessed=count * TB * TB * 4,
            transcendentals=0,
        ),
        name="products",
    )(rows, cols, place, *sources, terms, tiles)
    return outs[:CHUNKS], outs[CHUNKS : 2 * CHUNKS], *outs[2 * CHUNKS :]


def gram_kernel(mean, *refs):
    *values, out_ref = refs
    value = jnp.concatenate([ref[...] for ref in values], axis=0)
    parts = jnp.concatenate(two_parts(value), axis=0)
    gram = lax.dot_general(
        parts, parts, (((1,), (1,)), ((), ())), preferred_element_type=jnp.float32
    )
    k = value.shape[0]
    gram = mean * (gram[:k, :k] + (gram[:k, k:] + gram[k:, :k]) + gram[k:, k:])
    rows = out_ref.shape[1]
    packed = jnp.concatenate(
        [gram[q * rows : (q + 1) * rows] for q in range(gram.shape[0] // rows)], axis=1
    )
    for d in range(out_ref.shape[0]):
        out_ref[d] = packed


def gram_sum_kernel(parts_ref, out_ref):
    total = jnp.sum(parts_ref[...], axis=0)
    k = out_ref.shape[0]
    rows = total.shape[0]
    for q in range(k // rows):
        out_ref[q * rows : (q + 1) * rows, :] = total[:, q * k : (q + 1) * k]


def swap(value, axis, size, by):
    return lax.ppermute(value, axis, [(i, i ^ by) for i in range(size)])


def on_device(vectors, tiles, tile_row, tile_col):
    rows, cols = tile_row[0], tile_col[0]
    n_row = lax.axis_size("row")
    n_col = lax.axis_size("col")
    devices = n_row * n_col
    k, width = vectors.shape
    owned = width // TB
    part = k // CHUNKS
    chunks = range(CHUNKS)
    place = jnp.stack([lax.axis_index("row"), lax.axis_index("col")]).astype(jnp.int32)

    def spread(value):
        return [value] + [swap(value, "row", n_row, s) for s in reversed(range(1, n_row))][::-1]

    gathered = spread(vectors)
    sent = degree_terms(tiles, rows, n_row, n_col, owned)
    sent, gathered = lax.optimization_barrier((sent, gathered))
    terms = lax.all_to_all(
        sent.reshape(devices, owned, TB), ("row", "col"), 0, 0, tiled=True
    ).reshape(n_row, n_col, owned, TB)

    cut = lambda value: [value[c * part : (c + 1) * part] for c in chunks]
    sources = sum([cut(value) for value in gathered], [])
    current, previous = cut(vectors), None
    for step in range(STEPS):
        keeps, gives, scale, *loaded = products(
            sources, terms, tiles, rows, cols, place, n_row, n_col, step == 0
        )
        if loaded:
            tiles = loaded[0]
        chips = [keeps[c] + swap(gives[c], "col", n_col, 1) for c in chunks]
        taken = [
            [chips[c][0]]
            + [swap(chips[c][j], "col", n_col, 2 * j) for j in reversed(range(1, n_col // 2))]
            for c in chunks
        ]
        following, spreads = [], []
        for c in chunks:
            terms_here = taken[c]
            if spreads:
                terms_here, spreads[-1] = lax.optimization_barrier((terms_here, spreads[-1]))
            value = sum(terms_here[1:], terms_here[0]) * scale
            if step > 0:
                value = 2.0 * value - previous[c]
            following.append(value)
            if step < STEPS - 1:
                spreads.append(spread(value))
        previous, current = current, following
        if step < STEPS - 1:
            sources = [spreads[c][s] for s in range(n_row) for c in chunks]

    packed = jax.ShapeDtypeStruct((devices, k * k // TB, TB), jnp.float32)
    grams = pl.pallas_call(
        functools.partial(gram_kernel, 1.0 / (width * devices)),
        out_shape=packed,
        in_specs=[VECTORS] * CHUNKS,
        out_specs=VECTORS,
        name="gram",
    )(*current)
    grams = lax.all_to_all(grams, ("row", "col"), 0, 0, tiled=True)
    gram = pl.pallas_call(
        gram_sum_kernel,
        out_shape=jax.ShapeDtypeStruct((k, k), jnp.float32),
        in_specs=[VECTORS],
        out_specs=VECTORS,
        name="gram_sum",
    )(grams)
    return (jnp.concatenate(current, axis=0), gram)


def solution(mesh):
    in_specs = (
        P(None, ("row", "col")),
        P(("row", "col"), None, None),
        P(("row", "col"), None),
        P(("row", "col"), None),
    )
    out_specs = (P(None, ("row", "col")), P())
    return jax.shard_map(
        on_device, mesh=mesh, in_specs=in_specs, out_specs=out_specs, check_vma=False
    )
```

time: 276 us -> 120 us (0.43)
  blocking collectives: 99.2 us -> 11.4 us
  matrix products: 53.1 us -> 0 us
  waiting for transfers between devices: 89.3 us -> 50.7 us
  starting transfers between devices: 0.12 us -> 32.1 us
  Pallas kernels: 0 us -> 23.1 us
  between operations: 14.6 us -> 0.8 us
  other arithmetic: 10.4 us -> 1.04 us
  local copies, waits for them, and re-layouts: 7.97 us -> 0.75 us
    reduce_scatter x3 -> x0, waiting for transfers between devices: 89.3 us -> none  [operate(): lax.psum_scatter(partial_value, 'col', scatter_dimension=1, tiled=True)]
    dot_general x8 -> x0, matrix products: 53.1 us -> none  [the longest x3 46.4 us: operate(): jnp.einsum('tij,ktj->kti', tiles, picked, precision=lax.Precision.HIGHEST)]
    ppermute x0 -> x21, waiting for transfers between devices: none -> 42.6 us  [swap(): return lax.ppermute(value, axis, [(i, i ^ by) for i in range(size)])]
    psum x1 -> x0, blocking collectives: 38.1 us -> none  [on_device(): gram = lax.psum(local_gram, ('row', 'col')) / (width * n_row * n_col)]
    all_gather x3 -> x0, blocking collectives: 30.9 us -> none  [operate(): panel = lax.all_gather(scaled, 'row', axis=1, tiled=True)]
    unnamed x1 -> x0, blocking collectives: 30.3 us -> none
    ppermute x0 -> x21, starting transfers between devices: none -> 25.8 us  [swap(): return lax.ppermute(value, axis, [(i, i ^ by) for i in range(size)])]
    pallas_call x0 -> x6, Pallas kernels: none -> 23.1 us  [the longest x3 13.9 us: products(): pl.pallas_call(functools.partial(product_kernel, n_row, n_col, owned, loa...]
  transfers between devices with their start and end apart: 3 -> 22, of which waited for: 3 -> 17; matrix products, arithmetic and copies ran while one was open for 0% -> 0% of each run, Pallas kernels for 0% -> 5%
where the time goes in v2:
time: 120 us
  waiting for transfers between devices  50.7 us (42%)
  starting transfers between devices  32.1 us (27%)
  Pallas kernels  23.1 us (19%)
  blocking collectives  11.4 us (10%)
    ppermute x21, waiting for transfers between devices, swap(): return lax.ppermute(value, axis, [(i, i ^ by) for i in range(size)])  42.6 us
    ppermute x21, starting transfers between devices, swap(): return lax.ppermute(value, axis, [(i, i ^ by) for i in range(size)])  25.8 us
    pallas_call x3, Pallas kernels, products(): pl.pallas_call(functools.partial(product_kernel, n_row, n_col, owned, loa...  13.9 us
    all_to_all x1, blocking collectives, on_device(): grams = lax.all_to_all(grams, ('row', 'col'), 0, 0, tiled=True)  11.4 us
    all_to_all x1, waiting for transfers between devices, on_device(): lax.all_to_all(sent.reshape(devices, owned, TB), ('row', 'col'), 0, 0, ti...  8.09 us
    all_to_all x1, starting transfers between devices, on_device(): lax.all_to_all(sent.reshape(devices, owned, TB), ('row', 'col'), 0, 0, ti...  6.26 us
    pallas_call x1, Pallas kernels, degree_terms(): pl.pallas_call(degree_kernel, out_shape=jax.ShapeDtypeStruct((n_row, n_co...  5.66 us
  transfers between devices with their start and end apart: 22, of which 17 were waited for; matrix products, arithmetic and copies ran while one was open for 0% of the time, Pallas kernels for 5%

profile of v2, /device:TPU:0, one launch (start us, length us, event | category | flops | bytes accessed | tf_op | source)
XLA Modules:
  0.0 119.9 jit_solution(11398045292851353632)
XLA Ops:
  0.6 0.0 copy-start
  0.6 4.0 %collective-permute-start.2 = (f32[32,1024]{1,0:T(8,128)}, f32[32,1024]{1,0:T(8,128)S(1)}, u32[]{:S(2)}, u32[]{:S(2)}) collective-permute-start(f32[32,1024]{1,0:T(8,128)} %refs_0_), channel_id=1, source_target_pairs={{0,24},{8,16},{16,8},{24,0},{1,25},{9,17},{17,9},{25,1},{2,26},{10... | collective-permute-start | bytes 393224 | tf_op jit(solution)/shard_map/ppermute | solution.py:206
  4.6 0.5 collective-permute-start.1
  5.1 0.1 collective-permute-start
  5.2 0.0 copy-start.1
  5.2 0.7 copy-done.1
  5.9 0.0 copy-start.2
  5.9 5.7 %degree_terms.1 = f32[4,8,8,128]{3,2,1,0:T(8,128)} custom-call(s32[128]{0:T(128)S(1)} %bitcast.68, f32[128,128,128]{2,1,0:T(8,128)} %refs_5_.1), custom_call_target="tpu_custom_call" | custom-call | flops 134217728 | bytes 8388608 | tf_op jit(solution)/shard_map/degree_terms/pallas_call | solution.py:64
  11.6 0.0 collective-permute-done.2.refs_3_
  11.6 0.0 collective-permute-done.1.refs_2_
  11.6 0.0 collective-permute-done.refs_1_
  11.6 6.3 %all-to-all-start = ((f32[32,8,128]{2,1,0:T(8,128)}), f32[32,8,128]{2,1,0:T(8,128)S(1)}, u32[]{:S(2)}, u32[]{:S(2)}) async-start(f32[32,8,128]{2,1,0:T(8,128)} %bitcast.4), calls=%async_computation | async-start | bytes 262144 | tf_op jit(solution)/shard_map/all_to_all | solution.py:226
  17.9 0.1 pad_add_fusion.place
  17.9 8.1 %all-to-all-done = f32[32,8,128]{2,1,0:T(8,128)S(1)} async-done(((f32[32,8,128]{2,1,0:T(8,128)}), f32[32,8,128]{2,1,0:T(8,128)S(1)}, u32[]{:S(2)}, u32[]{:S(2)}) %all-to-all-start) | async-done | bytes 131104 | tf_op jit(solution)/shard_map/all_to_all | solution.py:226
  26.0 0.0 copy-done
  26.0 0.0 copy-done.2
  26.0 0.0 copy-done.3
  26.1 5.6 %products.3 = (f32[4,32,1024]{2,1,0:T(8,128)S(1)}, f32[4,32,1024]{2,1,0:T(8,128)S(1)}, f32[1,1024]{1,0:T(1,128)S(1)}, f32[128,128,128]{2,1,0:T(8,128)S(1)}) custom-call(s32[128]{0:T(128)S(1)} %bitcast.69, s32[128]{0:T(128)S(1)} %bitcast.72, s32[2]{0:T(128)S(1)} %pad_add_fusion.place, f32[32,1024]{1,0:T(8,128)S(1)} %copy-done, ...), custom_call_target="tpu_custom_call" | custom-call | flops 536870912 | bytes 8388608 | tf_op jit(solution)/shard_map/products/pallas_call | solution.py:155
  31.7 0.4 collective-permute-start.3
  32.1 1.6 %collective-permute-done.3 = f32[4,32,1024]{2,1,0:T(8,128)S(1)} collective-permute-done((f32[4,32,1024]{2,1,0:T(8,128)S(1)}, f32[4,32,1024]{2,1,0:T(8,128)S(1)}, u32[]{:S(2)}, u32[]{:S(2)}) %collective-permute-start.3) | collective-permute-done | bytes 524320 | tf_op jit(solution)/shard_map/ppermute | solution.py:206
  33.7 0.1 add.36
  33.8 1.0 collective-permute-start.4
  34.8 0.0 collective-permute-start.6
  34.8 3.4 %collective-permute-start.5 = (f32[32,1024]{1,0:T(8,128)S(1)}, f32[32,1024]{1,0:T(8,128)S(1)}, u32[]{:S(2)}, u32[]{:S(2)}) collective-permute-start(f32[32,1024]{1,0:T(8,128)S(1)} %get-tuple-element.40), channel_id=1, source_target_pairs={{0,4},{1,5},{2,6},{3,7},{4,0},{5,1},{6,2},{7,3},{8,12},{9,13},{10,... | collective-permute-start | bytes 393224 | tf_op jit(solution)/shard_map/ppermute | solution.py:206
  38.2 3.8 %collective-permute-done.4 = f32[32,1024]{1,0:T(8,128)S(1)} collective-permute-done((f32[32,1024]{1,0:T(8,128)S(1)}, f32[32,1024]{1,0:T(8,128)S(1)}, u32[]{:S(2)}, u32[]{:S(2)}) %collective-permute-start.4) | collective-permute-done | bytes 131104 | tf_op jit(solution)/shard_map/ppermute | solution.py:206
  42.0 3.2 %collective-permute-done.6 = f32[32,1024]{1,0:T(8,128)S(1)} collective-permute-done((f32[32,1024]{1,0:T(8,128)S(1)}, f32[32,1024]{1,0:T(8,128)S(1)}, u32[]{:S(2)}, u32[]{:S(2)}) %collective-permute-start.6) | collective-permute-done | bytes 131104 | tf_op jit(solution)/shard_map/ppermute | solution.py:206
  45.2 2.6 %collective-permute-done.5 = f32[32,1024]{1,0:T(8,128)S(1)} collective-permute-done((f32[32,1024]{1,0:T(8,128)S(1)}, f32[32,1024]{1,0:T(8,128)S(1)}, u32[]{:S(2)}, u32[]{:S(2)}) %collective-permute-start.5) | collective-permute-done | bytes 131104 | tf_op jit(solution)/shard_map/ppermute | solution.py:206
  47.9 0.7 collective-permute-start.9
  48.6 1.5 %collective-permute-start.8 = (f32[32,1024]{1,0:T(8,128)S(1)}, f32[32,1024]{1,0:T(8,128)S(1)}, u32[]{:S(2)}, u32[]{:S(2)}) collective-permute-start(f32[32,1024]{1,0:T(8,128)S(1)} %fusion.15.refs_0_), channel_id=1, source_target_pairs={{0,16},{8,24},{16,0},{24,8},{1,17},{9,25},{17,1},{25,9},{2,18},{10... | collective-permute-start | bytes 393224 | tf_op jit(solution)/shard_map/ppermute | solution.py:206
  50.1 1.4 %collective-permute-start.7 = (f32[32,1024]{1,0:T(8,128)S(1)}, f32[32,1024]{1,0:T(8,128)S(1)}, u32[]{:S(2)}, u32[]{:S(2)}) collective-permute-start(f32[32,1024]{1,0:T(8,128)S(1)} %fusion.15.refs_0_), channel_id=1, source_target_pairs={{0,8},{8,0},{16,24},{24,16},{1,9},{9,1},{17,25},{25,17},{2,10},{10... | collective-permute-start | bytes 393224 | tf_op jit(solution)/shard_map/ppermute | solution.py:206
  51.4 3.7 %collective-permute-done.9.refs_3_ = f32[32,1024]{1,0:T(8,128)S(1)} collective-permute-done((f32[32,1024]{1,0:T(8,128)S(1)}, f32[32,1024]{1,0:T(8,128)S(1)}, u32[]{:S(2)}, u32[]{:S(2)}) %collective-permute-start.9) | collective-permute-done | bytes 131104 | tf_op jit(solution)/shard_map/ppermute | solution.py:206
  55.1 1.0 collective-permute-done.8.refs_2_
  56.1 0.0 collective-permute-done.7.refs_1_
  56.1 4.1 %products.4 = (f32[4,32,1024]{2,1,0:T(8,128)S(1)}, f32[4,32,1024]{2,1,0:T(8,128)S(1)}, f32[1,1024]{1,0:T(1,128)S(1)}) custom-call(s32[128]{0:T(128)S(1)} %bitcast.70, s32[128]{0:T(128)S(1)} %bitcast.73, s32[2]{0:T(128)S(1)} %pad_add_fusion.place, f32[32,1024]{1,0:T(8,128)S(1)} %fusion.15.refs_0_, f32[32,1024]{1,0:T(8,128)S(1)} %collective-permute-done.7.refs_1_, ...), custom_call_target="tpu_custom_call" | custom-call | flops 536870912 | bytes 8388608 | tf_op jit(solution)/shard_map/products/pallas_call | solution.py:155
  60.2 0.1 collective-permute-start.10
  60.3 1.9 %collective-permute-done.10 = f32[4,32,1024]{2,1,0:T(8,128)S(1)} collective-permute-done((f32[4,32,1024]{2,1,0:T(8,128)S(1)}, f32[4,32,1024]{2,1,0:T(8,128)S(1)}, u32[]{:S(2)}, u32[]{:S(2)}) %collective-permute-start.10) | collective-permute-done | bytes 524320 | tf_op jit(solution)/shard_map/ppermute | solution.py:206
  62.2 0.1 add.40
  62.3 1.2 collective-permute-start.11
  63.5 0.0 collective-permute-start.13
  63.5 3.3 %collective-permute-start.12 = (f32[32,1024]{1,0:T(8,128)S(1)}, f32[32,1024]{1,0:T(8,128)S(1)}, u32[]{:S(2)}, u32[]{:S(2)}) collective-permute-start(f32[32,1024]{1,0:T(8,128)S(1)} %get-tuple-element.37), channel_id=1, source_target_pairs={{0,4},{1,5},{2,6},{3,7},{4,0},{5,1},{6,2},{7,3},{8,12},{9,13},{10,... | collective-permute-start | bytes 393224 | tf_op jit(solution)/shard_map/ppermute | solution.py:206
  66.8 3.8 %collective-permute-done.11 = f32[32,1024]{1,0:T(8,128)S(1)} collective-permute-done((f32[32,1024]{1,0:T(8,128)S(1)}, f32[32,1024]{1,0:T(8,128)S(1)}, u32[]{:S(2)}, u32[]{:S(2)}) %collective-permute-start.11) | collective-permute-done | bytes 131104 | tf_op jit(solution)/shard_map/ppermute | solution.py:206
  70.6 3.8 %collective-permute-done.13 = f32[32,1024]{1,0:T(8,128)S(1)} collective-permute-done((f32[32,1024]{1,0:T(8,128)S(1)}, f32[32,1024]{1,0:T(8,128)S(1)}, u32[]{:S(2)}, u32[]{:S(2)}) %collective-permute-start.13) | collective-permute-done | bytes 131104 | tf_op jit(solution)/shard_map/ppermute | solution.py:206
  74.4 0.0 collective-permute-done.12
  74.4 0.1 fusion.11.refs_0_
  74.4 1.4 %collective-permute-start.16 = (f32[32,1024]{1,0:T(8,128)S(1)}, f32[32,1024]{1,0:T(8,128)S(1)}, u32[]{:S(2)}, u32[]{:S(2)}) collective-permute-start(f32[32,1024]{1,0:T(8,128)S(1)} %fusion.11.refs_0_), channel_id=1, source_target_pairs={{0,24},{8,16},{16,8},{24,0},{1,25},{9,17},{17,9},{25,1},{2,26},{10... | collective-permute-start | bytes 393224 | tf_op jit(solution)/shard_map/ppermute | solution.py:206
  75.8 1.4 %collective-permute-start.15 = (f32[32,1024]{1,0:T(8,128)S(1)}, f32[32,1024]{1,0:T(8,128)S(1)}, u32[]{:S(2)}, u32[]{:S(2)}) collective-permute-start(f32[32,1024]{1,0:T(8,128)S(1)} %fusion.11.refs_0_), channel_id=1, source_target_pairs={{0,16},{8,24},{16,0},{24,8},{1,17},{9,25},{17,1},{25,9},{2,18},{10... | collective-permute-start | bytes 393224 | tf_op jit(solution)/shard_map/ppermute | solution.py:206
  77.2 1.0 collective-permute-start.14
  78.2 2.4 %collective-permute-done.16.refs_3_ = f32[32,1024]{1,0:T(8,128)S(1)} collective-permute-done((f32[32,1024]{1,0:T(8,128)S(1)}, f32[32,1024]{1,0:T(8,128)S(1)}, u32[]{:S(2)}, u32[]{:S(2)}) %collective-permute-start.16) | collective-permute-done | bytes 131104 | tf_op jit(solution)/shard_map/ppermute | solution.py:206
  80.7 2.1 %collective-permute-done.15.refs_2_ = f32[32,1024]{1,0:T(8,128)S(1)} collective-permute-done((f32[32,1024]{1,0:T(8,128)S(1)}, f32[32,1024]{1,0:T(8,128)S(1)}, u32[]{:S(2)}, u32[]{:S(2)}) %collective-permute-start.15) | collective-permute-done | bytes 131104 | tf_op jit(solution)/shard_map/ppermute | solution.py:206
  82.8 1.8 %collective-permute-done.14.refs_1_ = f32[32,1024]{1,0:T(8,128)S(1)} collective-permute-done((f32[32,1024]{1,0:T(8,128)S(1)}, f32[32,1024]{1,0:T(8,128)S(1)}, u32[]{:S(2)}, u32[]{:S(2)}) %collective-permute-start.14) | collective-permute-done | bytes 131104 | tf_op jit(solution)/shard_map/ppermute | solution.py:206
  84.5 4.1 %products.5 = (f32[4,32,1024]{2,1,0:T(8,128)S(1)}, f32[4,32,1024]{2,1,0:T(8,128)S(1)}, f32[1,1024]{1,0:T(1,128)S(1)}) custom-call(s32[128]{0:T(128)S(1)} %bitcast.71, s32[128]{0:T(128)S(1)} %bitcast.74, s32[2]{0:T(128)S(1)} %pad_add_fusion.place, f32[32,1024]{1,0:T(8,128)S(1)} %fusion.11.refs_0_, f32[32,1024]{1,0:T(8,128)S(1)} %collective-permute-done.14.refs_1_, ...), custom_call_target="tpu_custom_call" | custom-call | flops 536870912 | bytes 8388608 | tf_op jit(solution)/shard_map/products/pallas_call | solution.py:155
  88.7 0.1 collective-permute-start.17
  88.8 1.9 %collective-permute-done.17 = f32[4,32,1024]{2,1,0:T(8,128)S(1)} collective-permute-done((f32[4,32,1024]{2,1,0:T(8,128)S(1)}, f32[4,32,1024]{2,1,0:T(8,128)S(1)}, u32[]{:S(2)}, u32[]{:S(2)}) %collective-permute-start.17) | collective-permute-done | bytes 524320 | tf_op jit(solution)/shard_map/ppermute | solution.py:206
  90.7 0.1 add.44
  90.8 1.3 %collective-permute-start.18 = (f32[32,1024]{1,0:T(8,128)S(1)}, f32[32,1024]{1,0:T(8,128)S(1)}, u32[]{:S(2)}, u32[]{:S(2)}) collective-permute-start(f32[32,1024]{1,0:T(8,128)S(1)} %get-tuple-element.32), channel_id=1, source_target_pairs={{0,6},{1,7},{2,4},{3,5},{4,2},{5,3},{6,0},{7,1},{8,14},{9,15},{10,... | collective-permute-start | bytes 393224 | tf_op jit(solution)/shard_map/ppermute | solution.py:206
  92.1 0.0 collective-permute-start.20
  92.1 3.1 %collective-permute-start.19 = (f32[32,1024]{1,0:T(8,128)S(1)}, f32[32,1024]{1,0:T(8,128)S(1)}, u32[]{:S(2)}, u32[]{:S(2)}) collective-permute-start(f32[32,1024]{1,0:T(8,128)S(1)} %get-tuple-element.34), channel_id=1, source_target_pairs={{0,4},{1,5},{2,6},{3,7},{4,0},{5,1},{6,2},{7,3},{8,12},{9,13},{10,... | collective-permute-start | bytes 393224 | tf_op jit(solution)/shard_map/ppermute | solution.py:206
  95.2 3.8 %collective-permute-done.18 = f32[32,1024]{1,0:T(8,128)S(1)} collective-permute-done((f32[32,1024]{1,0:T(8,128)S(1)}, f32[32,1024]{1,0:T(8,128)S(1)}, u32[]{:S(2)}, u32[]{:S(2)}) %collective-permute-start.18) | collective-permute-done | bytes 131104 | tf_op jit(solution)/shard_map/ppermute | solution.py:206
  99.0 3.6 %collective-permute-done.20 = f32[32,1024]{1,0:T(8,128)S(1)} collective-permute-done((f32[32,1024]{1,0:T(8,128)S(1)}, f32[32,1024]{1,0:T(8,128)S(1)}, u32[]{:S(2)}, u32[]{:S(2)}) %collective-permute-start.20) | collective-permute-done | bytes 131104 | tf_op jit(solution)/shard_map/ppermute | solution.py:206
  102.7 1.6 %collective-permute-done.19 = f32[32,1024]{1,0:T(8,128)S(1)} collective-permute-done((f32[32,1024]{1,0:T(8,128)S(1)}, f32[32,1024]{1,0:T(8,128)S(1)}, u32[]{:S(2)}, u32[]{:S(2)}) %collective-permute-start.19) | collective-permute-done | bytes 131104 | tf_op jit(solution)/shard_map/ppermute | solution.py:206
  104.2 0.7 fusion.5.refs_0_
  104.9 1.9 %gram.1 = f32[32,8,128]{2,1,0:T(8,128)} custom-call(f32[32,1024]{1,0:T(8,128)} %fusion.5.refs_0_), custom_call_target="tpu_custom_call" | custom-call | tf_op jit(solution)/shard_map/gram/pallas_call | solution.py:261
  106.8 11.4 %all_to_all.10.parts_ref = f32[32,8,128]{2,1,0:T(8,128)} all-to-all(f32[32,8,128]{2,1,0:T(8,128)} %gram.1), channel_id=1, replica_groups=mesh['row'=4,'col'=8] {'row','col'}, dimensions={0} | all-to-all | bytes 262144 | tf_op jit(solution)/shard_map/all_to_all | solution.py:268
  118.3 1.6 %gram_sum.1 = f32[32,32]{1,0:T(8,128)} custom-call(f32[32,8,128]{2,1,0:T(8,128)} %all_to_all.10.parts_ref), custom_call_target="tpu_custom_call" | custom-call | tf_op jit(solution)/shard_map/gram_sum/pallas_call | solution.py:269
  (5 shorter events, 0.1 us)
Async XLA Ops:
  0.6 25.4 %copy-start = (f32[32,1024]{1,0:T(8,128)S(1)}, f32[32,1024]{1,0:T(8,128)}, u32[]{:S(2)}) copy-start(f32[32,1024]{1,0:T(8,128)} %refs_0_) | copy-start | bytes 393220
  0.6 10.9 %collective-permute-start.2 = (f32[32,1024]{1,0:T(8,128)}, f32[32,1024]{1,0:T(8,128)S(1)}, u32[]{:S(2)}, u32[]{:S(2)}) collective-permute-start(f32[32,1024]{1,0:T(8,128)} %refs_0_), channel_id=1, source_target_pairs={{0,24},{8,16},{16,8},{24,0},{1,25},{9,17},{17,9},{25,1},{2,26},{10... | collective-permute-start | bytes 393224 | tf_op jit(solution)/shard_map/ppermute | solution.py:206
  4.6 7.0 %collective-permute-start.1 = (f32[32,1024]{1,0:T(8,128)}, f32[32,1024]{1,0:T(8,128)S(1)}, u32[]{:S(2)}, u32[]{:S(2)}) collective-permute-start(f32[32,1024]{1,0:T(8,128)} %refs_0_), channel_id=1, source_target_pairs={{0,16},{8,24},{16,0},{24,8},{1,17},{9,25},{17,1},{25,9},{2,18},{10... | collective-permute-start | bytes 393224 | tf_op jit(solution)/shard_map/ppermute | solution.py:206
  5.1 6.5 %collective-permute-start = (f32[32,1024]{1,0:T(8,128)}, f32[32,1024]{1,0:T(8,128)S(1)}, u32[]{:S(2)}, u32[]{:S(2)}) collective-permute-start(f32[32,1024]{1,0:T(8,128)} %refs_0_), channel_id=1, source_target_pairs={{0,8},{8,0},{16,24},{24,16},{1,9},{9,1},{17,25},{25,17},{2,10},{10... | collective-permute-start | bytes 393224 | tf_op jit(solution)/shard_map/ppermute | solution.py:206
  5.2 0.7 copy-start.1
  5.9 20.1 %copy-start.2 = (s32[1,128]{1,0:T(1,128)S(1)}, s32[1,128]{1,0:T(1,128)}, u32[]{:S(2)}) copy-start(s32[1,128]{1,0:T(1,128)} %param.6) | copy-start | bytes 1540
  5.9 20.1 %copy-start.3 = (s32[1,128]{1,0:T(1,128)S(1)}, s32[1,128]{1,0:T(1,128)}, u32[]{:S(2)}) copy-start(s32[1,128]{1,0:T(1,128)} %param.7) | copy-start | bytes 1540
  11.6 14.4 %all-to-all-start = ((f32[32,8,128]{2,1,0:T(8,128)}), f32[32,8,128]{2,1,0:T(8,128)S(1)}, u32[]{:S(2)}, u32[]{:S(2)}) async-start(f32[32,8,128]{2,1,0:T(8,128)} %bitcast.4), calls=%async_computation | async-start | bytes 262144 | tf_op jit(solution)/shard_map/all_to_all | solution.py:226
  31.7 2.0 %collective-permute-start.3 = (f32[4,32,1024]{2,1,0:T(8,128)S(1)}, f32[4,32,1024]{2,1,0:T(8,128)S(1)}, u32[]{:S(2)}, u32[]{:S(2)}) collective-permute-start(f32[4,32,1024]{2,1,0:T(8,128)S(1)} %get-tuple-element.23), channel_id=1, source_target_pairs={{0,1},{1,0},{2,3},{3,2},{4,5},{5,4},{6,7},{7,6},{8,9},{9,8},{10,11... | collective-permute-start | bytes 1572872 | tf_op jit(solution)/shard_map/ppermute | solution.py:206
  33.8 8.2 %collective-permute-start.4 = (f32[32,1024]{1,0:T(8,128)S(1)}, f32[32,1024]{1,0:T(8,128)S(1)}, u32[]{:S(2)}, u32[]{:S(2)}) collective-permute-start(f32[32,1024]{1,0:T(8,128)S(1)} %get-tuple-element.38), channel_id=1, source_target_pairs={{0,6},{1,7},{2,4},{3,5},{4,2},{5,3},{6,0},{7,1},{8,14},{9,15},{10,... | collective-permute-start | bytes 393224 | tf_op jit(solution)/shard_map/ppermute | solution.py:206
  34.8 10.4 %collective-permute-start.6 = (f32[32,1024]{1,0:T(8,128)S(1)}, f32[32,1024]{1,0:T(8,128)S(1)}, u32[]{:S(2)}, u32[]{:S(2)}) collective-permute-start(f32[32,1024]{1,0:T(8,128)S(1)} %get-tuple-element.39), channel_id=1, source_target_pairs={{0,2},{1,3},{2,0},{3,1},{4,6},{5,7},{6,4},{7,5},{8,10},{9,11},{10,... | collective-permute-start | bytes 393224 | tf_op jit(solution)/shard_map/ppermute | solution.py:206
  34.8 13.0 %collective-permute-start.5 = (f32[32,1024]{1,0:T(8,128)S(1)}, f32[32,1024]{1,0:T(8,128)S(1)}, u32[]{:S(2)}, u32[]{:S(2)}) collective-permute-start(f32[32,1024]{1,0:T(8,128)S(1)} %get-tuple-element.40), channel_id=1, source_target_pairs={{0,4},{1,5},{2,6},{3,7},{4,0},{5,1},{6,2},{7,3},{8,12},{9,13},{10,... | collective-permute-start | bytes 393224 | tf_op jit(solution)/shard_map/ppermute | solution.py:206
  47.9 7.2 %collective-permute-start.9 = (f32[32,1024]{1,0:T(8,128)S(1)}, f32[32,1024]{1,0:T(8,128)S(1)}, u32[]{:S(2)}, u32[]{:S(2)}) collective-permute-start(f32[32,1024]{1,0:T(8,128)S(1)} %fusion.15.refs_0_), channel_id=1, source_target_pairs={{0,24},{8,16},{16,8},{24,0},{1,25},{9,17},{17,9},{25,1},{2,26},{10... | collective-permute-start | bytes 393224 | tf_op jit(solution)/shard_map/ppermute | solution.py:206
  48.6 7.5 %collective-permute-start.8 = (f32[32,1024]{1,0:T(8,128)S(1)}, f32[32,1024]{1,0:T(8,128)S(1)}, u32[]{:S(2)}, u32[]{:S(2)}) collective-permute-start(f32[32,1024]{1,0:T(8,128)S(1)} %fusion.15.refs_0_), channel_id=1, source_target_pairs={{0,16},{8,24},{16,0},{24,8},{1,17},{9,25},{17,1},{25,9},{2,18},{10... | collective-permute-start | bytes 393224 | tf_op jit(solution)/shard_map/ppermute | solution.py:206
  50.1 6.0 %collective-permute-start.7 = (f32[32,1024]{1,0:T(8,128)S(1)}, f32[32,1024]{1,0:T(8,128)S(1)}, u32[]{:S(2)}, u32[]{:S(2)}) collective-permute-start(f32[32,1024]{1,0:T(8,128)S(1)} %fusion.15.refs_0_), channel_id=1, source_target_pairs={{0,8},{8,0},{16,24},{24,16},{1,9},{9,1},{17,25},{25,17},{2,10},{10... | collective-permute-start | bytes 393224 | tf_op jit(solution)/shard_map/ppermute | solution.py:206
  60.2 2.0 %collective-permute-start.10 = (f32[4,32,1024]{2,1,0:T(8,128)S(1)}, f32[4,32,1024]{2,1,0:T(8,128)S(1)}, u32[]{:S(2)}, u32[]{:S(2)}) collective-permute-start(f32[4,32,1024]{2,1,0:T(8,128)S(1)} %get-tuple-element.27), channel_id=1, source_target_pairs={{0,1},{1,0},{2,3},{3,2},{4,5},{5,4},{6,7},{7,6},{8,9},{9,8},{10,11... | collective-permute-start | bytes 1572872 | tf_op jit(solution)/shard_map/ppermute | solution.py:206
  62.3 8.3 %collective-permute-start.11 = (f32[32,1024]{1,0:T(8,128)S(1)}, f32[32,1024]{1,0:T(8,128)S(1)}, u32[]{:S(2)}, u32[]{:S(2)}) collective-permute-start(f32[32,1024]{1,0:T(8,128)S(1)} %get-tuple-element.35), channel_id=1, source_target_pairs={{0,6},{1,7},{2,4},{3,5},{4,2},{5,3},{6,0},{7,1},{8,14},{9,15},{10,... | collective-permute-start | bytes 393224 | tf_op jit(solution)/shard_map/ppermute | solution.py:206
  63.5 10.9 %collective-permute-start.13 = (f32[32,1024]{1,0:T(8,128)S(1)}, f32[32,1024]{1,0:T(8,128)S(1)}, u32[]{:S(2)}, u32[]{:S(2)}) collective-permute-start(f32[32,1024]{1,0:T(8,128)S(1)} %get-tuple-element.36), channel_id=1, source_target_pairs={{0,2},{1,3},{2,0},{3,1},{4,6},{5,7},{6,4},{7,5},{8,10},{9,11},{10,... | collective-permute-start | bytes 393224 | tf_op jit(solution)/shard_map/ppermute | solution.py:206
  63.5 10.9 %collective-permute-start.12 = (f32[32,1024]{1,0:T(8,128)S(1)}, f32[32,1024]{1,0:T(8,128)S(1)}, u32[]{:S(2)}, u32[]{:S(2)}) collective-permute-start(f32[32,1024]{1,0:T(8,128)S(1)} %get-tuple-element.37), channel_id=1, source_target_pairs={{0,4},{1,5},{2,6},{3,7},{4,0},{5,1},{6,2},{7,3},{8,12},{9,13},{10,... | collective-permute-start | bytes 393224 | tf_op jit(solution)/shard_map/ppermute | solution.py:206
  74.4 6.2 %collective-permute-start.16 = (f32[32,1024]{1,0:T(8,128)S(1)}, f32[32,1024]{1,0:T(8,128)S(1)}, u32[]{:S(2)}, u32[]{:S(2)}) collective-permute-start(f32[32,1024]{1,0:T(8,128)S(1)} %fusion.11.refs_0_), channel_id=1, source_target_pairs={{0,24},{8,16},{16,8},{24,0},{1,25},{9,17},{17,9},{25,1},{2,26},{10... | collective-permute-start | bytes 393224 | tf_op jit(solution)/shard_map/ppermute | solution.py:206
  75.8 7.0 %collective-permute-start.15 = (f32[32,1024]{1,0:T(8,128)S(1)}, f32[32,1024]{1,0:T(8,128)S(1)}, u32[]{:S(2)}, u32[]{:S(2)}) collective-permute-start(f32[32,1024]{1,0:T(8,128)S(1)} %fusion.11.refs_0_), channel_id=1, source_target_pairs={{0,16},{8,24},{16,0},{24,8},{1,17},{9,25},{17,1},{25,9},{2,18},{10... | collective-permute-start | bytes 393224 | tf_op jit(solution)/shard_map/ppermute | solution.py:206
  77.2 7.3 %collective-permute-start.14 = (f32[32,1024]{1,0:T(8,128)S(1)}, f32[32,1024]{1,0:T(8,128)S(1)}, u32[]{:S(2)}, u32[]{:S(2)}) collective-permute-start(f32[32,1024]{1,0:T(8,128)S(1)} %fusion.11.refs_0_), channel_id=1, source_target_pairs={{0,8},{8,0},{16,24},{24,16},{1,9},{9,1},{17,25},{25,17},{2,10},{10... | collective-permute-start | bytes 393224 | tf_op jit(solution)/shard_map/ppermute | solution.py:206
  88.7 2.0 %collective-permute-start.17 = (f32[4,32,1024]{2,1,0:T(8,128)S(1)}, f32[4,32,1024]{2,1,0:T(8,128)S(1)}, u32[]{:S(2)}, u32[]{:S(2)}) collective-permute-start(f32[4,32,1024]{2,1,0:T(8,128)S(1)} %get-tuple-element.30), channel_id=1, source_target_pairs={{0,1},{1,0},{2,3},{3,2},{4,5},{5,4},{6,7},{7,6},{8,9},{9,8},{10,11... | collective-permute-start | bytes 1572872 | tf_op jit(solution)/shard_map/ppermute | solution.py:206
  90.8 8.3 %collective-permute-start.18 = (f32[32,1024]{1,0:T(8,128)S(1)}, f32[32,1024]{1,0:T(8,128)S(1)}, u32[]{:S(2)}, u32[]{:S(2)}) collective-permute-start(f32[32,1024]{1,0:T(8,128)S(1)} %get-tuple-element.32), channel_id=1, source_target_pairs={{0,6},{1,7},{2,4},{3,5},{4,2},{5,3},{6,0},{7,1},{8,14},{9,15},{10,... | collective-permute-start | bytes 393224 | tf_op jit(solution)/shard_map/ppermute | solution.py:206
  92.1 10.6 %collective-permute-start.20 = (f32[32,1024]{1,0:T(8,128)S(1)}, f32[32,1024]{1,0:T(8,128)S(1)}, u32[]{:S(2)}, u32[]{:S(2)}) collective-permute-start(f32[32,1024]{1,0:T(8,128)S(1)} %get-tuple-element.33), channel_id=1, source_target_pairs={{0,2},{1,3},{2,0},{3,1},{4,6},{5,7},{6,4},{7,5},{8,10},{9,11},{10,... | collective-permute-start | bytes 393224 | tf_op jit(solution)/shard_map/ppermute | solution.py:206
  92.1 12.1 %collective-permute-start.19 = (f32[32,1024]{1,0:T(8,128)S(1)}, f32[32,1024]{1,0:T(8,128)S(1)}, u32[]{:S(2)}, u32[]{:S(2)}) collective-permute-start(f32[32,1024]{1,0:T(8,128)S(1)} %get-tuple-element.34), channel_id=1, source_target_pairs={{0,4},{1,5},{2,6},{3,7},{4,0},{5,1},{6,2},{7,3},{8,12},{9,13},{10,... | collective-permute-start | bytes 393224 | tf_op jit(solution)/shard_map/ppermute | solution.py:206

commit v3 on v2

v3 whole, which is shorter than its diff:
```python
import functools

import jax
import jax.numpy as jnp
from jax import lax
from jax.experimental import pallas as pl
from jax.experimental.pallas import tpu as pltpu
from jax.sharding import PartitionSpec as P

TB = 128
STEPS = 3
GROUP = 16
UNROLL = 32

SCALARS = pl.BlockSpec(memory_space=pltpu.SMEM)
VECTORS = pl.BlockSpec(memory_space=pltpu.VMEM)


def same_row(rows, index):
    return jnp.logical_and(index > 0, rows[index] == rows[jnp.maximum(index - 1, 0)])


def two_parts(value):
    high = value.astype(jnp.bfloat16)
    return high, (value - high.astype(jnp.float32)).astype(jnp.bfloat16)


def degree_kernel(rows, tiles_hbm, sent_ref, buffer, arrived):
    count = tiles_hbm.shape[0]
    groups = count // GROUP
    n_row, n_col, owned, _ = sent_ref.shape
    lane = lax.broadcasted_iota(jnp.int32, (TB, TB), 1)

    def fetch(group):
        at = pl.ds(group * GROUP, GROUP)
        return pltpu.make_async_copy(tiles_hbm.at[at], buffer.at[at], arrived.at[group])

    for group in range(groups):
        fetch(group).start()

    def body(group, total):
        fetch(group).wait()
        for t in range(GROUP):
            index = group * GROUP + t
            sums = jnp.sum(jnp.abs(buffer[index]), axis=1, keepdims=True)
            total = total + jnp.where(lane == rows[index], sums, 0.0)
        return total

    total = lax.fori_loop(0, groups, body, jnp.zeros((TB, TB), jnp.float32)).T
    for s in range(n_row):
        for d in range(n_col):
            sent_ref[s, d] = total[d * owned : (d + 1) * owned]


def degree_terms(tiles, rows, n_row, n_col, owned):
    count = tiles.shape[0]
    assert n_col * owned <= TB
    return pl.pallas_call(
        degree_kernel,
        out_shape=pltpu.VMEM((n_row, n_col, owned, TB), jnp.float32),
        in_specs=[SCALARS, pl.BlockSpec(memory_space=pltpu.HBM)],
        out_specs=VECTORS,
        scratch_shapes=[
            pltpu.VMEM(tiles.shape, jnp.float32),
            pltpu.SemaphoreType.DMA((count // GROUP,)),
        ],
        compiler_params=pltpu.CompilerParams(vmem_limit_bytes=24 << 20),
        cost_estimate=pl.CostEstimate(
            flops=count * TB * TB * 2, bytes_accessed=count * TB * TB * 4, transcendentals=0
        ),
        name="degree_terms",
    )(
        pltpu.with_memory_space_constraint(rows, pltpu.HBM),
        pltpu.with_memory_space_constraint(tiles, pltpu.HBM),
    )


def product_kernel(n_row, n_col, owned, load, rows, cols, place, *refs):
    refs = list(refs)
    take = lambda n: [refs.pop(0) for _ in range(n)]
    sources = take(n_row)
    terms_ref, tiles_from, keep_ref, give_ref, scale_ref = take(5)
    tiles_ref = refs.pop(0) if load else tiles_from
    operand, sums = take(2)
    count = tiles_ref.shape[0]
    k = keep_ref.shape[1]
    a, b = place[0], place[1]

    def fetch(group):
        at = pl.ds(group * UNROLL, UNROLL)
        return pltpu.make_async_copy(tiles_from.at[at], tiles_ref.at[at], refs[0].at[group])

    if load:
        for group in range(count // UNROLL):
            fetch(group).start()
    for s in range(n_row):
        degree = 1.0 + jnp.sum(terms_ref[a ^ s], axis=0)
        scale = 1.0 / jnp.sqrt(degree)
        for o in range(owned):
            at = slice(o * TB, (o + 1) * TB)
            if s == 0:
                scale_ref[:, at] = scale[o : o + 1]
            parts = two_parts(sources[s][:, at] * scale[o : o + 1])
            for i, value in enumerate(parts):
                operand[s * owned + o, i * k : (i + 1) * k, 0:TB] = value
                operand[s * owned + o, i * k : (i + 1) * k, TB : 2 * TB] = value

    def body(group, total):
        if load:
            fetch(group).wait()
        for t in range(UNROLL):
            index = group * UNROLL + t
            row, col = rows[index], cols[index]
            where_from = (lax.div(col, owned) ^ a) * owned + lax.rem(col, owned)
            where_to = (lax.div(row, owned) ^ b) * owned + lax.rem(row, owned)
            both = lax.dot_general(
                operand[where_from],
                jnp.concatenate(two_parts(tiles_ref[index]), axis=1),
                (((1,), (1,)), ((), ())),
                preferred_element_type=jnp.float32,
            )
            total = both[0:k] + both[k : 2 * k] + jnp.where(same_row(rows, index), total, 0.0)
            sums[where_to] = total
        return total

    lax.fori_loop(0, count // UNROLL, body, jnp.zeros((k, TB), jnp.float32))
    for d in range(n_col):
        out = give_ref if d % 2 else keep_ref
        for o in range(owned):
            out[d // 2, :, o * TB : (o + 1) * TB] = sums[d * owned + o]


def products(sources, terms, tiles, rows, cols, place, n_row, n_col, load):
    k, width = sources[0].shape
    owned = width // TB
    count = tiles.shape[0]
    half = jax.ShapeDtypeStruct((n_col // 2, k, width), jnp.float32)
    loaded = [jax.ShapeDtypeStruct(tiles.shape, tiles.dtype)] * load
    if load:
        tiles = pltpu.with_memory_space_constraint(tiles, pltpu.HBM)
    return pl.pallas_call(
        functools.partial(product_kernel, n_row, n_col, owned, load),
        out_shape=[half, half, jax.ShapeDtypeStruct((1, width), jnp.float32)] + loaded,
        in_specs=[SCALARS] * 3
        + [VECTORS] * (n_row + 1)
        + [pl.BlockSpec(memory_space=pltpu.HBM) if load else VECTORS],
        out_specs=[VECTORS] * (3 + load),
        scratch_shapes=[
            pltpu.VMEM((n_row * owned, 2 * k, 2 * TB), jnp.bfloat16),
            pltpu.VMEM((n_col * owned, k, TB), jnp.float32),
        ]
        + [pltpu.SemaphoreType.DMA((count // UNROLL,))] * load,
        compiler_params=pltpu.CompilerParams(vmem_limit_bytes=24 << 20),
        cost_estimate=pl.CostEstimate(
            flops=count * TB * TB * 2 * k * 4,
            bytes_accessed=count * TB * TB * 4,
            transcendentals=0,
        ),
        name="products",
    )(rows, cols, place, *sources, terms, tiles)


def finish_kernel(mean, value_ref, filtered_ref, gram_ref, sent):
    copy = pltpu.make_async_copy(value_ref, filtered_ref, sent)
    copy.start()
    value = value_ref[...]
    k = value.shape[0]
    parts = jnp.concatenate(two_parts(value), axis=0)
    gram = lax.dot_general(
        parts, parts, (((1,), (1,)), ((), ())), preferred_element_type=jnp.float32
    )
    gram = mean * (gram[:k, :k] + (gram[:k, k:] + gram[k:, :k]) + gram[k:, k:])
    rows = gram_ref.shape[1]
    packed = jnp.concatenate([gram[q * rows : (q + 1) * rows] for q in range(k // rows)], axis=1)
    for d in range(gram_ref.shape[0]):
        gram_ref[d] = packed
    copy.wait()


def gram_sum_kernel(parts_ref, out_ref):
    total = jnp.sum(parts_ref[...], axis=0)
    k = out_ref.shape[0]
    rows = total.shape[0]
    for q in range(k // rows):
        out_ref[q * rows : (q + 1) * rows, :] = total[:, q * k : (q + 1) * k]


def swap(value, axis, size, by):
    return lax.ppermute(value, axis, [(i, i ^ by) for i in range(size)])


def on_device(vectors, tiles, tile_row, tile_col):
    rows, cols = tile_row[0], tile_col[0]
    n_row = lax.axis_size("row")
    n_col = lax.axis_size("col")
    devices = n_row * n_col
    k, width = vectors.shape
    owned = width // TB
    place = jnp.stack([lax.axis_index("row"), lax.axis_index("col")]).astype(jnp.int32)

    def spread(value):
        return [value] + [swap(value, "row", n_row, s) for s in reversed(range(1, n_row))][::-1]

    sources = spread(vectors)
    sent = degree_terms(tiles, rows, n_row, n_col, owned)
    sent, sources = lax.optimization_barrier((sent, sources))
    terms = lax.all_to_all(
        sent.reshape(devices, owned, TB), ("row", "col"), 0, 0, tiled=True
    ).reshape(n_row, n_col, owned, TB)

    previous, current = None, vectors
    for step in range(STEPS):
        keep, give, scale, *loaded = products(
            sources, terms, tiles, rows, cols, place, n_row, n_col, step == 0
        )
        if loaded:
            tiles = loaded[0]
        chip = keep + swap(give, "col", n_col, 1)
        totals = [chip[0]] + [
            swap(chip[j], "col", n_col, 2 * j) for j in reversed(range(1, n_col // 2))
        ]
        following = sum(totals[1:], totals[0]) * scale
        if step > 0:
            following = 2.0 * following - previous
        previous, current = current, following
        if step < STEPS - 1:
            sources = spread(current)

    filtered, grams = pl.pallas_call(
        functools.partial(finish_kernel, 1.0 / (width * devices)),
        out_shape=[
            jax.ShapeDtypeStruct((k, width), jnp.float32),
            pltpu.VMEM((devices, k * k // TB, TB), jnp.float32),
        ],
        in_specs=[VECTORS],
        out_specs=[pl.BlockSpec(memory_space=pltpu.HBM), VECTORS],
        scratch_shapes=[pltpu.SemaphoreType.DMA],
        name="finish",
    )(pltpu.with_memory_space_constraint(current, pltpu.VMEM))
    grams = lax.all_to_all(grams, ("row", "col"), 0, 0, tiled=True)
    gram = pl.pallas_call(
        gram_sum_kernel,
        out_shape=jax.ShapeDtypeStruct((k, k), jnp.float32),
        in_specs=[VECTORS],
        out_specs=VECTORS,
        name="gram_sum",
    )(pltpu.with_memory_space_constraint(grams, pltpu.VMEM))
    return (filtered, gram)


def solution(mesh):
    in_specs = (
        P(None, ("row", "col")),
        P(("row", "col"), None, None),
        P(("row", "col"), None),
        P(("row", "col"), None),
    )
    out_specs = (P(None, ("row", "col")), P())
    return jax.shard_map(
        on_device, mesh=mesh, in_specs=in_specs, out_specs=out_specs, check_vma=False
    )
```

time: 120 us -> 115 us (0.958)
  Pallas kernels: 23.1 us -> 20.7 us
  blocking collectives: 11.4 us -> 10.2 us
    pallas_call x2, Pallas kernels: 7.61 us -> 6.12 us  [the longest x1 5.46 us: degree_terms(): pl.pallas_call(degree_kernel, out_shape=pltpu.VMEM((n_row, n_col, owned,...]
  transfers between devices with their start and end apart: 22 -> 22, of which waited for: 17 -> 19; matrix products, arithmetic and copies ran while one was open for 0% -> 0% of each run, Pallas kernels for 5% -> 5%
where the time goes in v3:
time: 115 us
  waiting for transfers between devices  51.3 us (45%)
  starting transfers between devices  31.5 us (27%)
  Pallas kernels  20.7 us (18%)
  blocking collectives  10.2 us (9%)
    ppermute x21, waiting for transfers between devices, swap(): return lax.ppermute(value, axis, [(i, i ^ by) for i in range(size)])  43.2 us
    ppermute x21, starting transfers between devices, swap(): return lax.ppermute(value, axis, [(i, i ^ by) for i in range(size)])  25.8 us
    pallas_call x3, Pallas kernels, products(): pl.pallas_call(functools.partial(product_kernel, n_row, n_col, owned, loa...  13.9 us
    all_to_all x1, blocking collectives, on_device(): grams = lax.all_to_all(grams, ('row', 'col'), 0, 0, tiled=True)  10.2 us
    all_to_all x1, waiting for transfers between devices, on_device(): lax.all_to_all(sent.reshape(devices, owned, TB), ('row', 'col'), 0, 0, ti...  8.09 us
    all_to_all x1, starting transfers between devices, on_device(): lax.all_to_all(sent.reshape(devices, owned, TB), ('row', 'col'), 0, 0, ti...  5.63 us
    pallas_call x1, Pallas kernels, degree_terms(): pl.pallas_call(degree_kernel, out_shape=pltpu.VMEM((n_row, n_col, owned,...  5.46 us
  transfers between devices with their start and end apart: 22, of which 19 were waited for; matrix products, arithmetic and copies ran while one was open for 0% of the time, Pallas kernels for 5%

profile of v3, /device:TPU:0, one launch (start us, length us, event | category | flops | bytes accessed | tf_op | source)
XLA Modules:
  0.0 115.0 jit_solution(5158624266432910831)
XLA Ops:
  0.6 0.0 copy-start
  0.6 0.0 copy-start.1
  0.6 0.0 copy-start.2
  0.7 4.0 %collective-permute-start.2 = (f32[32,1024]{1,0:T(8,128)}, f32[32,1024]{1,0:T(8,128)S(1)}, u32[]{:S(2)}, u32[]{:S(2)}) collective-permute-start(f32[32,1024]{1,0:T(8,128)} %refs_0_), channel_id=1, source_target_pairs={{0,24},{8,16},{16,8},{24,0},{1,25},{9,17},{17,9},{25,1},{2,26},{10... | collective-permute-start | bytes 393224 | tf_op jit(solution)/shard_map/ppermute | solution.py:189
  4.6 0.5 collective-permute-start.1
  5.1 0.1 collective-permute-start
  5.3 5.5 %degree_terms.1 = f32[4,8,8,128]{3,2,1,0:T(8,128)} custom-call(s32[128]{0:T(128)} %bitcast.68, f32[128,128,128]{2,1,0:T(8,128)} %refs_5_.1), custom_call_target="tpu_custom_call" | custom-call | flops 4194304 | bytes 8388608 | tf_op jit(solution)/shard_map/degree_terms/pallas_call | solution.py:58
  10.7 0.0 collective-permute-done.2.refs_3_
  10.7 0.4 collective-permute-done.1.refs_2_
  11.1 0.2 collective-permute-done.refs_1_
  11.4 5.6 %all-to-all-start = ((f32[32,8,128]{2,1,0:T(8,128)}), f32[32,8,128]{2,1,0:T(8,128)S(1)}, u32[]{:S(2)}, u32[]{:S(2)}) async-start(f32[32,8,128]{2,1,0:T(8,128)} %bitcast.4), calls=%async_computation | async-start | bytes 262144 | tf_op jit(solution)/shard_map/all_to_all | solution.py:207
  17.0 0.1 pad_add_fusion.place
  17.1 8.1 %all-to-all-done = f32[32,8,128]{2,1,0:T(8,128)S(1)} async-done(((f32[32,8,128]{2,1,0:T(8,128)}), f32[32,8,128]{2,1,0:T(8,128)S(1)}, u32[]{:S(2)}, u32[]{:S(2)}) %all-to-all-start) | async-done | bytes 131104 | tf_op jit(solution)/shard_map/all_to_all | solution.py:207
  25.2 0.0 copy-done
  25.2 0.0 copy-done.1
  25.2 0.0 copy-done.2
  25.2 5.6 %products.3 = (f32[4,32,1024]{2,1,0:T(8,128)S(1)}, f32[4,32,1024]{2,1,0:T(8,128)S(1)}, f32[1,1024]{1,0:T(1,128)S(1)}, f32[128,128,128]{2,1,0:T(8,128)S(1)}) custom-call(s32[128]{0:T(128)S(1)} %bitcast.69, s32[128]{0:T(128)S(1)} %bitcast.72, s32[2]{0:T(128)S(1)} %pad_add_fusion.place, f32[32,1024]{1,0:T(8,128)S(1)} %copy-done, ...), custom_call_target="tpu_custom_call" | custom-call | flops 536870912 | bytes 8388608 | tf_op jit(solution)/shard_map/products/pallas_call | solution.py:141
  30.9 0.4 collective-permute-start.3
  31.2 1.6 %collective-permute-done.3 = f32[4,32,1024]{2,1,0:T(8,128)S(1)} collective-permute-done((f32[4,32,1024]{2,1,0:T(8,128)S(1)}, f32[4,32,1024]{2,1,0:T(8,128)S(1)}, u32[]{:S(2)}, u32[]{:S(2)}) %collective-permute-start.3) | collective-permute-done | bytes 524320 | tf_op jit(solution)/shard_map/ppermute | solution.py:189
  32.8 0.1 add.36
  32.9 1.0 collective-permute-start.4
  34.0 0.0 collective-permute-start.6
  34.0 3.4 %collective-permute-start.5 = (f32[32,1024]{1,0:T(8,128)S(1)}, f32[32,1024]{1,0:T(8,128)S(1)}, u32[]{:S(2)}, u32[]{:S(2)}) collective-permute-start(f32[32,1024]{1,0:T(8,128)S(1)} %get-tuple-element.44), channel_id=1, source_target_pairs={{0,4},{1,5},{2,6},{3,7},{4,0},{5,1},{6,2},{7,3},{8,12},{9,13},{10,... | collective-permute-start | bytes 393224 | tf_op jit(solution)/shard_map/ppermute | solution.py:189
  37.4 3.8 %collective-permute-done.4 = f32[32,1024]{1,0:T(8,128)S(1)} collective-permute-done((f32[32,1024]{1,0:T(8,128)S(1)}, f32[32,1024]{1,0:T(8,128)S(1)}, u32[]{:S(2)}, u32[]{:S(2)}) %collective-permute-start.4) | collective-permute-done | bytes 131104 | tf_op jit(solution)/shard_map/ppermute | solution.py:189
  41.2 3.2 %collective-permute-done.6 = f32[32,1024]{1,0:T(8,128)S(1)} collective-permute-done((f32[32,1024]{1,0:T(8,128)S(1)}, f32[32,1024]{1,0:T(8,128)S(1)}, u32[]{:S(2)}, u32[]{:S(2)}) %collective-permute-start.6) | collective-permute-done | bytes 131104 | tf_op jit(solution)/shard_map/ppermute | solution.py:189
  44.4 2.6 %collective-permute-done.5 = f32[32,1024]{1,0:T(8,128)S(1)} collective-permute-done((f32[32,1024]{1,0:T(8,128)S(1)}, f32[32,1024]{1,0:T(8,128)S(1)}, u32[]{:S(2)}, u32[]{:S(2)}) %collective-permute-start.5) | collective-permute-done | bytes 131104 | tf_op jit(solution)/shard_map/ppermute | solution.py:189
  47.0 0.7 collective-permute-start.9
  47.7 1.5 %collective-permute-start.8 = (f32[32,1024]{1,0:T(8,128)S(1)}, f32[32,1024]{1,0:T(8,128)S(1)}, u32[]{:S(2)}, u32[]{:S(2)}) collective-permute-start(f32[32,1024]{1,0:T(8,128)S(1)} %fusion.15.refs_0_), channel_id=1, source_target_pairs={{0,16},{8,24},{16,0},{24,8},{1,17},{9,25},{17,1},{25,9},{2,18},{10... | collective-permute-start | bytes 393224 | tf_op jit(solution)/shard_map/ppermute | solution.py:189
  49.2 1.4 %collective-permute-start.7 = (f32[32,1024]{1,0:T(8,128)S(1)}, f32[32,1024]{1,0:T(8,128)S(1)}, u32[]{:S(2)}, u32[]{:S(2)}) collective-permute-start(f32[32,1024]{1,0:T(8,128)S(1)} %fusion.15.refs_0_), channel_id=1, source_target_pairs={{0,8},{8,0},{16,24},{24,16},{1,9},{9,1},{17,25},{25,17},{2,10},{10... | collective-permute-start | bytes 393224 | tf_op jit(solution)/shard_map/ppermute | solution.py:189
  50.6 3.7 %collective-permute-done.9.refs_3_ = f32[32,1024]{1,0:T(8,128)S(1)} collective-permute-done((f32[32,1024]{1,0:T(8,128)S(1)}, f32[32,1024]{1,0:T(8,128)S(1)}, u32[]{:S(2)}, u32[]{:S(2)}) %collective-permute-start.9) | collective-permute-done | bytes 131104 | tf_op jit(solution)/shard_map/ppermute | solution.py:189
  54.3 1.0 collective-permute-done.8.refs_2_
  55.2 0.0 collective-permute-done.7.refs_1_
  55.2 4.1 %products.4 = (f32[4,32,1024]{2,1,0:T(8,128)S(1)}, f32[4,32,1024]{2,1,0:T(8,128)S(1)}, f32[1,1024]{1,0:T(1,128)S(1)}) custom-call(s32[128]{0:T(128)S(1)} %bitcast.70, s32[128]{0:T(128)S(1)} %bitcast.73, s32[2]{0:T(128)S(1)} %pad_add_fusion.place, f32[32,1024]{1,0:T(8,128)S(1)} %fusion.15.refs_0_, f32[32,1024]{1,0:T(8,128)S(1)} %collective-permute-done.7.refs_1_, ...), custom_call_target="tpu_custom_call" | custom-call | flops 536870912 | bytes 8388608 | tf_op jit(solution)/shard_map/products/pallas_call | solution.py:141
  59.4 0.1 collective-permute-start.10
  59.5 1.9 %collective-permute-done.10 = f32[4,32,1024]{2,1,0:T(8,128)S(1)} collective-permute-done((f32[4,32,1024]{2,1,0:T(8,128)S(1)}, f32[4,32,1024]{2,1,0:T(8,128)S(1)}, u32[]{:S(2)}, u32[]{:S(2)}) %collective-permute-start.10) | collective-permute-done | bytes 524320 | tf_op jit(solution)/shard_map/ppermute | solution.py:189
  61.4 0.1 add.40
  61.5 1.2 %collective-permute-start.11 = (f32[32,1024]{1,0:T(8,128)S(1)}, f32[32,1024]{1,0:T(8,128)S(1)}, u32[]{:S(2)}, u32[]{:S(2)}) collective-permute-start(f32[32,1024]{1,0:T(8,128)S(1)} %get-tuple-element.39), channel_id=1, source_target_pairs={{0,6},{1,7},{2,4},{3,5},{4,2},{5,3},{6,0},{7,1},{8,14},{9,15},{10,... | collective-permute-start | bytes 393224 | tf_op jit(solution)/shard_map/ppermute | solution.py:189
  62.7 0.0 collective-permute-start.13
  62.7 3.3 %collective-permute-start.12 = (f32[32,1024]{1,0:T(8,128)S(1)}, f32[32,1024]{1,0:T(8,128)S(1)}, u32[]{:S(2)}, u32[]{:S(2)}) collective-permute-start(f32[32,1024]{1,0:T(8,128)S(1)} %get-tuple-element.41), channel_id=1, source_target_pairs={{0,4},{1,5},{2,6},{3,7},{4,0},{5,1},{6,2},{7,3},{8,12},{9,13},{10,... | collective-permute-start | bytes 393224 | tf_op jit(solution)/shard_map/ppermute | solution.py:189
  65.9 3.8 %collective-permute-done.11 = f32[32,1024]{1,0:T(8,128)S(1)} collective-permute-done((f32[32,1024]{1,0:T(8,128)S(1)}, f32[32,1024]{1,0:T(8,128)S(1)}, u32[]{:S(2)}, u32[]{:S(2)}) %collective-permute-start.11) | collective-permute-done | bytes 131104 | tf_op jit(solution)/shard_map/ppermute | solution.py:189
  69.8 3.8 %collective-permute-done.13 = f32[32,1024]{1,0:T(8,128)S(1)} collective-permute-done((f32[32,1024]{1,0:T(8,128)S(1)}, f32[32,1024]{1,0:T(8,128)S(1)}, u32[]{:S(2)}, u32[]{:S(2)}) %collective-permute-start.13) | collective-permute-done | bytes 131104 | tf_op jit(solution)/shard_map/ppermute | solution.py:189
  73.5 0.0 collective-permute-done.12
  73.5 0.1 fusion.11.refs_0_
  73.6 1.4 %collective-permute-start.16 = (f32[32,1024]{1,0:T(8,128)S(1)}, f32[32,1024]{1,0:T(8,128)S(1)}, u32[]{:S(2)}, u32[]{:S(2)}) collective-permute-start(f32[32,1024]{1,0:T(8,128)S(1)} %fusion.11.refs_0_), channel_id=1, source_target_pairs={{0,24},{8,16},{16,8},{24,0},{1,25},{9,17},{17,9},{25,1},{2,26},{10... | collective-permute-start | bytes 393224 | tf_op jit(solution)/shard_map/ppermute | solution.py:189
  75.0 1.4 %collective-permute-start.15 = (f32[32,1024]{1,0:T(8,128)S(1)}, f32[32,1024]{1,0:T(8,128)S(1)}, u32[]{:S(2)}, u32[]{:S(2)}) collective-permute-start(f32[32,1024]{1,0:T(8,128)S(1)} %fusion.11.refs_0_), channel_id=1, source_target_pairs={{0,16},{8,24},{16,0},{24,8},{1,17},{9,25},{17,1},{25,9},{2,18},{10... | collective-permute-start | bytes 393224 | tf_op jit(solution)/shard_map/ppermute | solution.py:189
  76.4 1.0 collective-permute-start.14
  77.4 2.4 %collective-permute-done.16.refs_3_ = f32[32,1024]{1,0:T(8,128)S(1)} collective-permute-done((f32[32,1024]{1,0:T(8,128)S(1)}, f32[32,1024]{1,0:T(8,128)S(1)}, u32[]{:S(2)}, u32[]{:S(2)}) %collective-permute-start.16) | collective-permute-done | bytes 131104 | tf_op jit(solution)/shard_map/ppermute | solution.py:189
  79.8 2.1 %collective-permute-done.15.refs_2_ = f32[32,1024]{1,0:T(8,128)S(1)} collective-permute-done((f32[32,1024]{1,0:T(8,128)S(1)}, f32[32,1024]{1,0:T(8,128)S(1)}, u32[]{:S(2)}, u32[]{:S(2)}) %collective-permute-start.15) | collective-permute-done | bytes 131104 | tf_op jit(solution)/shard_map/ppermute | solution.py:189
  81.9 1.8 %collective-permute-done.14.refs_1_ = f32[32,1024]{1,0:T(8,128)S(1)} collective-permute-done((f32[32,1024]{1,0:T(8,128)S(1)}, f32[32,1024]{1,0:T(8,128)S(1)}, u32[]{:S(2)}, u32[]{:S(2)}) %collective-permute-start.14) | collective-permute-done | bytes 131104 | tf_op jit(solution)/shard_map/ppermute | solution.py:189
  83.7 4.1 %products.5 = (f32[4,32,1024]{2,1,0:T(8,128)S(1)}, f32[4,32,1024]{2,1,0:T(8,128)S(1)}, f32[1,1024]{1,0:T(1,128)S(1)}) custom-call(s32[128]{0:T(128)S(1)} %bitcast.71, s32[128]{0:T(128)S(1)} %bitcast.74, s32[2]{0:T(128)S(1)} %pad_add_fusion.place, f32[32,1024]{1,0:T(8,128)S(1)} %fusion.11.refs_0_, f32[32,1024]{1,0:T(8,128)S(1)} %collective-permute-done.14.refs_1_, ...), custom_call_target="tpu_custom_call" | custom-call | flops 536870912 | bytes 8388608 | tf_op jit(solution)/shard_map/products/pallas_call | solution.py:141
  87.8 0.1 collective-permute-start.17
  87.9 1.9 %collective-permute-done.17 = f32[4,32,1024]{2,1,0:T(8,128)S(1)} collective-permute-done((f32[4,32,1024]{2,1,0:T(8,128)S(1)}, f32[4,32,1024]{2,1,0:T(8,128)S(1)}, u32[]{:S(2)}, u32[]{:S(2)}) %collective-permute-start.17) | collective-permute-done | bytes 524320 | tf_op jit(solution)/shard_map/ppermute | solution.py:189
  89.8 0.1 add.44
  89.9 1.3 %collective-permute-start.18 = (f32[32,1024]{1,0:T(8,128)S(1)}, f32[32,1024]{1,0:T(8,128)S(1)}, u32[]{:S(2)}, u32[]{:S(2)}) collective-permute-start(f32[32,1024]{1,0:T(8,128)S(1)} %get-tuple-element.36), channel_id=1, source_target_pairs={{0,6},{1,7},{2,4},{3,5},{4,2},{5,3},{6,0},{7,1},{8,14},{9,15},{10,... | collective-permute-start | bytes 393224 | tf_op jit(solution)/shard_map/ppermute | solution.py:189
  91.2 0.0 collective-permute-start.20
  91.2 3.1 %collective-permute-start.19 = (f32[32,1024]{1,0:T(8,128)S(1)}, f32[32,1024]{1,0:T(8,128)S(1)}, u32[]{:S(2)}, u32[]{:S(2)}) collective-permute-start(f32[32,1024]{1,0:T(8,128)S(1)} %get-tuple-element.38), channel_id=1, source_target_pairs={{0,4},{1,5},{2,6},{3,7},{4,0},{5,1},{6,2},{7,3},{8,12},{9,13},{10,... | collective-permute-start | bytes 393224 | tf_op jit(solution)/shard_map/ppermute | solution.py:189
  94.4 3.8 %collective-permute-done.18 = f32[32,1024]{1,0:T(8,128)S(1)} collective-permute-done((f32[32,1024]{1,0:T(8,128)S(1)}, f32[32,1024]{1,0:T(8,128)S(1)}, u32[]{:S(2)}, u32[]{:S(2)}) %collective-permute-start.18) | collective-permute-done | bytes 131104 | tf_op jit(solution)/shard_map/ppermute | solution.py:189
  98.2 3.6 %collective-permute-done.20 = f32[32,1024]{1,0:T(8,128)S(1)} collective-permute-done((f32[32,1024]{1,0:T(8,128)S(1)}, f32[32,1024]{1,0:T(8,128)S(1)}, u32[]{:S(2)}, u32[]{:S(2)}) %collective-permute-start.20) | collective-permute-done | bytes 131104 | tf_op jit(solution)/shard_map/ppermute | solution.py:189
  101.8 1.5 %collective-permute-done.19 = f32[32,1024]{1,0:T(8,128)S(1)} collective-permute-done((f32[32,1024]{1,0:T(8,128)S(1)}, f32[32,1024]{1,0:T(8,128)S(1)}, u32[]{:S(2)}, u32[]{:S(2)}) %collective-permute-start.19) | collective-permute-done | bytes 131104 | tf_op jit(solution)/shard_map/ppermute | solution.py:189
  103.4 0.7 finish.1
  104.1 10.2 %all_to_all.10.parts_ref = f32[32,8,128]{2,1,0:T(8,128)S(1)} all-to-all(f32[32,8,128]{2,1,0:T(8,128)S(1)} %get-tuple-element.35), channel_id=1, replica_groups=mesh['row'=4,'col'=8] {'row','col'}, dimensions={0} | all-to-all | bytes 262144 | tf_op jit(solution)/shard_map/all_to_all | solution.py:240
  114.3 0.7 gram_sum.1
  (5 shorter events, 0.2 us)
Async XLA Ops:
  0.6 24.6 %copy-start = (f32[32,1024]{1,0:T(8,128)S(1)}, f32[32,1024]{1,0:T(8,128)}, u32[]{:S(2)}) copy-start(f32[32,1024]{1,0:T(8,128)} %refs_0_) | copy-start | bytes 393220
  0.6 24.6 %copy-start.1 = (s32[1,128]{1,0:T(1,128)S(1)}, s32[1,128]{1,0:T(1,128)}, u32[]{:S(2)}) copy-start(s32[1,128]{1,0:T(1,128)} %param.6) | copy-start | bytes 1540
  0.6 24.6 %copy-start.2 = (s32[1,128]{1,0:T(1,128)S(1)}, s32[1,128]{1,0:T(1,128)}, u32[]{:S(2)}) copy-start(s32[1,128]{1,0:T(1,128)} %param.7) | copy-start | bytes 1540
  0.7 10.1 %collective-permute-start.2 = (f32[32,1024]{1,0:T(8,128)}, f32[32,1024]{1,0:T(8,128)S(1)}, u32[]{:S(2)}, u32[]{:S(2)}) collective-permute-start(f32[32,1024]{1,0:T(8,128)} %refs_0_), channel_id=1, source_target_pairs={{0,24},{8,16},{16,8},{24,0},{1,25},{9,17},{17,9},{25,1},{2,26},{10... | collective-permute-start | bytes 393224 | tf_op jit(solution)/shard_map/ppermute | solution.py:189
  4.6 6.5 %collective-permute-start.1 = (f32[32,1024]{1,0:T(8,128)}, f32[32,1024]{1,0:T(8,128)S(1)}, u32[]{:S(2)}, u32[]{:S(2)}) collective-permute-start(f32[32,1024]{1,0:T(8,128)} %refs_0_), channel_id=1, source_target_pairs={{0,16},{8,24},{16,0},{24,8},{1,17},{9,25},{17,1},{25,9},{2,18},{10... | collective-permute-start | bytes 393224 | tf_op jit(solution)/shard_map/ppermute | solution.py:189
  5.1 6.3 %collective-permute-start = (f32[32,1024]{1,0:T(8,128)}, f32[32,1024]{1,0:T(8,128)S(1)}, u32[]{:S(2)}, u32[]{:S(2)}) collective-permute-start(f32[32,1024]{1,0:T(8,128)} %refs_0_), channel_id=1, source_target_pairs={{0,8},{8,0},{16,24},{24,16},{1,9},{9,1},{17,25},{25,17},{2,10},{10... | collective-permute-start | bytes 393224 | tf_op jit(solution)/shard_map/ppermute | solution.py:189
  11.4 13.8 %all-to-all-start = ((f32[32,8,128]{2,1,0:T(8,128)}), f32[32,8,128]{2,1,0:T(8,128)S(1)}, u32[]{:S(2)}, u32[]{:S(2)}) async-start(f32[32,8,128]{2,1,0:T(8,128)} %bitcast.4), calls=%async_computation | async-start | bytes 262144 | tf_op jit(solution)/shard_map/all_to_all | solution.py:207
  30.9 2.0 %collective-permute-start.3 = (f32[4,32,1024]{2,1,0:T(8,128)S(1)}, f32[4,32,1024]{2,1,0:T(8,128)S(1)}, u32[]{:S(2)}, u32[]{:S(2)}) collective-permute-start(f32[4,32,1024]{2,1,0:T(8,128)S(1)} %get-tuple-element.25), channel_id=1, source_target_pairs={{0,1},{1,0},{2,3},{3,2},{4,5},{5,4},{6,7},{7,6},{8,9},{9,8},{10,11... | collective-permute-start | bytes 1572872 | tf_op jit(solution)/shard_map/ppermute | solution.py:189
  32.9 8.2 %collective-permute-start.4 = (f32[32,1024]{1,0:T(8,128)S(1)}, f32[32,1024]{1,0:T(8,128)S(1)}, u32[]{:S(2)}, u32[]{:S(2)}) collective-permute-start(f32[32,1024]{1,0:T(8,128)S(1)} %get-tuple-element.42), channel_id=1, source_target_pairs={{0,6},{1,7},{2,4},{3,5},{4,2},{5,3},{6,0},{7,1},{8,14},{9,15},{10,... | collective-permute-start | bytes 393224 | tf_op jit(solution)/shard_map/ppermute | solution.py:189
  34.0 10.4 %collective-permute-start.6 = (f32[32,1024]{1,0:T(8,128)S(1)}, f32[32,1024]{1,0:T(8,128)S(1)}, u32[]{:S(2)}, u32[]{:S(2)}) collective-permute-start(f32[32,1024]{1,0:T(8,128)S(1)} %get-tuple-element.43), channel_id=1, source_target_pairs={{0,2},{1,3},{2,0},{3,1},{4,6},{5,7},{6,4},{7,5},{8,10},{9,11},{10,... | collective-permute-start | bytes 393224 | tf_op jit(solution)/shard_map/ppermute | solution.py:189
  34.0 13.0 %collective-permute-start.5 = (f32[32,1024]{1,0:T(8,128)S(1)}, f32[32,1024]{1,0:T(8,128)S(1)}, u32[]{:S(2)}, u32[]{:S(2)}) collective-permute-start(f32[32,1024]{1,0:T(8,128)S(1)} %get-tuple-element.44), channel_id=1, source_target_pairs={{0,4},{1,5},{2,6},{3,7},{4,0},{5,1},{6,2},{7,3},{8,12},{9,13},{10,... | collective-permute-start | bytes 393224 | tf_op jit(solution)/shard_map/ppermute | solution.py:189
  47.0 7.2 %collective-permute-start.9 = (f32[32,1024]{1,0:T(8,128)S(1)}, f32[32,1024]{1,0:T(8,128)S(1)}, u32[]{:S(2)}, u32[]{:S(2)}) collective-permute-start(f32[32,1024]{1,0:T(8,128)S(1)} %fusion.15.refs_0_), channel_id=1, source_target_pairs={{0,24},{8,16},{16,8},{24,0},{1,25},{9,17},{17,9},{25,1},{2,26},{10... | collective-permute-start | bytes 393224 | tf_op jit(solution)/shard_map/ppermute | solution.py:189
  47.7 7.5 %collective-permute-start.8 = (f32[32,1024]{1,0:T(8,128)S(1)}, f32[32,1024]{1,0:T(8,128)S(1)}, u32[]{:S(2)}, u32[]{:S(2)}) collective-permute-start(f32[32,1024]{1,0:T(8,128)S(1)} %fusion.15.refs_0_), channel_id=1, source_target_pairs={{0,16},{8,24},{16,0},{24,8},{1,17},{9,25},{17,1},{25,9},{2,18},{10... | collective-permute-start | bytes 393224 | tf_op jit(solution)/shard_map/ppermute | solution.py:189
  49.2 6.0 %collective-permute-start.7 = (f32[32,1024]{1,0:T(8,128)S(1)}, f32[32,1024]{1,0:T(8,128)S(1)}, u32[]{:S(2)}, u32[]{:S(2)}) collective-permute-start(f32[32,1024]{1,0:T(8,128)S(1)} %fusion.15.refs_0_), channel_id=1, source_target_pairs={{0,8},{8,0},{16,24},{24,16},{1,9},{9,1},{17,25},{25,17},{2,10},{10... | collective-permute-start | bytes 393224 | tf_op jit(solution)/shard_map/ppermute | solution.py:189
  59.4 2.0 %collective-permute-start.10 = (f32[4,32,1024]{2,1,0:T(8,128)S(1)}, f32[4,32,1024]{2,1,0:T(8,128)S(1)}, u32[]{:S(2)}, u32[]{:S(2)}) collective-permute-start(f32[4,32,1024]{2,1,0:T(8,128)S(1)} %get-tuple-element.29), channel_id=1, source_target_pairs={{0,1},{1,0},{2,3},{3,2},{4,5},{5,4},{6,7},{7,6},{8,9},{9,8},{10,11... | collective-permute-start | bytes 1572872 | tf_op jit(solution)/shard_map/ppermute | solution.py:189
  61.5 8.3 %collective-permute-start.11 = (f32[32,1024]{1,0:T(8,128)S(1)}, f32[32,1024]{1,0:T(8,128)S(1)}, u32[]{:S(2)}, u32[]{:S(2)}) collective-permute-start(f32[32,1024]{1,0:T(8,128)S(1)} %get-tuple-element.39), channel_id=1, source_target_pairs={{0,6},{1,7},{2,4},{3,5},{4,2},{5,3},{6,0},{7,1},{8,14},{9,15},{10,... | collective-permute-start | bytes 393224 | tf_op jit(solution)/shard_map/ppermute | solution.py:189
  62.7 10.9 %collective-permute-start.13 = (f32[32,1024]{1,0:T(8,128)S(1)}, f32[32,1024]{1,0:T(8,128)S(1)}, u32[]{:S(2)}, u32[]{:S(2)}) collective-permute-start(f32[32,1024]{1,0:T(8,128)S(1)} %get-tuple-element.40), channel_id=1, source_target_pairs={{0,2},{1,3},{2,0},{3,1},{4,6},{5,7},{6,4},{7,5},{8,10},{9,11},{10,... | collective-permute-start | bytes 393224 | tf_op jit(solution)/shard_map/ppermute | solution.py:189
  62.7 10.9 %collective-permute-start.12 = (f32[32,1024]{1,0:T(8,128)S(1)}, f32[32,1024]{1,0:T(8,128)S(1)}, u32[]{:S(2)}, u32[]{:S(2)}) collective-permute-start(f32[32,1024]{1,0:T(8,128)S(1)} %get-tuple-element.41), channel_id=1, source_target_pairs={{0,4},{1,5},{2,6},{3,7},{4,0},{5,1},{6,2},{7,3},{8,12},{9,13},{10,... | collective-permute-start | bytes 393224 | tf_op jit(solution)/shard_map/ppermute | solution.py:189
  73.6 6.2 %collective-permute-start.16 = (f32[32,1024]{1,0:T(8,128)S(1)}, f32[32,1024]{1,0:T(8,128)S(1)}, u32[]{:S(2)}, u32[]{:S(2)}) collective-permute-start(f32[32,1024]{1,0:T(8,128)S(1)} %fusion.11.refs_0_), channel_id=1, source_target_pairs={{0,24},{8,16},{16,8},{24,0},{1,25},{9,17},{17,9},{25,1},{2,26},{10... | collective-permute-start | bytes 393224 | tf_op jit(solution)/shard_map/ppermute | solution.py:189
  75.0 6.9 %collective-permute-start.15 = (f32[32,1024]{1,0:T(8,128)S(1)}, f32[32,1024]{1,0:T(8,128)S(1)}, u32[]{:S(2)}, u32[]{:S(2)}) collective-permute-start(f32[32,1024]{1,0:T(8,128)S(1)} %fusion.11.refs_0_), channel_id=1, source_target_pairs={{0,16},{8,24},{16,0},{24,8},{1,17},{9,25},{17,1},{25,9},{2,18},{10... | collective-permute-start | bytes 393224 | tf_op jit(solution)/shard_map/ppermute | solution.py:189
  76.4 7.3 %collective-permute-start.14 = (f32[32,1024]{1,0:T(8,128)S(1)}, f32[32,1024]{1,0:T(8,128)S(1)}, u32[]{:S(2)}, u32[]{:S(2)}) collective-permute-start(f32[32,1024]{1,0:T(8,128)S(1)} %fusion.11.refs_0_), channel_id=1, source_target_pairs={{0,8},{8,0},{16,24},{24,16},{1,9},{9,1},{17,25},{25,17},{2,10},{10... | collective-permute-start | bytes 393224 | tf_op jit(solution)/shard_map/ppermute | solution.py:189
  87.8 2.0 %collective-permute-start.17 = (f32[4,32,1024]{2,1,0:T(8,128)S(1)}, f32[4,32,1024]{2,1,0:T(8,128)S(1)}, u32[]{:S(2)}, u32[]{:S(2)}) collective-permute-start(f32[4,32,1024]{2,1,0:T(8,128)S(1)} %get-tuple-element.32), channel_id=1, source_target_pairs={{0,1},{1,0},{2,3},{3,2},{4,5},{5,4},{6,7},{7,6},{8,9},{9,8},{10,11... | collective-permute-start | bytes 1572872 | tf_op jit(solution)/shard_map/ppermute | solution.py:189
  89.9 8.3 %collective-permute-start.18 = (f32[32,1024]{1,0:T(8,128)S(1)}, f32[32,1024]{1,0:T(8,128)S(1)}, u32[]{:S(2)}, u32[]{:S(2)}) collective-permute-start(f32[32,1024]{1,0:T(8,128)S(1)} %get-tuple-element.36), channel_id=1, source_target_pairs={{0,6},{1,7},{2,4},{3,5},{4,2},{5,3},{6,0},{7,1},{8,14},{9,15},{10,... | collective-permute-start | bytes 393224 | tf_op jit(solution)/shard_map/ppermute | solution.py:189
  91.2 10.6 %collective-permute-start.20 = (f32[32,1024]{1,0:T(8,128)S(1)}, f32[32,1024]{1,0:T(8,128)S(1)}, u32[]{:S(2)}, u32[]{:S(2)}) collective-permute-start(f32[32,1024]{1,0:T(8,128)S(1)} %get-tuple-element.37), channel_id=1, source_target_pairs={{0,2},{1,3},{2,0},{3,1},{4,6},{5,7},{6,4},{7,5},{8,10},{9,11},{10,... | collective-permute-start | bytes 393224 | tf_op jit(solution)/shard_map/ppermute | solution.py:189
  91.2 12.1 %collective-permute-start.19 = (f32[32,1024]{1,0:T(8,128)S(1)}, f32[32,1024]{1,0:T(8,128)S(1)}, u32[]{:S(2)}, u32[]{:S(2)}) collective-permute-start(f32[32,1024]{1,0:T(8,128)S(1)} %get-tuple-element.38), channel_id=1, source_target_pairs={{0,4},{1,5},{2,6},{3,7},{4,0},{5,1},{6,2},{7,3},{8,12},{9,13},{10,... | collective-permute-start | bytes 393224 | tf_op jit(solution)/shard_map/ppermute | solution.py:189

commit v4 on v3

--- a/solution.py
+++ b/solution.py
@@ -25,11 +25,13 @@
     return high, (value - high.astype(jnp.float32)).astype(jnp.bfloat16)
 
 
-def degree_kernel(rows, tiles_hbm, sent_ref, buffer, arrived):
+def degree_kernel(rows, tiles_hbm, sent_ref, buffer, terms, arrived):
     count = tiles_hbm.shape[0]
     groups = count // GROUP
     n_row, n_col, owned, _ = sent_ref.shape
     lane = lax.broadcasted_iota(jnp.int32, (TB, TB), 1)
+    ones = jnp.ones((16, 2 * TB), jnp.bfloat16)
+    terms[...] = jnp.zeros_like(terms)
 
     def fetch(group):
         at = pl.ds(group * GROUP, GROUP)
@@ -40,16 +42,25 @@
 
     def body(group, total):
         fetch(group).wait()
-        for t in range(GROUP):
+        for t in range(0, GROUP, 2):
             index = group * GROUP + t
             sums = jnp.sum(jnp.abs(buffer[index]), axis=1, keepdims=True)
             total = total + jnp.where(lane == rows[index], sums, 0.0)
+            sums = lax.dot_general(
+                ones,
+                jnp.concatenate(two_parts(jnp.abs(buffer[index + 1])), axis=1),
+                (((1,), (1,)), ((), ())),
+                preferred_element_type=jnp.float32,
+            )
+            at = pl.ds(rows[index + 1], 1)
+            terms[at, :] = terms[at, :] + sums[0:1]
         return total
 
     total = lax.fori_loop(0, groups, body, jnp.zeros((TB, TB), jnp.float32)).T
     for s in range(n_row):
         for d in range(n_col):
-            sent_ref[s, d] = total[d * owned : (d + 1) * owned]
+            at = slice(d * owned, (d + 1) * owned)
+            sent_ref[s, d] = total[at] + terms[at]
 
 
 def degree_terms(tiles, rows, n_row, n_col, owned):
@@ -62,6 +73,7 @@
         out_specs=VECTORS,
         scratch_shapes=[
             pltpu.VMEM(tiles.shape, jnp.float32),
+            pltpu.VMEM((n_col * owned, TB), jnp.float32),
             pltpu.SemaphoreType.DMA((count // GROUP,)),
         ],
         compiler_params=pltpu.CompilerParams(vmem_limit_bytes=24 << 20),
@@ -75,7 +87,7 @@
     )
 
 
-def product_kernel(n_row, n_col, owned, load, rows, cols, place, *refs):
+def product_kernel(n_row, n_col, owned, load, unroll, rows, cols, place, *refs):
     refs = list(refs)
     take = lambda n: [refs.pop(0) for _ in range(n)]
     sources = take(n_row)
@@ -87,11 +99,11 @@
     a, b = place[0], place[1]
 
     def fetch(group):
-        at = pl.ds(group * UNROLL, UNROLL)
+        at = pl.ds(group * unroll, unroll)
         return pltpu.make_async_copy(tiles_from.at[at], tiles_ref.at[at], refs[0].at[group])
 
     if load:
-        for group in range(count // UNROLL):
+        for group in range(count // unroll):
             fetch(group).start()
     for s in range(n_row):
         degree = 1.0 + jnp.sum(terms_ref[a ^ s], axis=0)
@@ -108,8 +120,8 @@
     def body(group, total):
         if load:
             fetch(group).wait()
-        for t in range(UNROLL):
-            index = group * UNROLL + t
+        for t in range(unroll):
+            index = group * unroll + t
             row, col = rows[index], cols[index]
             where_from = (lax.div(col, owned) ^ a) * owned + lax.rem(col, owned)
             where_to = (lax.div(row, owned) ^ b) * owned + lax.rem(row, owned)
@@ -123,7 +135,7 @@
             sums[where_to] = total
         return total
 
-    lax.fori_loop(0, count // UNROLL, body, jnp.zeros((k, TB), jnp.float32))
+    lax.fori_loop(0, count // unroll, body, jnp.zeros((k, TB), jnp.float32))
     for d in range(n_col):
         out = give_ref if d % 2 else keep_ref
         for o in range(owned):
@@ -135,11 +147,12 @@
     owned = width // TB
     count = tiles.shape[0]
     half = jax.ShapeDtypeStruct((n_col // 2, k, width), jnp.float32)
+    unroll = UNROLL if load else min(count, 4 * UNROLL)
     loaded = [jax.ShapeDtypeStruct(tiles.shape, tiles.dtype)] * load
     if load:
         tiles = pltpu.with_memory_space_constraint(tiles, pltpu.HBM)
     return pl.pallas_call(
-        functools.partial(product_kernel, n_row, n_col, owned, load),
+        functools.partial(product_kernel, n_row, n_col, owned, load, unroll),
         out_shape=[half, half, jax.ShapeDtypeStruct((1, width), jnp.float32)] + loaded,
         in_specs=[SCALARS] * 3
         + [VECTORS] * (n_row + 1)
@@ -149,7 +162,7 @@
             pltpu.VMEM((n_row * owned, 2 * k, 2 * TB), jnp.bfloat16),
             pltpu.VMEM((n_col * owned, k, TB), jnp.float32),
         ]
-        + [pltpu.SemaphoreType.DMA((count // UNROLL,))] * load,
+        + [pltpu.SemaphoreType.DMA((count // unroll,))] * load,
         compiler_params=pltpu.CompilerParams(vmem_limit_bytes=24 << 20),
         cost_estimate=pl.CostEstimate(
             flops=count * TB * TB * 2 * k * 4,

time: 115 us -> 114 us (level)
  transfers between devices with their start and end apart: 22 -> 22, of which waited for: 19 -> 19; matrix products, arithmetic and copies ran while one was open for 0% -> 0% of each run, Pallas kernels for 5% -> 4%
where the time goes in v4:
time: 114 us
  waiting for transfers between devices  51.7 us (45%)
  starting transfers between devices  31.1 us (27%)
  Pallas kernels  19.6 us (17%)
  blocking collectives  10.2 us (9%)
    ppermute x21, waiting for transfers between devices, swap(): return lax.ppermute(value, axis, [(i, i ^ by) for i in range(size)])  43.6 us
    ppermute x21, starting transfers between devices, swap(): return lax.ppermute(value, axis, [(i, i ^ by) for i in range(size)])  25.8 us
    pallas_call x3, Pallas kernels, products(): pl.pallas_call(functools.partial(product_kernel, n_row, n_col, owned, loa...  13.1 us
    all_to_all x1, blocking collectives, on_device(): grams = lax.all_to_all(grams, ('row', 'col'), 0, 0, tiled=True)  10.2 us
    all_to_all x1, waiting for transfers between devices, on_device(): lax.all_to_all(sent.reshape(devices, owned, TB), ('row', 'col'), 0, 0, ti...  8.09 us
    all_to_all x1, starting transfers between devices, on_device(): lax.all_to_all(sent.reshape(devices, owned, TB), ('row', 'col'), 0, 0, ti...  5.25 us
    pallas_call x1, Pallas kernels, degree_terms(): pl.pallas_call(degree_kernel, out_shape=pltpu.VMEM((n_row, n_col, owned,...  5.08 us
  transfers between devices with their start and end apart: 22, of which 19 were waited for; matrix products, arithmetic and copies ran while one was open for 0% of the time, Pallas kernels for 4%

profile of v4, /device:TPU:0, one launch (start us, length us, event | category | flops | bytes accessed | tf_op | source)
XLA Modules:
  0.0 113.9 jit_solution(3483308923463284815)
XLA Ops:
  0.6 0.0 copy-start
  0.6 0.0 copy-start.1
  0.6 0.0 copy-start.2
  0.7 4.0 %collective-permute-start.2 = (f32[32,1024]{1,0:T(8,128)}, f32[32,1024]{1,0:T(8,128)S(1)}, u32[]{:S(2)}, u32[]{:S(2)}) collective-permute-start(f32[32,1024]{1,0:T(8,128)} %refs_0_), channel_id=1, source_target_pairs={{0,24},{8,16},{16,8},{24,0},{1,25},{9,17},{17,9},{25,1},{2,26},{10... | collective-permute-start | bytes 393224 | tf_op jit(solution)/shard_map/ppermute | solution.py:202
  4.6 0.5 collective-permute-start.1
  5.1 0.1 collective-permute-start
  5.3 5.1 %degree_terms.1 = f32[4,8,8,128]{3,2,1,0:T(8,128)} custom-call(s32[128]{0:T(128)} %bitcast.68, f32[128,128,128]{2,1,0:T(8,128)} %refs_5_.1), custom_call_target="tpu_custom_call" | custom-call | flops 4194304 | bytes 8388608 | tf_op jit(solution)/shard_map/degree_terms/pallas_call | solution.py:69
  10.3 0.0 collective-permute-done.2.refs_3_
  10.4 0.8 collective-permute-done.1.refs_2_
  11.1 0.2 collective-permute-done.refs_1_
  11.4 5.2 %all-to-all-start = ((f32[32,8,128]{2,1,0:T(8,128)}), f32[32,8,128]{2,1,0:T(8,128)S(1)}, u32[]{:S(2)}, u32[]{:S(2)}) async-start(f32[32,8,128]{2,1,0:T(8,128)} %bitcast.4), calls=%async_computation | async-start | bytes 262144 | tf_op jit(solution)/shard_map/all_to_all | solution.py:220
  16.6 0.1 pad_add_fusion.place
  16.7 8.1 %all-to-all-done = f32[32,8,128]{2,1,0:T(8,128)S(1)} async-done(((f32[32,8,128]{2,1,0:T(8,128)}), f32[32,8,128]{2,1,0:T(8,128)S(1)}, u32[]{:S(2)}, u32[]{:S(2)}) %all-to-all-start) | async-done | bytes 131104 | tf_op jit(solution)/shard_map/all_to_all | solution.py:220
  24.8 0.0 copy-done
  24.8 0.0 copy-done.1
  24.8 0.0 copy-done.2
  24.8 5.6 %products.3 = (f32[4,32,1024]{2,1,0:T(8,128)S(1)}, f32[4,32,1024]{2,1,0:T(8,128)S(1)}, f32[1,1024]{1,0:T(1,128)S(1)}, f32[128,128,128]{2,1,0:T(8,128)S(1)}) custom-call(s32[128]{0:T(128)S(1)} %bitcast.69, s32[128]{0:T(128)S(1)} %bitcast.72, s32[2]{0:T(128)S(1)} %pad_add_fusion.place, f32[32,1024]{1,0:T(8,128)S(1)} %copy-done, ...), custom_call_target="tpu_custom_call" | custom-call | flops 536870912 | bytes 8388608 | tf_op jit(solution)/shard_map/products/pallas_call | solution.py:154
  30.5 0.4 collective-permute-start.3
  30.9 1.6 %collective-permute-done.3 = f32[4,32,1024]{2,1,0:T(8,128)S(1)} collective-permute-done((f32[4,32,1024]{2,1,0:T(8,128)S(1)}, f32[4,32,1024]{2,1,0:T(8,128)S(1)}, u32[]{:S(2)}, u32[]{:S(2)}) %collective-permute-start.3) | collective-permute-done | bytes 524320 | tf_op jit(solution)/shard_map/ppermute | solution.py:202
  32.4 0.1 add.36
  32.5 1.0 collective-permute-start.4
  33.6 0.0 collective-permute-start.6
  33.6 3.4 %collective-permute-start.5 = (f32[32,1024]{1,0:T(8,128)S(1)}, f32[32,1024]{1,0:T(8,128)S(1)}, u32[]{:S(2)}, u32[]{:S(2)}) collective-permute-start(f32[32,1024]{1,0:T(8,128)S(1)} %get-tuple-element.44), channel_id=1, source_target_pairs={{0,4},{1,5},{2,6},{3,7},{4,0},{5,1},{6,2},{7,3},{8,12},{9,13},{10,... | collective-permute-start | bytes 393224 | tf_op jit(solution)/shard_map/ppermute | solution.py:202
  37.0 3.8 %collective-permute-done.4 = f32[32,1024]{1,0:T(8,128)S(1)} collective-permute-done((f32[32,1024]{1,0:T(8,128)S(1)}, f32[32,1024]{1,0:T(8,128)S(1)}, u32[]{:S(2)}, u32[]{:S(2)}) %collective-permute-start.4) | collective-permute-done | bytes 131104 | tf_op jit(solution)/shard_map/ppermute | solution.py:202
  40.8 3.2 %collective-permute-done.6 = f32[32,1024]{1,0:T(8,128)S(1)} collective-permute-done((f32[32,1024]{1,0:T(8,128)S(1)}, f32[32,1024]{1,0:T(8,128)S(1)}, u32[]{:S(2)}, u32[]{:S(2)}) %collective-permute-start.6) | collective-permute-done | bytes 131104 | tf_op jit(solution)/shard_map/ppermute | solution.py:202
  44.0 2.6 %collective-permute-done.5 = f32[32,1024]{1,0:T(8,128)S(1)} collective-permute-done((f32[32,1024]{1,0:T(8,128)S(1)}, f32[32,1024]{1,0:T(8,128)S(1)}, u32[]{:S(2)}, u32[]{:S(2)}) %collective-permute-start.5) | collective-permute-done | bytes 131104 | tf_op jit(solution)/shard_map/ppermute | solution.py:202
  46.6 0.7 collective-permute-start.9
  47.3 1.5 %collective-permute-start.8 = (f32[32,1024]{1,0:T(8,128)S(1)}, f32[32,1024]{1,0:T(8,128)S(1)}, u32[]{:S(2)}, u32[]{:S(2)}) collective-permute-start(f32[32,1024]{1,0:T(8,128)S(1)} %fusion.15.refs_0_), channel_id=1, source_target_pairs={{0,16},{8,24},{16,0},{24,8},{1,17},{9,25},{17,1},{25,9},{2,18},{10... | collective-permute-start | bytes 393224 | tf_op jit(solution)/shard_map/ppermute | solution.py:202
  48.8 1.4 %collective-permute-start.7 = (f32[32,1024]{1,0:T(8,128)S(1)}, f32[32,1024]{1,0:T(8,128)S(1)}, u32[]{:S(2)}, u32[]{:S(2)}) collective-permute-start(f32[32,1024]{1,0:T(8,128)S(1)} %fusion.15.refs_0_), channel_id=1, source_target_pairs={{0,8},{8,0},{16,24},{24,16},{1,9},{9,1},{17,25},{25,17},{2,10},{10... | collective-permute-start | bytes 393224 | tf_op jit(solution)/shard_map/ppermute | solution.py:202
  50.2 3.7 %collective-permute-done.9.refs_3_ = f32[32,1024]{1,0:T(8,128)S(1)} collective-permute-done((f32[32,1024]{1,0:T(8,128)S(1)}, f32[32,1024]{1,0:T(8,128)S(1)}, u32[]{:S(2)}, u32[]{:S(2)}) %collective-permute-start.9) | collective-permute-done | bytes 131104 | tf_op jit(solution)/shard_map/ppermute | solution.py:202
  53.9 1.0 collective-permute-done.8.refs_2_
  54.9 0.0 collective-permute-done.7.refs_1_
  54.9 3.8 %products.4 = (f32[4,32,1024]{2,1,0:T(8,128)S(1)}, f32[4,32,1024]{2,1,0:T(8,128)S(1)}, f32[1,1024]{1,0:T(1,128)S(1)}) custom-call(s32[128]{0:T(128)S(1)} %bitcast.70, s32[128]{0:T(128)S(1)} %bitcast.73, s32[2]{0:T(128)S(1)} %pad_add_fusion.place, f32[32,1024]{1,0:T(8,128)S(1)} %fusion.15.refs_0_, f32[32,1024]{1,0:T(8,128)S(1)} %collective-permute-done.7.refs_1_, ...), custom_call_target="tpu_custom_call" | custom-call | flops 536870912 | bytes 8388608 | tf_op jit(solution)/shard_map/products/pallas_call | solution.py:154
  58.6 0.1 collective-permute-start.10
  58.7 1.9 %collective-permute-done.10 = f32[4,32,1024]{2,1,0:T(8,128)S(1)} collective-permute-done((f32[4,32,1024]{2,1,0:T(8,128)S(1)}, f32[4,32,1024]{2,1,0:T(8,128)S(1)}, u32[]{:S(2)}, u32[]{:S(2)}) %collective-permute-start.10) | collective-permute-done | bytes 524320 | tf_op jit(solution)/shard_map/ppermute | solution.py:202
  60.6 0.1 add.40
  60.7 1.2 %collective-permute-start.11 = (f32[32,1024]{1,0:T(8,128)S(1)}, f32[32,1024]{1,0:T(8,128)S(1)}, u32[]{:S(2)}, u32[]{:S(2)}) collective-permute-start(f32[32,1024]{1,0:T(8,128)S(1)} %get-tuple-element.39), channel_id=1, source_target_pairs={{0,6},{1,7},{2,4},{3,5},{4,2},{5,3},{6,0},{7,1},{8,14},{9,15},{10,... | collective-permute-start | bytes 393224 | tf_op jit(solution)/shard_map/ppermute | solution.py:202
  61.9 0.0 collective-permute-start.13
  61.9 3.3 %collective-permute-start.12 = (f32[32,1024]{1,0:T(8,128)S(1)}, f32[32,1024]{1,0:T(8,128)S(1)}, u32[]{:S(2)}, u32[]{:S(2)}) collective-permute-start(f32[32,1024]{1,0:T(8,128)S(1)} %get-tuple-element.41), channel_id=1, source_target_pairs={{0,4},{1,5},{2,6},{3,7},{4,0},{5,1},{6,2},{7,3},{8,12},{9,13},{10,... | collective-permute-start | bytes 393224 | tf_op jit(solution)/shard_map/ppermute | solution.py:202
  65.2 3.9 %collective-permute-done.11 = f32[32,1024]{1,0:T(8,128)S(1)} collective-permute-done((f32[32,1024]{1,0:T(8,128)S(1)}, f32[32,1024]{1,0:T(8,128)S(1)}, u32[]{:S(2)}, u32[]{:S(2)}) %collective-permute-start.11) | collective-permute-done | bytes 131104 | tf_op jit(solution)/shard_map/ppermute | solution.py:202
  69.0 3.8 %collective-permute-done.13 = f32[32,1024]{1,0:T(8,128)S(1)} collective-permute-done((f32[32,1024]{1,0:T(8,128)S(1)}, f32[32,1024]{1,0:T(8,128)S(1)}, u32[]{:S(2)}, u32[]{:S(2)}) %collective-permute-start.13) | collective-permute-done | bytes 131104 | tf_op jit(solution)/shard_map/ppermute | solution.py:202
  72.8 0.0 collective-permute-done.12
  72.8 0.1 fusion.11.refs_0_
  72.8 1.4 %collective-permute-start.16 = (f32[32,1024]{1,0:T(8,128)S(1)}, f32[32,1024]{1,0:T(8,128)S(1)}, u32[]{:S(2)}, u32[]{:S(2)}) collective-permute-start(f32[32,1024]{1,0:T(8,128)S(1)} %fusion.11.refs_0_), channel_id=1, source_target_pairs={{0,24},{8,16},{16,8},{24,0},{1,25},{9,17},{17,9},{25,1},{2,26},{10... | collective-permute-start | bytes 393224 | tf_op jit(solution)/shard_map/ppermute | solution.py:202
  74.2 1.4 %collective-permute-start.15 = (f32[32,1024]{1,0:T(8,128)S(1)}, f32[32,1024]{1,0:T(8,128)S(1)}, u32[]{:S(2)}, u32[]{:S(2)}) collective-permute-start(f32[32,1024]{1,0:T(8,128)S(1)} %fusion.11.refs_0_), channel_id=1, source_target_pairs={{0,16},{8,24},{16,0},{24,8},{1,17},{9,25},{17,1},{25,9},{2,18},{10... | collective-permute-start | bytes 393224 | tf_op jit(solution)/shard_map/ppermute | solution.py:202
  75.6 1.0 collective-permute-start.14
  76.6 2.4 %collective-permute-done.16.refs_3_ = f32[32,1024]{1,0:T(8,128)S(1)} collective-permute-done((f32[32,1024]{1,0:T(8,128)S(1)}, f32[32,1024]{1,0:T(8,128)S(1)}, u32[]{:S(2)}, u32[]{:S(2)}) %collective-permute-start.16) | collective-permute-done | bytes 131104 | tf_op jit(solution)/shard_map/ppermute | solution.py:202
  79.1 2.1 %collective-permute-done.15.refs_2_ = f32[32,1024]{1,0:T(8,128)S(1)} collective-permute-done((f32[32,1024]{1,0:T(8,128)S(1)}, f32[32,1024]{1,0:T(8,128)S(1)}, u32[]{:S(2)}, u32[]{:S(2)}) %collective-permute-start.15) | collective-permute-done | bytes 131104 | tf_op jit(solution)/shard_map/ppermute | solution.py:202
  81.2 1.8 %collective-permute-done.14.refs_1_ = f32[32,1024]{1,0:T(8,128)S(1)} collective-permute-done((f32[32,1024]{1,0:T(8,128)S(1)}, f32[32,1024]{1,0:T(8,128)S(1)}, u32[]{:S(2)}, u32[]{:S(2)}) %collective-permute-start.14) | collective-permute-done | bytes 131104 | tf_op jit(solution)/shard_map/ppermute | solution.py:202
  82.9 3.8 %products.5 = (f32[4,32,1024]{2,1,0:T(8,128)S(1)}, f32[4,32,1024]{2,1,0:T(8,128)S(1)}, f32[1,1024]{1,0:T(1,128)S(1)}) custom-call(s32[128]{0:T(128)S(1)} %bitcast.71, s32[128]{0:T(128)S(1)} %bitcast.74, s32[2]{0:T(128)S(1)} %pad_add_fusion.place, f32[32,1024]{1,0:T(8,128)S(1)} %fusion.11.refs_0_, f32[32,1024]{1,0:T(8,128)S(1)} %collective-permute-done.14.refs_1_, ...), custom_call_target="tpu_custom_call" | custom-call | flops 536870912 | bytes 8388608 | tf_op jit(solution)/shard_map/products/pallas_call | solution.py:154
  86.7 0.1 collective-permute-start.17
  86.8 1.9 %collective-permute-done.17 = f32[4,32,1024]{2,1,0:T(8,128)S(1)} collective-permute-done((f32[4,32,1024]{2,1,0:T(8,128)S(1)}, f32[4,32,1024]{2,1,0:T(8,128)S(1)}, u32[]{:S(2)}, u32[]{:S(2)}) %collective-permute-start.17) | collective-permute-done | bytes 524320 | tf_op jit(solution)/shard_map/ppermute | solution.py:202
  88.7 0.1 add.44
  88.8 1.3 %collective-permute-start.18 = (f32[32,1024]{1,0:T(8,128)S(1)}, f32[32,1024]{1,0:T(8,128)S(1)}, u32[]{:S(2)}, u32[]{:S(2)}) collective-permute-start(f32[32,1024]{1,0:T(8,128)S(1)} %get-tuple-element.36), channel_id=1, source_target_pairs={{0,6},{1,7},{2,4},{3,5},{4,2},{5,3},{6,0},{7,1},{8,14},{9,15},{10,... | collective-permute-start | bytes 393224 | tf_op jit(solution)/shard_map/ppermute | solution.py:202
  90.1 0.0 collective-permute-start.20
  90.1 3.1 %collective-permute-start.19 = (f32[32,1024]{1,0:T(8,128)S(1)}, f32[32,1024]{1,0:T(8,128)S(1)}, u32[]{:S(2)}, u32[]{:S(2)}) collective-permute-start(f32[32,1024]{1,0:T(8,128)S(1)} %get-tuple-element.38), channel_id=1, source_target_pairs={{0,4},{1,5},{2,6},{3,7},{4,0},{5,1},{6,2},{7,3},{8,12},{9,13},{10,... | collective-permute-start | bytes 393224 | tf_op jit(solution)/shard_map/ppermute | solution.py:202
  93.2 3.8 %collective-permute-done.18 = f32[32,1024]{1,0:T(8,128)S(1)} collective-permute-done((f32[32,1024]{1,0:T(8,128)S(1)}, f32[32,1024]{1,0:T(8,128)S(1)}, u32[]{:S(2)}, u32[]{:S(2)}) %collective-permute-start.18) | collective-permute-done | bytes 131104 | tf_op jit(solution)/shard_map/ppermute | solution.py:202
  97.1 3.6 %collective-permute-done.20 = f32[32,1024]{1,0:T(8,128)S(1)} collective-permute-done((f32[32,1024]{1,0:T(8,128)S(1)}, f32[32,1024]{1,0:T(8,128)S(1)}, u32[]{:S(2)}, u32[]{:S(2)}) %collective-permute-start.20) | collective-permute-done | bytes 131104 | tf_op jit(solution)/shard_map/ppermute | solution.py:202
  100.7 1.5 %collective-permute-done.19 = f32[32,1024]{1,0:T(8,128)S(1)} collective-permute-done((f32[32,1024]{1,0:T(8,128)S(1)}, f32[32,1024]{1,0:T(8,128)S(1)}, u32[]{:S(2)}, u32[]{:S(2)}) %collective-permute-start.19) | collective-permute-done | bytes 131104 | tf_op jit(solution)/shard_map/ppermute | solution.py:202
  102.2 0.7 finish.1
  102.9 10.2 %all_to_all.10.parts_ref = f32[32,8,128]{2,1,0:T(8,128)S(1)} all-to-all(f32[32,8,128]{2,1,0:T(8,128)S(1)} %get-tuple-element.35), channel_id=1, replica_groups=mesh['row'=4,'col'=8] {'row','col'}, dimensions={0} | all-to-all | bytes 262144 | tf_op jit(solution)/shard_map/all_to_all | solution.py:253
  113.2 0.7 gram_sum.1
  (5 shorter events, 0.2 us)
Async XLA Ops:
  0.6 24.2 %copy-start = (f32[32,1024]{1,0:T(8,128)S(1)}, f32[32,1024]{1,0:T(8,128)}, u32[]{:S(2)}) copy-start(f32[32,1024]{1,0:T(8,128)} %refs_0_) | copy-start | bytes 393220
  0.6 24.2 %copy-start.1 = (s32[1,128]{1,0:T(1,128)S(1)}, s32[1,128]{1,0:T(1,128)}, u32[]{:S(2)}) copy-start(s32[1,128]{1,0:T(1,128)} %param.6) | copy-start | bytes 1540
  0.6 24.2 %copy-start.2 = (s32[1,128]{1,0:T(1,128)S(1)}, s32[1,128]{1,0:T(1,128)}, u32[]{:S(2)}) copy-start(s32[1,128]{1,0:T(1,128)} %param.7) | copy-start | bytes 1540
  0.7 9.7 %collective-permute-start.2 = (f32[32,1024]{1,0:T(8,128)}, f32[32,1024]{1,0:T(8,128)S(1)}, u32[]{:S(2)}, u32[]{:S(2)}) collective-permute-start(f32[32,1024]{1,0:T(8,128)} %refs_0_), channel_id=1, source_target_pairs={{0,24},{8,16},{16,8},{24,0},{1,25},{9,17},{17,9},{25,1},{2,26},{10... | collective-permute-start | bytes 393224 | tf_op jit(solution)/shard_map/ppermute | solution.py:202
  4.6 6.5 %collective-permute-start.1 = (f32[32,1024]{1,0:T(8,128)}, f32[32,1024]{1,0:T(8,128)S(1)}, u32[]{:S(2)}, u32[]{:S(2)}) collective-permute-start(f32[32,1024]{1,0:T(8,128)} %refs_0_), channel_id=1, source_target_pairs={{0,16},{8,24},{16,0},{24,8},{1,17},{9,25},{17,1},{25,9},{2,18},{10... | collective-permute-start | bytes 393224 | tf_op jit(solution)/shard_map/ppermute | solution.py:202
  5.1 6.3 %collective-permute-start = (f32[32,1024]{1,0:T(8,128)}, f32[32,1024]{1,0:T(8,128)S(1)}, u32[]{:S(2)}, u32[]{:S(2)}) collective-permute-start(f32[32,1024]{1,0:T(8,128)} %refs_0_), channel_id=1, source_target_pairs={{0,8},{8,0},{16,24},{24,16},{1,9},{9,1},{17,25},{25,17},{2,10},{10... | collective-permute-start | bytes 393224 | tf_op jit(solution)/shard_map/ppermute | solution.py:202
  11.4 13.4 %all-to-all-start = ((f32[32,8,128]{2,1,0:T(8,128)}), f32[32,8,128]{2,1,0:T(8,128)S(1)}, u32[]{:S(2)}, u32[]{:S(2)}) async-start(f32[32,8,128]{2,1,0:T(8,128)} %bitcast.4), calls=%async_computation | async-start | bytes 262144 | tf_op jit(solution)/shard_map/all_to_all | solution.py:220
  30.5 2.0 %collective-permute-start.3 = (f32[4,32,1024]{2,1,0:T(8,128)S(1)}, f32[4,32,1024]{2,1,0:T(8,128)S(1)}, u32[]{:S(2)}, u32[]{:S(2)}) collective-permute-start(f32[4,32,1024]{2,1,0:T(8,128)S(1)} %get-tuple-element.25), channel_id=1, source_target_pairs={{0,1},{1,0},{2,3},{3,2},{4,5},{5,4},{6,7},{7,6},{8,9},{9,8},{10,11... | collective-permute-start | bytes 1572872 | tf_op jit(solution)/shard_map/ppermute | solution.py:202
  32.5 8.2 %collective-permute-start.4 = (f32[32,1024]{1,0:T(8,128)S(1)}, f32[32,1024]{1,0:T(8,128)S(1)}, u32[]{:S(2)}, u32[]{:S(2)}) collective-permute-start(f32[32,1024]{1,0:T(8,128)S(1)} %get-tuple-element.42), channel_id=1, source_target_pairs={{0,6},{1,7},{2,4},{3,5},{4,2},{5,3},{6,0},{7,1},{8,14},{9,15},{10,... | collective-permute-start | bytes 393224 | tf_op jit(solution)/shard_map/ppermute | solution.py:202
  33.6 10.4 %collective-permute-start.6 = (f32[32,1024]{1,0:T(8,128)S(1)}, f32[32,1024]{1,0:T(8,128)S(1)}, u32[]{:S(2)}, u32[]{:S(2)}) collective-permute-start(f32[32,1024]{1,0:T(8,128)S(1)} %get-tuple-element.43), channel_id=1, source_target_pairs={{0,2},{1,3},{2,0},{3,1},{4,6},{5,7},{6,4},{7,5},{8,10},{9,11},{10,... | collective-permute-start | bytes 393224 | tf_op jit(solution)/shard_map/ppermute | solution.py:202
  33.6 13.0 %collective-permute-start.5 = (f32[32,1024]{1,0:T(8,128)S(1)}, f32[32,1024]{1,0:T(8,128)S(1)}, u32[]{:S(2)}, u32[]{:S(2)}) collective-permute-start(f32[32,1024]{1,0:T(8,128)S(1)} %get-tuple-element.44), channel_id=1, source_target_pairs={{0,4},{1,5},{2,6},{3,7},{4,0},{5,1},{6,2},{7,3},{8,12},{9,13},{10,... | collective-permute-start | bytes 393224 | tf_op jit(solution)/shard_map/ppermute | solution.py:202
  46.6 7.3 %collective-permute-start.9 = (f32[32,1024]{1,0:T(8,128)S(1)}, f32[32,1024]{1,0:T(8,128)S(1)}, u32[]{:S(2)}, u32[]{:S(2)}) collective-permute-start(f32[32,1024]{1,0:T(8,128)S(1)} %fusion.15.refs_0_), channel_id=1, source_target_pairs={{0,24},{8,16},{16,8},{24,0},{1,25},{9,17},{17,9},{25,1},{2,26},{10... | collective-permute-start | bytes 393224 | tf_op jit(solution)/shard_map/ppermute | solution.py:202
  47.3 7.5 %collective-permute-start.8 = (f32[32,1024]{1,0:T(8,128)S(1)}, f32[32,1024]{1,0:T(8,128)S(1)}, u32[]{:S(2)}, u32[]{:S(2)}) collective-permute-start(f32[32,1024]{1,0:T(8,128)S(1)} %fusion.15.refs_0_), channel_id=1, source_target_pairs={{0,16},{8,24},{16,0},{24,8},{1,17},{9,25},{17,1},{25,9},{2,18},{10... | collective-permute-start | bytes 393224 | tf_op jit(solution)/shard_map/ppermute | solution.py:202
  48.8 6.0 %collective-permute-start.7 = (f32[32,1024]{1,0:T(8,128)S(1)}, f32[32,1024]{1,0:T(8,128)S(1)}, u32[]{:S(2)}, u32[]{:S(2)}) collective-permute-start(f32[32,1024]{1,0:T(8,128)S(1)} %fusion.15.refs_0_), channel_id=1, source_target_pairs={{0,8},{8,0},{16,24},{24,16},{1,9},{9,1},{17,25},{25,17},{2,10},{10... | collective-permute-start | bytes 393224 | tf_op jit(solution)/shard_map/ppermute | solution.py:202
  58.6 2.0 %collective-permute-start.10 = (f32[4,32,1024]{2,1,0:T(8,128)S(1)}, f32[4,32,1024]{2,1,0:T(8,128)S(1)}, u32[]{:S(2)}, u32[]{:S(2)}) collective-permute-start(f32[4,32,1024]{2,1,0:T(8,128)S(1)} %get-tuple-element.29), channel_id=1, source_target_pairs={{0,1},{1,0},{2,3},{3,2},{4,5},{5,4},{6,7},{7,6},{8,9},{9,8},{10,11... | collective-permute-start | bytes 1572872 | tf_op jit(solution)/shard_map/ppermute | solution.py:202
  60.7 8.3 %collective-permute-start.11 = (f32[32,1024]{1,0:T(8,128)S(1)}, f32[32,1024]{1,0:T(8,128)S(1)}, u32[]{:S(2)}, u32[]{:S(2)}) collective-permute-start(f32[32,1024]{1,0:T(8,128)S(1)} %get-tuple-element.39), channel_id=1, source_target_pairs={{0,6},{1,7},{2,4},{3,5},{4,2},{5,3},{6,0},{7,1},{8,14},{9,15},{10,... | collective-permute-start | bytes 393224 | tf_op jit(solution)/shard_map/ppermute | solution.py:202
  61.9 10.9 %collective-permute-start.13 = (f32[32,1024]{1,0:T(8,128)S(1)}, f32[32,1024]{1,0:T(8,128)S(1)}, u32[]{:S(2)}, u32[]{:S(2)}) collective-permute-start(f32[32,1024]{1,0:T(8,128)S(1)} %get-tuple-element.40), channel_id=1, source_target_pairs={{0,2},{1,3},{2,0},{3,1},{4,6},{5,7},{6,4},{7,5},{8,10},{9,11},{10,... | collective-permute-start | bytes 393224 | tf_op jit(solution)/shard_map/ppermute | solution.py:202
  61.9 10.9 %collective-permute-start.12 = (f32[32,1024]{1,0:T(8,128)S(1)}, f32[32,1024]{1,0:T(8,128)S(1)}, u32[]{:S(2)}, u32[]{:S(2)}) collective-permute-start(f32[32,1024]{1,0:T(8,128)S(1)} %get-tuple-element.41), channel_id=1, source_target_pairs={{0,4},{1,5},{2,6},{3,7},{4,0},{5,1},{6,2},{7,3},{8,12},{9,13},{10,... | collective-permute-start | bytes 393224 | tf_op jit(solution)/shard_map/ppermute | solution.py:202
  72.8 6.2 %collective-permute-start.16 = (f32[32,1024]{1,0:T(8,128)S(1)}, f32[32,1024]{1,0:T(8,128)S(1)}, u32[]{:S(2)}, u32[]{:S(2)}) collective-permute-start(f32[32,1024]{1,0:T(8,128)S(1)} %fusion.11.refs_0_), channel_id=1, source_target_pairs={{0,24},{8,16},{16,8},{24,0},{1,25},{9,17},{17,9},{25,1},{2,26},{10... | collective-permute-start | bytes 393224 | tf_op jit(solution)/shard_map/ppermute | solution.py:202
  74.2 6.9 %collective-permute-start.15 = (f32[32,1024]{1,0:T(8,128)S(1)}, f32[32,1024]{1,0:T(8,128)S(1)}, u32[]{:S(2)}, u32[]{:S(2)}) collective-permute-start(f32[32,1024]{1,0:T(8,128)S(1)} %fusion.11.refs_0_), channel_id=1, source_target_pairs={{0,16},{8,24},{16,0},{24,8},{1,17},{9,25},{17,1},{25,9},{2,18},{10... | collective-permute-start | bytes 393224 | tf_op jit(solution)/shard_map/ppermute | solution.py:202
  75.6 7.3 %collective-permute-start.14 = (f32[32,1024]{1,0:T(8,128)S(1)}, f32[32,1024]{1,0:T(8,128)S(1)}, u32[]{:S(2)}, u32[]{:S(2)}) collective-permute-start(f32[32,1024]{1,0:T(8,128)S(1)} %fusion.11.refs_0_), channel_id=1, source_target_pairs={{0,8},{8,0},{16,24},{24,16},{1,9},{9,1},{17,25},{25,17},{2,10},{10... | collective-permute-start | bytes 393224 | tf_op jit(solution)/shard_map/ppermute | solution.py:202
  86.7 2.0 %collective-permute-start.17 = (f32[4,32,1024]{2,1,0:T(8,128)S(1)}, f32[4,32,1024]{2,1,0:T(8,128)S(1)}, u32[]{:S(2)}, u32[]{:S(2)}) collective-permute-start(f32[4,32,1024]{2,1,0:T(8,128)S(1)} %get-tuple-element.32), channel_id=1, source_target_pairs={{0,1},{1,0},{2,3},{3,2},{4,5},{5,4},{6,7},{7,6},{8,9},{9,8},{10,11... | collective-permute-start | bytes 1572872 | tf_op jit(solution)/shard_map/ppermute | solution.py:202
  88.8 8.3 %collective-permute-start.18 = (f32[32,1024]{1,0:T(8,128)S(1)}, f32[32,1024]{1,0:T(8,128)S(1)}, u32[]{:S(2)}, u32[]{:S(2)}) collective-permute-start(f32[32,1024]{1,0:T(8,128)S(1)} %get-tuple-element.36), channel_id=1, source_target_pairs={{0,6},{1,7},{2,4},{3,5},{4,2},{5,3},{6,0},{7,1},{8,14},{9,15},{10,... | collective-permute-start | bytes 393224 | tf_op jit(solution)/shard_map/ppermute | solution.py:202
  90.1 10.6 %collective-permute-start.20 = (f32[32,1024]{1,0:T(8,128)S(1)}, f32[32,1024]{1,0:T(8,128)S(1)}, u32[]{:S(2)}, u32[]{:S(2)}) collective-permute-start(f32[32,1024]{1,0:T(8,128)S(1)} %get-tuple-element.37), channel_id=1, source_target_pairs={{0,2},{1,3},{2,0},{3,1},{4,6},{5,7},{6,4},{7,5},{8,10},{9,11},{10,... | collective-permute-start | bytes 393224 | tf_op jit(solution)/shard_map/ppermute | solution.py:202
  90.1 12.1 %collective-permute-start.19 = (f32[32,1024]{1,0:T(8,128)S(1)}, f32[32,1024]{1,0:T(8,128)S(1)}, u32[]{:S(2)}, u32[]{:S(2)}) collective-permute-start(f32[32,1024]{1,0:T(8,128)S(1)} %get-tuple-element.38), channel_id=1, source_target_pairs={{0,4},{1,5},{2,6},{3,7},{4,0},{5,1},{6,2},{7,3},{8,12},{9,13},{10,... | collective-permute-start | bytes 393224 | tf_op jit(solution)/shard_map/ppermute | solution.py:202

commit v5 on v4

--- a/solution.py
+++ b/solution.py
@@ -229,10 +229,19 @@
         if loaded:
             tiles = loaded[0]
         chip = keep + swap(give, "col", n_col, 1)
-        totals = [chip[0]] + [
-            swap(chip[j], "col", n_col, 2 * j) for j in reversed(range(1, n_col // 2))
-        ]
-        following = sum(totals[1:], totals[0]) * scale
+        if n_col == 8:
+            half = k // 2
+            passed = swap(chip[3, :half], "col", n_col, 2)
+            across = swap(chip[3, half:], "col", n_col, 6)
+            second = swap(chip[2, half:], "col", n_col, 4)
+            merged = swap(chip[2, :half] + passed, "col", n_col, 4)
+            first = swap(chip[1], "col", n_col, 2)
+            total = chip[0] + first + jnp.concatenate([merged, second + across], axis=0)
+        else:
+            total = chip[0]
+            for j in reversed(range(1, n_col // 2)):
+                total = total + swap(chip[j], "col", n_col, 2 * j)
+        following = total * scale
         if step > 0:
             following = 2.0 * following - previous
         previous, current = current, following

time: 114 us -> 114 us (level)
  waiting for transfers between devices: 51.7 us -> 46.5 us
  starting transfers between devices: 31.1 us -> 35.3 us
    ppermute x21 -> x27, waiting for transfers between devices: 43.6 us -> 38.4 us  [swap(): return lax.ppermute(value, axis, [(i, i ^ by) for i in range(size)])]
    ppermute x21 -> x27, starting transfers between devices: 25.8 us -> 30.1 us  [swap(): return lax.ppermute(value, axis, [(i, i ^ by) for i in range(size)])]
  transfers between devices with their start and end apart: 22 -> 28, of which waited for: 19 -> 22; matrix products, arithmetic and copies ran while one was open for 0% -> 0% of each run, Pallas kernels for 4% -> 4%
where the time goes in v5:
time: 114 us
  waiting for transfers between devices  46.5 us (41%)
  starting transfers between devices  35.3 us (31%)
  Pallas kernels  19.6 us (17%)
  blocking collectives  11.1 us (10%)
    ppermute x27, waiting for transfers between devices, swap(): return lax.ppermute(value, axis, [(i, i ^ by) for i in range(size)])  38.4 us
    ppermute x27, starting transfers between devices, swap(): return lax.ppermute(value, axis, [(i, i ^ by) for i in range(size)])  30.1 us
    pallas_call x3, Pallas kernels, products(): pl.pallas_call(functools.partial(product_kernel, n_row, n_col, owned, loa...  13.1 us
    all_to_all x1, blocking collectives, on_device(): grams = lax.all_to_all(grams, ('row', 'col'), 0, 0, tiled=True)  11.1 us
    all_to_all x1, waiting for transfers between devices, on_device(): lax.all_to_all(sent.reshape(devices, owned, TB), ('row', 'col'), 0, 0, ti...  8.09 us
    all_to_all x1, starting transfers between devices, on_device(): lax.all_to_all(sent.reshape(devices, owned, TB), ('row', 'col'), 0, 0, ti...  5.25 us
    pallas_call x1, Pallas kernels, degree_terms(): pl.pallas_call(degree_kernel, out_shape=pltpu.VMEM((n_row, n_col, owned,...  5.08 us
  transfers between devices with their start and end apart: 28, of which 22 were waited for; matrix products, arithmetic and copies ran while one was open for 0% of the time, Pallas kernels for 4%

profile of v5, /device:TPU:0, one launch (start us, length us, event | category | flops | bytes accessed | tf_op | source)
XLA Modules:
  0.0 113.9 jit_solution(15505936005754309066)
XLA Ops:
  0.7 4.0 %collective-permute-start.2 = (f32[32,1024]{1,0:T(8,128)}, f32[32,1024]{1,0:T(8,128)S(1)}, u32[]{:S(2)}, u32[]{:S(2)}) collective-permute-start(f32[32,1024]{1,0:T(8,128)} %refs_0_), channel_id=1, source_target_pairs={{0,24},{8,16},{16,8},{24,0},{1,25},{9,17},{17,9},{25,1},{2,26},{10... | collective-permute-start | bytes 393224 | tf_op jit(solution)/shard_map/ppermute | solution.py:202
  4.6 0.5 collective-permute-start.1
  5.1 0.1 collective-permute-start
  5.3 5.1 %degree_terms.1 = f32[4,8,8,128]{3,2,1,0:T(8,128)} custom-call(s32[128]{0:T(128)} %bitcast.80, f32[128,128,128]{2,1,0:T(8,128)} %refs_5_.1), custom_call_target="tpu_custom_call" | custom-call | flops 4194304 | bytes 8388608 | tf_op jit(solution)/shard_map/degree_terms/pallas_call | solution.py:69
  10.4 0.8 collective-permute-done.1.refs_2_
  11.1 0.2 collective-permute-done.refs_1_
  11.4 5.2 %all-to-all-start = ((f32[32,8,128]{2,1,0:T(8,128)}), f32[32,8,128]{2,1,0:T(8,128)S(1)}, u32[]{:S(2)}, u32[]{:S(2)}) async-start(f32[32,8,128]{2,1,0:T(8,128)} %bitcast.4), calls=%async_computation | async-start | bytes 262144 | tf_op jit(solution)/shard_map/all_to_all | solution.py:220
  16.6 0.1 pad_add_fusion.place
  16.7 8.1 %all-to-all-done = f32[32,8,128]{2,1,0:T(8,128)S(1)} async-done(((f32[32,8,128]{2,1,0:T(8,128)}), f32[32,8,128]{2,1,0:T(8,128)S(1)}, u32[]{:S(2)}, u32[]{:S(2)}) %all-to-all-start) | async-done | bytes 131104 | tf_op jit(solution)/shard_map/all_to_all | solution.py:220
  24.8 5.6 %products.3 = (f32[4,32,1024]{2,1,0:T(8,128)S(1)}, f32[4,32,1024]{2,1,0:T(8,128)S(1)}, f32[1,1024]{1,0:T(1,128)S(1)}, f32[128,128,128]{2,1,0:T(8,128)S(1)}) custom-call(s32[128]{0:T(128)S(1)} %bitcast.81, s32[128]{0:T(128)S(1)} %bitcast.84, s32[2]{0:T(128)S(1)} %pad_add_fusion.place, f32[32,1024]{1,0:T(8,128)S(1)} %copy-done, ...), custom_call_target="tpu_custom_call" | custom-call | flops 536870912 | bytes 8388608 | tf_op jit(solution)/shard_map/products/pallas_call | solution.py:154
  30.5 0.4 collective-permute-start.3
  30.9 1.6 %collective-permute-done.3 = f32[4,32,1024]{2,1,0:T(8,128)S(1)} collective-permute-done((f32[4,32,1024]{2,1,0:T(8,128)S(1)}, f32[4,32,1024]{2,1,0:T(8,128)S(1)}, u32[]{:S(2)}, u32[]{:S(2)}) %collective-permute-start.3) | collective-permute-done | bytes 524320 | tf_op jit(solution)/shard_map/ppermute | solution.py:202
  32.4 0.1 add.45
  32.5 0.6 collective-permute-start.5
  33.2 1.5 %collective-permute-start.4 = (f32[32,1024]{1,0:T(8,128)S(1)}, f32[32,1024]{1,0:T(8,128)S(1)}, u32[]{:S(2)}, u32[]{:S(2)}) collective-permute-start(f32[32,1024]{1,0:T(8,128)S(1)} %slice_bitcast_fusion.4), channel_id=1, source_target_pairs={{0,2},{1,3},{2,0},{3,1},{4,6},{5,7},{6,4},{7,5},{8,10},{9,11},{10,... | collective-permute-start | bytes 393224 | tf_op jit(solution)/shard_map/ppermute | solution.py:202
  34.7 1.0 collective-permute-start.8
  35.7 1.1 collective-permute-start.7
  36.7 0.8 collective-permute-done.5
  37.5 1.2 %collective-permute-start.6 = (f32[16,1024]{1,0:T(8,128)S(1)}, f32[16,1024]{1,0:T(8,128)S(1)}, u32[]{:S(2)}, u32[]{:S(2)}) collective-permute-start(f32[16,1024]{1,0:T(8,128)S(1)} %fusion.15), channel_id=1, source_target_pairs={{0,4},{1,5},{2,6},{3,7},{4,0},{5,1},{6,2},{7,3},{8,12},{9,13},{10,... | collective-permute-start | bytes 196616 | tf_op jit(solution)/shard_map/ppermute | solution.py:202
  38.7 2.9 %collective-permute-done.8 = f32[16,1024]{1,0:T(8,128)S(1)} collective-permute-done((f32[16,1024]{1,0:T(8,128)S(1)}, f32[16,1024]{1,0:T(8,128)S(1)}, u32[]{:S(2)}, u32[]{:S(2)}) %collective-permute-start.8) | collective-permute-done | bytes 65568 | tf_op jit(solution)/shard_map/ppermute | solution.py:202
  41.6 3.6 %collective-permute-done.7 = f32[16,1024]{1,0:T(8,128)S(1)} collective-permute-done((f32[16,1024]{1,0:T(8,128)S(1)}, f32[16,1024]{1,0:T(8,128)S(1)}, u32[]{:S(2)}, u32[]{:S(2)}) %collective-permute-start.7) | collective-permute-done | bytes 65568 | tf_op jit(solution)/shard_map/ppermute | solution.py:202
  45.3 0.0 collective-permute-done.4
  45.3 0.7 collective-permute-done.6
  46.0 0.7 collective-permute-start.11
  46.8 1.3 %collective-permute-start.10 = (f32[32,1024]{1,0:T(8,128)S(1)}, f32[32,1024]{1,0:T(8,128)S(1)}, u32[]{:S(2)}, u32[]{:S(2)}) collective-permute-start(f32[32,1024]{1,0:T(8,128)S(1)} %fusion.12.refs_0_), channel_id=1, source_target_pairs={{0,16},{8,24},{16,0},{24,8},{1,17},{9,25},{17,1},{25,9},{2,18},{10... | collective-permute-start | bytes 393224 | tf_op jit(solution)/shard_map/ppermute | solution.py:202
  48.0 1.6 %collective-permute-start.9 = (f32[32,1024]{1,0:T(8,128)S(1)}, f32[32,1024]{1,0:T(8,128)S(1)}, u32[]{:S(2)}, u32[]{:S(2)}) collective-permute-start(f32[32,1024]{1,0:T(8,128)S(1)} %fusion.12.refs_0_), channel_id=1, source_target_pairs={{0,8},{8,0},{16,24},{24,16},{1,9},{9,1},{17,25},{25,17},{2,10},{10... | collective-permute-start | bytes 393224 | tf_op jit(solution)/shard_map/ppermute | solution.py:202
  49.6 3.7 %collective-permute-done.11.refs_3_ = f32[32,1024]{1,0:T(8,128)S(1)} collective-permute-done((f32[32,1024]{1,0:T(8,128)S(1)}, f32[32,1024]{1,0:T(8,128)S(1)}, u32[]{:S(2)}, u32[]{:S(2)}) %collective-permute-start.11) | collective-permute-done | bytes 131104 | tf_op jit(solution)/shard_map/ppermute | solution.py:202
  53.3 0.7 collective-permute-done.10.refs_2_
  54.1 0.0 collective-permute-done.9.refs_1_
  54.1 3.8 %products.4 = (f32[4,32,1024]{2,1,0:T(8,128)S(1)}, f32[4,32,1024]{2,1,0:T(8,128)S(1)}, f32[1,1024]{1,0:T(1,128)S(1)}) custom-call(s32[128]{0:T(128)S(1)} %bitcast.82, s32[128]{0:T(128)S(1)} %bitcast.85, s32[2]{0:T(128)S(1)} %pad_add_fusion.place, f32[32,1024]{1,0:T(8,128)S(1)} %fusion.12.refs_0_, f32[32,1024]{1,0:T(8,128)S(1)} %collective-permute-done.9.refs_1_, ...), custom_call_target="tpu_custom_call" | custom-call | flops 536870912 | bytes 8388608 | tf_op jit(solution)/shard_map/products/pallas_call | solution.py:154
  57.8 0.1 collective-permute-start.12
  57.9 1.9 %collective-permute-done.12 = f32[4,32,1024]{2,1,0:T(8,128)S(1)} collective-permute-done((f32[4,32,1024]{2,1,0:T(8,128)S(1)}, f32[4,32,1024]{2,1,0:T(8,128)S(1)}, u32[]{:S(2)}, u32[]{:S(2)}) %collective-permute-start.12) | collective-permute-done | bytes 524320 | tf_op jit(solution)/shard_map/ppermute | solution.py:202
  59.8 0.1 add.50
  59.9 0.1 collective-permute-start.14
  60.0 2.1 %collective-permute-start.13 = (f32[32,1024]{1,0:T(8,128)S(1)}, f32[32,1024]{1,0:T(8,128)S(1)}, u32[]{:S(2)}, u32[]{:S(2)}) collective-permute-start(f32[32,1024]{1,0:T(8,128)S(1)} %slice_bitcast_fusion.2), channel_id=1, source_target_pairs={{0,2},{1,3},{2,0},{3,1},{4,6},{5,7},{6,4},{7,5},{8,10},{9,11},{10,... | collective-permute-start | bytes 393224 | tf_op jit(solution)/shard_map/ppermute | solution.py:202
  62.1 2.1 %collective-permute-start.17 = (f32[16,1024]{1,0:T(8,128)S(1)}, f32[16,1024]{1,0:T(8,128)S(1)}, u32[]{:S(2)}, u32[]{:S(2)}) collective-permute-start(f32[16,1024]{1,0:T(8,128)S(1)} %get-tuple-element.40), channel_id=1, source_target_pairs={{0,6},{1,7},{2,4},{3,5},{4,2},{5,3},{6,0},{7,1},{8,14},{9,15},{10,... | collective-permute-start | bytes 196616 | tf_op jit(solution)/shard_map/ppermute | solution.py:202
  64.2 0.0 collective-permute-start.16
  64.2 0.7 collective-permute-done.14
  64.9 2.3 %collective-permute-start.15 = (f32[16,1024]{1,0:T(8,128)S(1)}, f32[16,1024]{1,0:T(8,128)S(1)}, u32[]{:S(2)}, u32[]{:S(2)}) collective-permute-start(f32[16,1024]{1,0:T(8,128)S(1)} %fusion.14), channel_id=1, source_target_pairs={{0,4},{1,5},{2,6},{3,7},{4,0},{5,1},{6,2},{7,3},{8,12},{9,13},{10,... | collective-permute-start | bytes 196616 | tf_op jit(solution)/shard_map/ppermute | solution.py:202
  67.2 2.9 %collective-permute-done.17 = f32[16,1024]{1,0:T(8,128)S(1)} collective-permute-done((f32[16,1024]{1,0:T(8,128)S(1)}, f32[16,1024]{1,0:T(8,128)S(1)}, u32[]{:S(2)}, u32[]{:S(2)}) %collective-permute-start.17) | collective-permute-done | bytes 65568 | tf_op jit(solution)/shard_map/ppermute | solution.py:202
  70.0 2.9 %collective-permute-done.16 = f32[16,1024]{1,0:T(8,128)S(1)} collective-permute-done((f32[16,1024]{1,0:T(8,128)S(1)}, f32[16,1024]{1,0:T(8,128)S(1)}, u32[]{:S(2)}, u32[]{:S(2)}) %collective-permute-start.16) | collective-permute-done | bytes 65568 | tf_op jit(solution)/shard_map/ppermute | solution.py:202
  73.0 0.0 collective-permute-done.13
  73.0 0.7 collective-permute-done.15
  73.7 1.2 %collective-permute-start.20 = (f32[32,1024]{1,0:T(8,128)S(1)}, f32[32,1024]{1,0:T(8,128)S(1)}, u32[]{:S(2)}, u32[]{:S(2)}) collective-permute-start(f32[32,1024]{1,0:T(8,128)S(1)} %fusion.9.refs_0_), channel_id=1, source_target_pairs={{0,24},{8,16},{16,8},{24,0},{1,25},{9,17},{17,9},{25,1},{2,26},{10... | collective-permute-start | bytes 393224 | tf_op jit(solution)/shard_map/ppermute | solution.py:202
  74.9 1.3 %collective-permute-start.19 = (f32[32,1024]{1,0:T(8,128)S(1)}, f32[32,1024]{1,0:T(8,128)S(1)}, u32[]{:S(2)}, u32[]{:S(2)}) collective-permute-start(f32[32,1024]{1,0:T(8,128)S(1)} %fusion.9.refs_0_), channel_id=1, source_target_pairs={{0,16},{8,24},{16,0},{24,8},{1,17},{9,25},{17,1},{25,9},{2,18},{10... | collective-permute-start | bytes 393224 | tf_op jit(solution)/shard_map/ppermute | solution.py:202
  76.2 1.0 collective-permute-start.18
  77.2 3.5 %collective-permute-done.20.refs_3_ = f32[32,1024]{1,0:T(8,128)S(1)} collective-permute-done((f32[32,1024]{1,0:T(8,128)S(1)}, f32[32,1024]{1,0:T(8,128)S(1)}, u32[]{:S(2)}, u32[]{:S(2)}) %collective-permute-start.20) | collective-permute-done | bytes 131104 | tf_op jit(solution)/shard_map/ppermute | solution.py:202
  80.7 1.3 %collective-permute-done.19.refs_2_ = f32[32,1024]{1,0:T(8,128)S(1)} collective-permute-done((f32[32,1024]{1,0:T(8,128)S(1)}, f32[32,1024]{1,0:T(8,128)S(1)}, u32[]{:S(2)}, u32[]{:S(2)}) %collective-permute-start.19) | collective-permute-done | bytes 131104 | tf_op jit(solution)/shard_map/ppermute | solution.py:202
  82.0 0.0 collective-permute-done.18.refs_1_
  82.0 3.8 %products.5 = (f32[4,32,1024]{2,1,0:T(8,128)S(1)}, f32[4,32,1024]{2,1,0:T(8,128)S(1)}, f32[1,1024]{1,0:T(1,128)S(1)}) custom-call(s32[128]{0:T(128)S(1)} %bitcast.83, s32[128]{0:T(128)S(1)} %bitcast.86, s32[2]{0:T(128)S(1)} %pad_add_fusion.place, f32[32,1024]{1,0:T(8,128)S(1)} %fusion.9.refs_0_, f32[32,1024]{1,0:T(8,128)S(1)} %collective-permute-done.18.refs_1_, ...), custom_call_target="tpu_custom_call" | custom-call | flops 536870912 | bytes 8388608 | tf_op jit(solution)/shard_map/products/pallas_call | solution.py:154
  85.8 0.1 collective-permute-start.21
  85.9 1.9 %collective-permute-done.21 = f32[4,32,1024]{2,1,0:T(8,128)S(1)} collective-permute-done((f32[4,32,1024]{2,1,0:T(8,128)S(1)}, f32[4,32,1024]{2,1,0:T(8,128)S(1)}, u32[]{:S(2)}, u32[]{:S(2)}) %collective-permute-start.21) | collective-permute-done | bytes 524320 | tf_op jit(solution)/shard_map/ppermute | solution.py:202
  87.8 0.1 add.55
  87.9 0.1 collective-permute-start.23
  88.0 2.1 %collective-permute-start.22 = (f32[32,1024]{1,0:T(8,128)S(1)}, f32[32,1024]{1,0:T(8,128)S(1)}, u32[]{:S(2)}, u32[]{:S(2)}) collective-permute-start(f32[32,1024]{1,0:T(8,128)S(1)} %slice_bitcast_fusion), channel_id=1, source_target_pairs={{0,2},{1,3},{2,0},{3,1},{4,6},{5,7},{6,4},{7,5},{8,10},{9,11},{10,... | collective-permute-start | bytes 393224 | tf_op jit(solution)/shard_map/ppermute | solution.py:202
  90.0 1.8 %collective-permute-start.26 = (f32[16,1024]{1,0:T(8,128)S(1)}, f32[16,1024]{1,0:T(8,128)S(1)}, u32[]{:S(2)}, u32[]{:S(2)}) collective-permute-start(f32[16,1024]{1,0:T(8,128)S(1)} %get-tuple-element.37), channel_id=1, source_target_pairs={{0,6},{1,7},{2,4},{3,5},{4,2},{5,3},{6,0},{7,1},{8,14},{9,15},{10,... | collective-permute-start | bytes 196616 | tf_op jit(solution)/shard_map/ppermute | solution.py:202
  91.8 1.0 collective-permute-done.23
  92.9 2.0 %collective-permute-start.24 = (f32[16,1024]{1,0:T(8,128)S(1)}, f32[16,1024]{1,0:T(8,128)S(1)}, u32[]{:S(2)}, u32[]{:S(2)}) collective-permute-start(f32[16,1024]{1,0:T(8,128)S(1)} %fusion.13), channel_id=1, source_target_pairs={{0,4},{1,5},{2,6},{3,7},{4,0},{5,1},{6,2},{7,3},{8,12},{9,13},{10,... | collective-permute-start | bytes 196616 | tf_op jit(solution)/shard_map/ppermute | solution.py:202
  94.8 2.8 %collective-permute-done.26 = f32[16,1024]{1,0:T(8,128)S(1)} collective-permute-done((f32[16,1024]{1,0:T(8,128)S(1)}, f32[16,1024]{1,0:T(8,128)S(1)}, u32[]{:S(2)}, u32[]{:S(2)}) %collective-permute-start.26) | collective-permute-done | bytes 65568 | tf_op jit(solution)/shard_map/ppermute | solution.py:202
  97.7 3.0 %collective-permute-done.25 = f32[16,1024]{1,0:T(8,128)S(1)} collective-permute-done((f32[16,1024]{1,0:T(8,128)S(1)}, f32[16,1024]{1,0:T(8,128)S(1)}, u32[]{:S(2)}, u32[]{:S(2)}) %collective-permute-start.25) | collective-permute-done | bytes 65568 | tf_op jit(solution)/shard_map/ppermute | solution.py:202
  100.7 0.7 collective-permute-done.24
  101.4 0.7 finish.1
  102.0 11.1 %all_to_all.10.parts_ref = f32[32,8,128]{2,1,0:T(8,128)S(1)} all-to-all(f32[32,8,128]{2,1,0:T(8,128)S(1)} %get-tuple-element.35), channel_id=1, replica_groups=mesh['row'=4,'col'=8] {'row','col'}, dimensions={0} | all-to-all | bytes 262144 | tf_op jit(solution)/shard_map/all_to_all | solution.py:262
  113.2 0.7 gram_sum.1
  (24 shorter events, 0.3 us)
Async XLA Ops:
  0.6 24.2 %copy-start = (f32[32,1024]{1,0:T(8,128)S(1)}, f32[32,1024]{1,0:T(8,128)}, u32[]{:S(2)}) copy-start(f32[32,1024]{1,0:T(8,128)} %refs_0_) | copy-start | bytes 393220
  0.6 24.2 %copy-start.1 = (s32[1,128]{1,0:T(1,128)S(1)}, s32[1,128]{1,0:T(1,128)}, u32[]{:S(2)}) copy-start(s32[1,128]{1,0:T(1,128)} %param.6) | copy-start | bytes 1540
  0.6 24.2 %copy-start.2 = (s32[1,128]{1,0:T(1,128)S(1)}, s32[1,128]{1,0:T(1,128)}, u32[]{:S(2)}) copy-start(s32[1,128]{1,0:T(1,128)} %param.7) | copy-start | bytes 1540
  0.7 9.7 %collective-permute-start.2 = (f32[32,1024]{1,0:T(8,128)}, f32[32,1024]{1,0:T(8,128)S(1)}, u32[]{:S(2)}, u32[]{:S(2)}) collective-permute-start(f32[32,1024]{1,0:T(8,128)} %refs_0_), channel_id=1, source_target_pairs={{0,24},{8,16},{16,8},{24,0},{1,25},{9,17},{17,9},{25,1},{2,26},{10... | collective-permute-start | bytes 393224 | tf_op jit(solution)/shard_map/ppermute | solution.py:202
  4.6 6.5 %collective-permute-start.1 = (f32[32,1024]{1,0:T(8,128)}, f32[32,1024]{1,0:T(8,128)S(1)}, u32[]{:S(2)}, u32[]{:S(2)}) collective-permute-start(f32[32,1024]{1,0:T(8,128)} %refs_0_), channel_id=1, source_target_pairs={{0,16},{8,24},{16,0},{24,8},{1,17},{9,25},{17,1},{25,9},{2,18},{10... | collective-permute-start | bytes 393224 | tf_op jit(solution)/shard_map/ppermute | solution.py:202
  5.1 6.3 %collective-permute-start = (f32[32,1024]{1,0:T(8,128)}, f32[32,1024]{1,0:T(8,128)S(1)}, u32[]{:S(2)}, u32[]{:S(2)}) collective-permute-start(f32[32,1024]{1,0:T(8,128)} %refs_0_), channel_id=1, source_target_pairs={{0,8},{8,0},{16,24},{24,16},{1,9},{9,1},{17,25},{25,17},{2,10},{10... | collective-permute-start | bytes 393224 | tf_op jit(solution)/shard_map/ppermute | solution.py:202
  11.4 13.4 %all-to-all-start = ((f32[32,8,128]{2,1,0:T(8,128)}), f32[32,8,128]{2,1,0:T(8,128)S(1)}, u32[]{:S(2)}, u32[]{:S(2)}) async-start(f32[32,8,128]{2,1,0:T(8,128)} %bitcast.4), calls=%async_computation | async-start | bytes 262144 | tf_op jit(solution)/shard_map/all_to_all | solution.py:220
  30.5 2.0 %collective-permute-start.3 = (f32[4,32,1024]{2,1,0:T(8,128)S(1)}, f32[4,32,1024]{2,1,0:T(8,128)S(1)}, u32[]{:S(2)}, u32[]{:S(2)}) collective-permute-start(f32[4,32,1024]{2,1,0:T(8,128)S(1)} %get-tuple-element.25), channel_id=1, source_target_pairs={{0,1},{1,0},{2,3},{3,2},{4,5},{5,4},{6,7},{7,6},{8,9},{9,8},{10,11... | collective-permute-start | bytes 1572872 | tf_op jit(solution)/shard_map/ppermute | solution.py:202
  32.5 5.0 %collective-permute-start.5 = (f32[16,1024]{1,0:T(8,128)S(1)}, f32[16,1024]{1,0:T(8,128)S(1)}, u32[]{:S(2)}, u32[]{:S(2)}) collective-permute-start(f32[16,1024]{1,0:T(8,128)S(1)} %get-tuple-element.42), channel_id=1, source_target_pairs={{0,2},{1,3},{2,0},{3,1},{4,6},{5,7},{6,4},{7,5},{8,10},{9,11},{10,... | collective-permute-start | bytes 196616 | tf_op jit(solution)/shard_map/ppermute | solution.py:202
  33.2 12.1 %collective-permute-start.4 = (f32[32,1024]{1,0:T(8,128)S(1)}, f32[32,1024]{1,0:T(8,128)S(1)}, u32[]{:S(2)}, u32[]{:S(2)}) collective-permute-start(f32[32,1024]{1,0:T(8,128)S(1)} %slice_bitcast_fusion.4), channel_id=1, source_target_pairs={{0,2},{1,3},{2,0},{3,1},{4,6},{5,7},{6,4},{7,5},{8,10},{9,11},{10,... | collective-permute-start | bytes 393224 | tf_op jit(solution)/shard_map/ppermute | solution.py:202
  34.7 6.9 %collective-permute-start.8 = (f32[16,1024]{1,0:T(8,128)S(1)}, f32[16,1024]{1,0:T(8,128)S(1)}, u32[]{:S(2)}, u32[]{:S(2)}) collective-permute-start(f32[16,1024]{1,0:T(8,128)S(1)} %get-tuple-element.43), channel_id=1, source_target_pairs={{0,6},{1,7},{2,4},{3,5},{4,2},{5,3},{6,0},{7,1},{8,14},{9,15},{10,... | collective-permute-start | bytes 196616 | tf_op jit(solution)/shard_map/ppermute | solution.py:202
  35.7 9.6 %collective-permute-start.7 = (f32[16,1024]{1,0:T(8,128)S(1)}, f32[16,1024]{1,0:T(8,128)S(1)}, u32[]{:S(2)}, u32[]{:S(2)}) collective-permute-start(f32[16,1024]{1,0:T(8,128)S(1)} %get-tuple-element.44), channel_id=1, source_target_pairs={{0,4},{1,5},{2,6},{3,7},{4,0},{5,1},{6,2},{7,3},{8,12},{9,13},{10,... | collective-permute-start | bytes 196616 | tf_op jit(solution)/shard_map/ppermute | solution.py:202
  37.5 8.5 %collective-permute-start.6 = (f32[16,1024]{1,0:T(8,128)S(1)}, f32[16,1024]{1,0:T(8,128)S(1)}, u32[]{:S(2)}, u32[]{:S(2)}) collective-permute-start(f32[16,1024]{1,0:T(8,128)S(1)} %fusion.15), channel_id=1, source_target_pairs={{0,4},{1,5},{2,6},{3,7},{4,0},{5,1},{6,2},{7,3},{8,12},{9,13},{10,... | collective-permute-start | bytes 196616 | tf_op jit(solution)/shard_map/ppermute | solution.py:202
  46.0 7.3 %collective-permute-start.11 = (f32[32,1024]{1,0:T(8,128)S(1)}, f32[32,1024]{1,0:T(8,128)S(1)}, u32[]{:S(2)}, u32[]{:S(2)}) collective-permute-start(f32[32,1024]{1,0:T(8,128)S(1)} %fusion.12.refs_0_), channel_id=1, source_target_pairs={{0,24},{8,16},{16,8},{24,0},{1,25},{9,17},{17,9},{25,1},{2,26},{10... | collective-permute-start | bytes 393224 | tf_op jit(solution)/shard_map/ppermute | solution.py:202
  46.8 7.3 %collective-permute-start.10 = (f32[32,1024]{1,0:T(8,128)S(1)}, f32[32,1024]{1,0:T(8,128)S(1)}, u32[]{:S(2)}, u32[]{:S(2)}) collective-permute-start(f32[32,1024]{1,0:T(8,128)S(1)} %fusion.12.refs_0_), channel_id=1, source_target_pairs={{0,16},{8,24},{16,0},{24,8},{1,17},{9,25},{17,1},{25,9},{2,18},{10... | collective-permute-start | bytes 393224 | tf_op jit(solution)/shard_map/ppermute | solution.py:202
  48.0 6.0 %collective-permute-start.9 = (f32[32,1024]{1,0:T(8,128)S(1)}, f32[32,1024]{1,0:T(8,128)S(1)}, u32[]{:S(2)}, u32[]{:S(2)}) collective-permute-start(f32[32,1024]{1,0:T(8,128)S(1)} %fusion.12.refs_0_), channel_id=1, source_target_pairs={{0,8},{8,0},{16,24},{24,16},{1,9},{9,1},{17,25},{25,17},{2,10},{10... | collective-permute-start | bytes 393224 | tf_op jit(solution)/shard_map/ppermute | solution.py:202
  57.8 2.0 %collective-permute-start.12 = (f32[4,32,1024]{2,1,0:T(8,128)S(1)}, f32[4,32,1024]{2,1,0:T(8,128)S(1)}, u32[]{:S(2)}, u32[]{:S(2)}) collective-permute-start(f32[4,32,1024]{2,1,0:T(8,128)S(1)} %get-tuple-element.29), channel_id=1, source_target_pairs={{0,1},{1,0},{2,3},{3,2},{4,5},{5,4},{6,7},{7,6},{8,9},{9,8},{10,11... | collective-permute-start | bytes 1572872 | tf_op jit(solution)/shard_map/ppermute | solution.py:202
  59.9 5.0 %collective-permute-start.14 = (f32[16,1024]{1,0:T(8,128)S(1)}, f32[16,1024]{1,0:T(8,128)S(1)}, u32[]{:S(2)}, u32[]{:S(2)}) collective-permute-start(f32[16,1024]{1,0:T(8,128)S(1)} %get-tuple-element.39), channel_id=1, source_target_pairs={{0,2},{1,3},{2,0},{3,1},{4,6},{5,7},{6,4},{7,5},{8,10},{9,11},{10,... | collective-permute-start | bytes 196616 | tf_op jit(solution)/shard_map/ppermute | solution.py:202
  60.0 13.0 %collective-permute-start.13 = (f32[32,1024]{1,0:T(8,128)S(1)}, f32[32,1024]{1,0:T(8,128)S(1)}, u32[]{:S(2)}, u32[]{:S(2)}) collective-permute-start(f32[32,1024]{1,0:T(8,128)S(1)} %slice_bitcast_fusion.2), channel_id=1, source_target_pairs={{0,2},{1,3},{2,0},{3,1},{4,6},{5,7},{6,4},{7,5},{8,10},{9,11},{10,... | collective-permute-start | bytes 393224 | tf_op jit(solution)/shard_map/ppermute | solution.py:202
  62.1 8.0 %collective-permute-start.17 = (f32[16,1024]{1,0:T(8,128)S(1)}, f32[16,1024]{1,0:T(8,128)S(1)}, u32[]{:S(2)}, u32[]{:S(2)}) collective-permute-start(f32[16,1024]{1,0:T(8,128)S(1)} %get-tuple-element.40), channel_id=1, source_target_pairs={{0,6},{1,7},{2,4},{3,5},{4,2},{5,3},{6,0},{7,1},{8,14},{9,15},{10,... | collective-permute-start | bytes 196616 | tf_op jit(solution)/shard_map/ppermute | solution.py:202
  64.2 8.8 %collective-permute-start.16 = (f32[16,1024]{1,0:T(8,128)S(1)}, f32[16,1024]{1,0:T(8,128)S(1)}, u32[]{:S(2)}, u32[]{:S(2)}) collective-permute-start(f32[16,1024]{1,0:T(8,128)S(1)} %get-tuple-element.41), channel_id=1, source_target_pairs={{0,4},{1,5},{2,6},{3,7},{4,0},{5,1},{6,2},{7,3},{8,12},{9,13},{10,... | collective-permute-start | bytes 196616 | tf_op jit(solution)/shard_map/ppermute | solution.py:202
  64.9 8.7 %collective-permute-start.15 = (f32[16,1024]{1,0:T(8,128)S(1)}, f32[16,1024]{1,0:T(8,128)S(1)}, u32[]{:S(2)}, u32[]{:S(2)}) collective-permute-start(f32[16,1024]{1,0:T(8,128)S(1)} %fusion.14), channel_id=1, source_target_pairs={{0,4},{1,5},{2,6},{3,7},{4,0},{5,1},{6,2},{7,3},{8,12},{9,13},{10,... | collective-permute-start | bytes 196616 | tf_op jit(solution)/shard_map/ppermute | solution.py:202
  73.7 7.0 %collective-permute-start.20 = (f32[32,1024]{1,0:T(8,128)S(1)}, f32[32,1024]{1,0:T(8,128)S(1)}, u32[]{:S(2)}, u32[]{:S(2)}) collective-permute-start(f32[32,1024]{1,0:T(8,128)S(1)} %fusion.9.refs_0_), channel_id=1, source_target_pairs={{0,24},{8,16},{16,8},{24,0},{1,25},{9,17},{17,9},{25,1},{2,26},{10... | collective-permute-start | bytes 393224 | tf_op jit(solution)/shard_map/ppermute | solution.py:202
  74.9 7.1 %collective-permute-start.19 = (f32[32,1024]{1,0:T(8,128)S(1)}, f32[32,1024]{1,0:T(8,128)S(1)}, u32[]{:S(2)}, u32[]{:S(2)}) collective-permute-start(f32[32,1024]{1,0:T(8,128)S(1)} %fusion.9.refs_0_), channel_id=1, source_target_pairs={{0,16},{8,24},{16,0},{24,8},{1,17},{9,25},{17,1},{25,9},{2,18},{10... | collective-permute-start | bytes 393224 | tf_op jit(solution)/shard_map/ppermute | solution.py:202
  76.2 5.8 %collective-permute-start.18 = (f32[32,1024]{1,0:T(8,128)S(1)}, f32[32,1024]{1,0:T(8,128)S(1)}, u32[]{:S(2)}, u32[]{:S(2)}) collective-permute-start(f32[32,1024]{1,0:T(8,128)S(1)} %fusion.9.refs_0_), channel_id=1, source_target_pairs={{0,8},{8,0},{16,24},{24,16},{1,9},{9,1},{17,25},{25,17},{2,10},{10... | collective-permute-start | bytes 393224 | tf_op jit(solution)/shard_map/ppermute | solution.py:202
  85.8 2.0 %collective-permute-start.21 = (f32[4,32,1024]{2,1,0:T(8,128)S(1)}, f32[4,32,1024]{2,1,0:T(8,128)S(1)}, u32[]{:S(2)}, u32[]{:S(2)}) collective-permute-start(f32[4,32,1024]{2,1,0:T(8,128)S(1)} %get-tuple-element.32), channel_id=1, source_target_pairs={{0,1},{1,0},{2,3},{3,2},{4,5},{5,4},{6,7},{7,6},{8,9},{9,8},{10,11... | collective-permute-start | bytes 1572872 | tf_op jit(solution)/shard_map/ppermute | solution.py:202
  87.9 5.0 %collective-permute-start.23 = (f32[16,1024]{1,0:T(8,128)S(1)}, f32[16,1024]{1,0:T(8,128)S(1)}, u32[]{:S(2)}, u32[]{:S(2)}) collective-permute-start(f32[16,1024]{1,0:T(8,128)S(1)} %get-tuple-element.36), channel_id=1, source_target_pairs={{0,2},{1,3},{2,0},{3,1},{4,6},{5,7},{6,4},{7,5},{8,10},{9,11},{10,... | collective-permute-start | bytes 196616 | tf_op jit(solution)/shard_map/ppermute | solution.py:202
  88.0 12.7 %collective-permute-start.22 = (f32[32,1024]{1,0:T(8,128)S(1)}, f32[32,1024]{1,0:T(8,128)S(1)}, u32[]{:S(2)}, u32[]{:S(2)}) collective-permute-start(f32[32,1024]{1,0:T(8,128)S(1)} %slice_bitcast_fusion), channel_id=1, source_target_pairs={{0,2},{1,3},{2,0},{3,1},{4,6},{5,7},{6,4},{7,5},{8,10},{9,11},{10,... | collective-permute-start | bytes 393224 | tf_op jit(solution)/shard_map/ppermute | solution.py:202
  90.0 7.6 %collective-permute-start.26 = (f32[16,1024]{1,0:T(8,128)S(1)}, f32[16,1024]{1,0:T(8,128)S(1)}, u32[]{:S(2)}, u32[]{:S(2)}) collective-permute-start(f32[16,1024]{1,0:T(8,128)S(1)} %get-tuple-element.37), channel_id=1, source_target_pairs={{0,6},{1,7},{2,4},{3,5},{4,2},{5,3},{6,0},{7,1},{8,14},{9,15},{10,... | collective-permute-start | bytes 196616 | tf_op jit(solution)/shard_map/ppermute | solution.py:202
  91.8 8.8 %collective-permute-start.25 = (f32[16,1024]{1,0:T(8,128)S(1)}, f32[16,1024]{1,0:T(8,128)S(1)}, u32[]{:S(2)}, u32[]{:S(2)}) collective-permute-start(f32[16,1024]{1,0:T(8,128)S(1)} %get-tuple-element.38), channel_id=1, source_target_pairs={{0,4},{1,5},{2,6},{3,7},{4,0},{5,1},{6,2},{7,3},{8,12},{9,13},{10,... | collective-permute-start | bytes 196616 | tf_op jit(solution)/shard_map/ppermute | solution.py:202
  92.9 8.5 %collective-permute-start.24 = (f32[16,1024]{1,0:T(8,128)S(1)}, f32[16,1024]{1,0:T(8,128)S(1)}, u32[]{:S(2)}, u32[]{:S(2)}) collective-permute-start(f32[16,1024]{1,0:T(8,128)S(1)} %fusion.13), channel_id=1, source_target_pairs={{0,4},{1,5},{2,6},{3,7},{4,0},{5,1},{6,2},{7,3},{8,12},{9,13},{10,... | collective-permute-start | bytes 196616 | tf_op jit(solution)/shard_map/ppermute | solution.py:202
